TPU v7x, 32 devices: a whole 2x2x4 slice. The times are simulated.
32 devices in a mesh: dp: 8 (over z, core), ctx: 4 (over y, x).
Axes of the slice: x: 2, y: 2, z: 4, core: 2. Of those that a mesh axis runs over, the one named last changes fastest.
Arguments:
- tokens: bfloat16 [8, 1024, 1024], P('dp', 'ctx'), may hold values from -6 to 6
- segments: int32 [8, 1024], P('dp'), may hold values from 0 to 3, never falling along the last dimension, each value on 1 to 512 neighbouring positions
- qkv_weight: bfloat16 [1024, 3072], P(('dp', 'ctx')), may hold values from -0.1875 to 0.1875
- qkv_bias: bfloat16 [3072], P(('dp', 'ctx')), may hold values from -3 to 3
- out_weight: bfloat16 [1024, 1024], P(('dp', 'ctx')), may hold values from -0.75 to 0.75
- out_bias: bfloat16 [1024], P(('dp', 'ctx')), may hold values from -3 to 3
- fc1_weight: bfloat16 [1024, 4096], P(('dp', 'ctx')), may hold values from -0.1875 to 0.1875
- fc1_bias: bfloat16 [4096], P(('dp', 'ctx')), may hold values from -3 to 3
- fc2_weight: bfloat16 [4096, 1024], P(('dp', 'ctx')), may hold values from -0.09375 to 0.09375
- fc2_bias: bfloat16 [1024], P(('dp', 'ctx')), may hold values from -3 to 3
- norm_gain: bfloat16 [1024], P(('dp', 'ctx')), may hold values from 0.5 to 1.5
- norm_shift: bfloat16 [1024], P(('dp', 'ctx')), may hold values from -2 to 2
- cotangent: bfloat16 [8, 1024, 1024], P('dp', 'ctx'), may hold values from -6 to 6
Outputs:
- result: bfloat16 [8, 1024, 1024], P('dp', 'ctx')
- grad_tokens: bfloat16 [8, 1024, 1024], P('dp', 'ctx')
- grad_qkv_weight: float32 [1024, 3072], P(('dp', 'ctx'))
- grad_qkv_bias: float32 [3072], P(('dp', 'ctx'))
- grad_out_weight: float32 [1024, 1024], P(('dp', 'ctx'))
- grad_out_bias: float32 [1024], P(('dp', 'ctx'))
- grad_fc1_weight: float32 [1024, 4096], P(('dp', 'ctx'))
- grad_fc1_bias: float32 [4096], P(('dp', 'ctx'))
- grad_fc2_weight: float32 [4096, 1024], P(('dp', 'ctx'))
- grad_fc2_bias: float32 [1024], P(('dp', 'ctx'))
- grad_norm_gain: float32 [1024], P(('dp', 'ctx'))
- grad_norm_shift: float32 [1024], P(('dp', 'ctx'))
Inputs may be any that keep to these rules, and one draw needn't show every extreme that they name: `segments`: segment numbers never fall along a sequence; each document has 1 to 512 tokens, and one of each sequence has exactly 512.
All inputs are finite; a program needn't handle non-finite values.
Results may differ from a plain program's by a relative error of at most 0.0093.
Values may be sent and summed in bfloat16 or wider, within the bound.
A program may use at most 192 MiB of HBM per device.

v0:
```python
import functools

import jax
import jax.numpy as jnp
from jax import lax
from jax.experimental import pallas as pl
from jax.experimental.pallas import tpu as pltpu
from jax.sharding import PartitionSpec as P

HEADS = 16
ROT = 32
epsilon = 1e-05
BOTH = ("dp", "ctx")
MESH = pl.DeviceIdType.MESH


def angles(positions, rotary):
    freq_table = 1.0 / 10000.0 ** (jnp.arange(0, rotary, 2, dtype=jnp.float32) / rotary)
    theta = positions.astype(jnp.float32)[:, None] * freq_table[None, :]
    return (jnp.cos(theta)[:, None, :], jnp.sin(theta)[:, None, :])


def rotate(tensor, cosine, sine_table, rotary):
    half_len = rotary // 2
    first_half = tensor[..., :half_len]
    second_half = tensor[..., half_len:rotary]
    return jnp.concatenate(
        [
            first_half * cosine - second_half * sine_table,
            second_half * cosine + first_half * sine_table,
            tensor[..., rotary:],
        ],
        axis=-1,
    )


def contract_rows(left, right):
    return lax.dot_general(
        left, right, (((0,), (0,)), ((), ())), preferred_element_type=jnp.float32
    )


def times_transposed(left, right):
    return lax.dot_general(
        left, right, (((1,), (1,)), ((), ())), preferred_element_type=jnp.float32
    )


def times(left, right):
    return jnp.dot(left, right, preferred_element_type=jnp.float32)


def gelu_tanh(hidden_in):
    return jax.nn.gelu(hidden_in, approximate=True)


def normalise(inputs):
    center = inputs - jnp.mean(inputs, axis=-1, keepdims=True)
    inverse = lax.rsqrt(jnp.mean(center * center, axis=-1, keepdims=True) + epsilon)
    return center * inverse, inverse


def attention(q, k, v, segments, back, cosine, sine):
    length, head_dim = q.shape[1], q.shape[3]
    scale = float(head_dim) ** (-0.5)
    index = jnp.arange(length, dtype=jnp.int32)
    allowed = (segments[:, :, None] == segments[:, None, :]) & (index[None, :] <= index[:, None])[
        None
    ]
    scores = jnp.einsum("sqhd,skhd->shqk", q, k, preferred_element_type=jnp.float32) * scale
    scores = jnp.where(allowed[:, None], scores, -1e30)
    row_max = jnp.max(scores, axis=-1, keepdims=True)
    log_total = row_max + jnp.log(jnp.sum(jnp.exp(scores - row_max), axis=-1, keepdims=True))
    probs = jnp.exp(scores - log_total)
    probs_low = probs.astype(jnp.bfloat16)
    attended = jnp.einsum("shqk,skhd->sqhd", probs_low, v, preferred_element_type=jnp.float32)

    def backward(grad_attended):
        grad_weights = jnp.einsum(
            "sqhd,skhd->shqk", grad_attended, v, preferred_element_type=jnp.float32
        )
        row_dot = jnp.sum(grad_weights * probs, axis=-1, keepdims=True)
        grad_scores = (probs * (grad_weights - row_dot)).astype(jnp.bfloat16)
        grad_q = (
            jnp.einsum("shqk,skhd->sqhd", grad_scores, k, preferred_element_type=jnp.float32)
            * scale
        )
        grad_k = (
            jnp.einsum("shqk,sqhd->skhd", grad_scores, q, preferred_element_type=jnp.float32)
            * scale
        )
        grad_v = jnp.einsum(
            "shqk,sqhd->skhd", probs_low, grad_attended, preferred_element_type=jnp.float32
        )
        return grad_q, grad_k, grad_v

    return attended, backward


def gather_kernel(
    nz, nc,
    tok_ref, cot_ref, qkv_ref, fc1_ref, fc2_ref, out_ref, small_ref,
    tok_all, cot_all, w_qkv, w_fc1, w_fc2, w_out, small_all,
    ctx_send, ctx_recv, z_send, z_recv, sib_send, sib_recv, loc,
):
    d, c = lax.axis_index("dp"), lax.axis_index("ctx")
    z, k = d // 2, lax.rem(d, 2)
    other = 2 * z + 1 - k
    wr, width = out_ref.shape
    dl = width // nc
    fr = fc2_ref.shape[0]
    nd = 2 * nz

    def ctx_to(j):
        return lax.rem(c + j, nc)

    def ctx_from(j):
        return lax.rem(c + nc - j, nc)

    def z_to(j):
        return 2 * lax.rem(z + j, nz) + k

    def z_from(j):
        return 2 * lax.rem(z + nz - j, nz) + k

    barrier = pltpu.get_barrier_semaphore()
    for j in range(1, nc):
        pl.semaphore_signal(barrier, inc=1, device_id=(d, ctx_to(j)), device_id_type=MESH)
    for j in range(1, nz):
        pl.semaphore_signal(barrier, inc=1, device_id=(z_to(j), c), device_id_type=MESH)
    pl.semaphore_signal(barrier, inc=1, device_id=(other, c), device_id_type=MESH)
    pl.semaphore_wait(barrier, nc + nz - 1)

    def remote(src, dst, send, recv, device):
        return pltpu.make_async_remote_copy(
            src_ref=src, dst_ref=dst, send_sem=send, recv_sem=recv,
            device_id=device, device_id_type=MESH,
        )

    def rows(at):
        return pl.ds(pl.multiple_of(at * wr, wr), wr)

    def lanes(at, size):
        return pl.ds(pl.multiple_of(at * size, size), size)

    SMALL, QKV, FC1, TOK, COT, OUT, FC2 = range(7)

    def qkv_pieces(to, owner, sub):
        return [
            (qkv_ref.at[:, lanes(t * nc + to, dl)], w_qkv.at[owner, rows(sub), pl.ds(t * dl, dl)])
            for t in range(3)
        ]

    def fc1_pieces(to, owner, sub):
        return [
            (fc1_ref.at[:, lanes(g * nc + to, fr)], w_fc1.at[owner, rows(sub), pl.ds(g * fr, fr)])
            for g in range(nd)
        ]

    def ctx_pieces(array, to):
        if array == SMALL:
            return [(small_ref, small_all.at[d, c])]
        if array == QKV:
            return qkv_pieces(to, d, c)
        if array == FC1:
            return fc1_pieces(to, d, c)
        if array == TOK:
            return [(tok_ref, tok_all.at[c])]
        return [(cot_ref, cot_all.at[c])]

    def ctx_whole(array, sub):
        return {
            SMALL: lambda: small_all.at[d, sub],
            QKV: lambda: w_qkv.at[d, rows(sub), :],
            FC1: lambda: w_fc1.at[d, rows(sub), :],
            TOK: lambda: tok_all.at[sub],
            COT: lambda: cot_all.at[sub],
        }[array]()

    def ctx_start(array):
        for j in range(1, nc):
            for src, dst in ctx_pieces(array, ctx_to(j)):
                remote(src, dst, ctx_send.at[array, j], ctx_recv.at[array, j], (d, ctx_to(j))).start()
        for src, dst in ctx_pieces(array, c):
            pltpu.make_async_copy(src, dst, loc.at[array]).start()

    def ctx_finish(array):
        for j in range(1, nc):
            got = ctx_whole(array, ctx_from(j))
            remote(got, got, ctx_send.at[array, j], ctx_recv.at[array, j], (d, ctx_to(j))).wait()
        mine = ctx_whole(array, c)
        pltpu.make_async_copy(mine, mine, loc.at[array]).wait()

    blocks = {SMALL: small_all, QKV: w_qkv, FC1: w_fc1, FC2: w_fc2}

    def z_copy(array, j, own):
        block = blocks[array].at[own]
        src = fc2_ref if array == FC2 else block
        return remote(src, block, z_send.at[array, j], z_recv.at[array, j], (z_to(j), c))

    def sib_copy(array, j, at):
        block = blocks[array].at[at]
        src = fc2_ref if array == FC2 and j == 0 else block
        return remote(src, block, sib_send.at[array, j], sib_recv.at[array, j], (other, c))

    def z_start(array):
        for j in range(1, nz):
            z_copy(array, j, d).start()
        sib_copy(array, 0, d).start()

    def z_pass_on(array):
        for j in range(1, nz):
            z_copy(array, j, z_from(j)).wait_recv()
            sib_copy(array, j, z_from(j)).start()

    def z_finish(array):
        for j in range(1, nz):
            z_copy(array, j, d).wait_send()
        for j in range(nz):
            sib_copy(array, j, d if j == 0 else z_from(j)).wait_send()
            sib_copy(array, j, lax.rem(z + nz - j, nz) * 2 + 1 - k).wait_recv()

    def out_copy(j, to, sub):
        return remote(out_ref, w_out.at[k, rows(sub), :], ctx_send.at[OUT, j], ctx_recv.at[OUT, j], (d, to))

    half = w_out.at[k]

    def out_z(j, to):
        return remote(half, half, z_send.at[OUT, j], z_recv.at[OUT, j], (to, c))

    ctx_start(SMALL)
    ctx_start(QKV)
    ctx_start(TOK)
    ctx_start(FC1)
    own_fc2 = pltpu.make_async_copy(fc2_ref, w_fc2.at[d], loc.at[FC2])
    own_fc2.start()
    own_out = pltpu.make_async_copy(out_ref, w_out.at[k, rows(c), :], loc.at[OUT])

    @pl.when(z == c)
    def _():
        own_out.start()

    for j in range(1, nc):
        @pl.when(ctx_to(j) == z)
        def _():
            out_copy(j, z, c).start()

    ctx_finish(SMALL)
    z_start(SMALL)
    ctx_finish(QKV)
    z_start(QKV)
    ctx_start(COT)
    ctx_finish(FC1)
    z_start(FC1)
    z_start(FC2)

    @pl.when(z == c)
    def _():
        for j in range(1, nc):
            out_copy(j, z, ctx_from(j)).wait_recv()
        own_out.wait()
        for j in range(1, nz):
            out_z(j, z_to(j)).start()

    for j in range(1, nc):
        @pl.when(ctx_to(j) == z)
        def _():
            out_copy(j, z, c).wait_send()

    z_pass_on(SMALL)
    z_finish(SMALL)
    z_pass_on(QKV)
    z_finish(QKV)
    ctx_finish(TOK)
    z_pass_on(FC1)
    z_finish(FC1)
    ctx_finish(COT)
    own_fc2.wait()
    z_pass_on(FC2)
    z_finish(FC2)

    for j in range(1, nz):
        @pl.when(lax.rem(z + nz - j, nz) == c)
        def _():
            out_z(j, z_to(j)).wait_recv()

    @pl.when(z == c)
    def _():
        for j in range(1, nz):
            out_z(j, z_to(j)).wait_send()

    give = remote(half, half, sib_send.at[OUT, 0], sib_recv.at[OUT, 0], (other, c))
    give.start()
    give.wait()


def gather_all(nz, nc, tokens, cotangent, qkv_weight, fc1_weight, fc2_weight, out_weight, small):
    part, width = tokens.shape
    wr, fr = qkv_weight.shape[0], fc2_weight.shape[0]
    nd, dl = 2 * nz, width // nc
    b16 = jnp.bfloat16
    shapes = [
        ((nc, part, width), b16),
        ((nc, part, width), b16),
        ((nd, nc * wr, 3 * dl), b16),
        ((nd, nc * wr, nd * fr), b16),
        ((nd, fr, width), b16),
        ((2, nc * wr, width), b16),
        ((nd, nc) + small.shape, jnp.float32),
    ]
    return pl.pallas_call(
        functools.partial(gather_kernel, nz, nc),
        out_shape=[jax.ShapeDtypeStruct(s, t) for s, t in shapes],
        in_specs=[pl.BlockSpec(memory_space=pl.ANY)] * 7,
        out_specs=[pl.BlockSpec(memory_space=pl.ANY)] * 7,
        scratch_shapes=[
            pltpu.SemaphoreType.DMA((7, nc)),
            pltpu.SemaphoreType.DMA((7, nc)),
            pltpu.SemaphoreType.DMA((7, nz)),
            pltpu.SemaphoreType.DMA((7, nz)),
            pltpu.SemaphoreType.DMA((7, nz)),
            pltpu.SemaphoreType.DMA((7, nz)),
            pltpu.SemaphoreType.DMA((7,)),
        ],
        compiler_params=pltpu.CompilerParams(collective_id=0, has_side_effects=True),
        name="gather",
    )(tokens, cotangent, qkv_weight, fc1_weight, fc2_weight, out_weight, small)


def local(
    dp,
    ctx,
    tokens,
    segments,
    qkv_weight,
    qkv_bias,
    out_weight,
    out_bias,
    fc1_weight,
    fc1_bias,
    fc2_weight,
    fc2_bias,
    norm_gain,
    norm_shift,
    cotangent,
):
    f32, b16 = jnp.float32, jnp.bfloat16
    seqs, part, width = tokens.shape
    length = part * ctx
    rows = seqs * length
    ff = fc1_weight.shape[1]
    fl, dl = ff // ctx, width // ctx
    heads = HEADS // ctx
    head_dim = width // HEADS
    wr, fr = qkv_weight.shape[0], fc2_weight.shape[0]
    mine = lax.axis_index("ctx")
    devices = dp * ctx

    pieces = [qkv_bias, fc1_bias, out_bias, fc2_bias, norm_gain, norm_shift]
    marks = [0]
    for piece in pieces:
        marks.append(marks[-1] + piece.shape[0])
    direct = wr % 16 == 0 and dp == 2 * ctx and seqs == 1
    if direct:
        vector = jnp.concatenate(pieces).astype(f32)
        vector = jnp.pad(vector, (0, -marks[-1] % 128))[None]
        tokens_all, cot_all, w_qkv, w_fc1, w_fc2, w_out, small = gather_all(
            dp // 2,
            ctx,
            tokens[0],
            cotangent[0],
            qkv_weight,
            fc1_weight,
            fc2_weight,
            out_weight,
            vector,
        )
        tokens_all = tokens_all.reshape(seqs, length, width)
        cot_all = cot_all.reshape(seqs, length, width)
        w_qkv, w_fc1 = w_qkv.reshape(width, 3 * dl), w_fc1.reshape(width, fl)
        w_fc2, w_out = w_fc2.reshape(fl, width), w_out.reshape(dl, width)
        small = small.reshape(devices, -1)
    else:
        small = lax.all_gather(jnp.concatenate(pieces), BOTH, axis=0)
    parts = [small[:, a:b] for a, b in zip(marks, marks[1:])]
    b_qkv = lax.dynamic_index_in_dim(
        parts[0].reshape(3, ctx, dl), mine, 1, keepdims=False
    ).reshape(3 * dl)
    b_fc1 = lax.dynamic_index_in_dim(
        parts[1].reshape(dp, ctx, fr), mine, 1, keepdims=False
    ).reshape(fl)
    b_out, b_fc2, gain, shift = [p.reshape(width).astype(f32) for p in parts[2:]]

    out_perm = [(b, (b % dp) * ctx + b // dp) for b in range(devices)]
    out_back = [(j, i) for i, j in out_perm]
    if not direct:
        send_qkv = jnp.moveaxis(qkv_weight.reshape(wr, 3, ctx, dl), 2, 0).reshape(ctx, wr, 3 * dl)
        send_fc1 = jnp.moveaxis(fc1_weight.reshape(wr, dp, ctx, fr), 2, 0).reshape(ctx, wr, fl)
        sent = lax.all_to_all(
            jnp.concatenate([send_qkv, send_fc1], axis=2), "ctx", split_axis=0, concat_axis=0
        )
        out_piece = lax.ppermute(out_weight, BOTH, out_perm)
        w_qkv = lax.all_gather(sent[:, :, : 3 * dl], "dp", axis=0).reshape(width, 3 * dl)
        w_fc1 = lax.all_gather(sent[:, :, 3 * dl :], "dp", axis=0).reshape(width, fl)
        w_fc2 = lax.all_gather(fc2_weight, "dp", axis=0).reshape(fl, width)
        w_out = lax.all_gather(out_piece, "dp", axis=0).reshape(dl, width)

        tokens_all = lax.all_gather(tokens, "ctx", axis=1, tiled=True)
        cot_all = lax.all_gather(cotangent, "ctx", axis=1, tiled=True)

    positions = jnp.arange(length, dtype=jnp.int32)
    cosine, sine = angles(positions, ROT)

    scaled_all, _ = normalise(tokens_all.astype(f32).reshape(rows, width))
    normed = (scaled_all * gain + shift).astype(b16)
    grad_out = cot_all.reshape(rows, width)

    mixed = times(normed, w_qkv) + b_qkv.astype(f32)
    shape4 = (seqs, length, heads, head_dim)
    q = rotate(mixed[:, :dl].reshape(shape4), cosine, sine, ROT).astype(b16)
    k = rotate(mixed[:, dl : 2 * dl].reshape(shape4), cosine, sine, ROT).astype(b16)
    v = mixed[:, 2 * dl :].astype(b16).reshape(shape4)
    attended, attention_back = attention(q, k, v, segments, None, cosine, sine)
    attended = attended.reshape(rows, dl).astype(b16)

    hidden = times(normed, w_fc1) + b_fc1.astype(f32)
    act, gelu_back = jax.vjp(gelu_tanh, hidden)
    act = act.astype(b16)
    partial = times(attended, w_out) + times(act, w_fc2)
    summed = lax.psum_scatter(
        partial.astype(b16).reshape(seqs, length, width), "ctx", scatter_dimension=1, tiled=True
    )
    result = (tokens.astype(f32) + summed.astype(f32) + (b_out + b_fc2)).astype(b16)

    grad_act = times_transposed(grad_out, w_fc2)
    grad_hidden = gelu_back(grad_act)[0].astype(b16)
    grad_fc2 = contract_rows(act, grad_out)
    grad_fc2 = lax.psum_scatter(grad_fc2.astype(b16), "dp", scatter_dimension=0, tiled=True)
    grad_fc1 = contract_rows(normed, grad_hidden)
    grad_fc1_b = jnp.sum(grad_hidden, axis=0, dtype=f32)
    grad_fc1 = lax.psum_scatter(grad_fc1.astype(b16), "dp", scatter_dimension=0, tiled=True)
    grad_out_w = contract_rows(attended, grad_out)
    grad_out_w = lax.psum_scatter(grad_out_w.astype(b16), "dp", scatter_dimension=0, tiled=True)
    grad_attended = times_transposed(grad_out, w_out).astype(b16).reshape(shape4)
    grad_q, grad_k, grad_v = attention_back(grad_attended)
    grad_mixed = jnp.concatenate(
        [
            rotate(grad_q, cosine, -sine, ROT).reshape(rows, dl),
            rotate(grad_k, cosine, -sine, ROT).reshape(rows, dl),
            grad_v.reshape(rows, dl),
        ],
        axis=1,
    ).astype(b16)
    grad_normed = times_transposed(grad_hidden, w_fc1) + times_transposed(grad_mixed, w_qkv)
    grad_normed = lax.psum_scatter(
        grad_normed.astype(b16).reshape(seqs, length, width), "ctx", scatter_dimension=1, tiled=True
    ).astype(f32)
    grad_qkv = contract_rows(normed, grad_mixed)
    grad_qkv_b = jnp.sum(grad_mixed, axis=0, dtype=f32)
    grad_qkv = lax.psum_scatter(grad_qkv.astype(b16), "dp", scatter_dimension=0, tiled=True)

    back = lax.all_to_all(
        jnp.concatenate([grad_qkv, grad_fc1], axis=1).reshape(ctx, wr, 3 * dl + fl),
        "ctx",
        split_axis=0,
        concat_axis=0,
    ).astype(f32)
    grad_qkv = jnp.moveaxis(back[:, :, : 3 * dl].reshape(ctx, wr, 3, dl), 0, 2).reshape(
        wr, 3 * width
    )
    grad_fc1 = jnp.moveaxis(back[:, :, 3 * dl :].reshape(ctx, wr, dp, fr), 0, 2).reshape(wr, ff)
    grad_out_w = lax.ppermute(grad_out_w, BOTH, out_back).astype(f32)
    grad_fc2 = grad_fc2.astype(f32)

    grad_normed = grad_normed.reshape(seqs, part, width)
    own = tokens.astype(f32)
    cot = cotangent.astype(f32)
    scaled, inverse = normalise(own)
    grad_gain = jnp.sum(grad_normed * scaled, axis=(0, 1))
    grad_shift = jnp.sum(grad_normed, axis=(0, 1))
    grad_scaled = grad_normed * gain
    grad_input = inverse * (
        grad_scaled
        - jnp.mean(grad_scaled, axis=-1, keepdims=True)
        - scaled * jnp.mean(grad_scaled * scaled, axis=-1, keepdims=True)
    )
    grad_tokens = (cot + grad_input).astype(b16)

    wide_qkv_b = lax.dynamic_update_index_in_dim(
        jnp.zeros((3, ctx, dl), f32), grad_qkv_b.reshape(3, dl), mine, 1
    )
    wide_fc1_b = lax.dynamic_update_index_in_dim(
        jnp.zeros((dp, ctx, fr), f32), grad_fc1_b.reshape(dp, fr), mine, 1
    )
    bias_out = jnp.sum(cot, axis=(0, 1))
    sums = jnp.concatenate(
        [
            x.reshape(devices, -1)
            for x in (wide_qkv_b, wide_fc1_b, bias_out, grad_gain, grad_shift)
        ],
        axis=1,
    )
    sums = lax.psum_scatter(sums, BOTH, scatter_dimension=0, tiled=True)[0]
    at = [0, marks[1], marks[2], marks[3], marks[3] + wr, marks[3] + 2 * wr]
    g_qkv_b, g_fc1_b, g_bias, g_gain, g_shift = [sums[a:b] for a, b in zip(at, at[1:])]
    return (
        result,
        grad_tokens,
        grad_qkv,
        g_qkv_b,
        grad_out_w,
        g_bias,
        grad_fc1,
        g_fc1_b,
        grad_fc2,
        g_bias,
        g_gain,
        g_shift,
    )


def solution(mesh):
    sizes = (mesh.shape["dp"], mesh.shape["ctx"])
    seq, mat, vec = P("dp", "ctx", None), P(BOTH, None), P(BOTH)
    placed = (seq, P("dp", None), mat, vec, mat, vec, mat, vec, mat, vec, vec, vec, seq)
    return jax.shard_map(
        lambda *args: local(*sizes, *args),
        mesh=mesh,
        in_specs=placed,
        out_specs=(seq, seq, mat, vec, mat, vec, mat, vec, mat, vec, vec, vec),
        check_vma=False,
    )
```

profile of v0, /device:TPU:0, one launch (start us, length us, event | category | flops | bytes accessed | tf_op | source)
XLA Modules:
  0.0 388.0 jit_solution(12369882623736503720)
XLA Ops:
  7.3 4.1 %concatenate.49 = bf16[352]{0:T(512)(128)(2,1)S(1)} concatenate(bf16[96]{0:T(256)(128)(2,1)} %param.16, bf16[128]{0:T(256)(128)(2,1)} %param.20, bf16[32]{0:T(256)(128)(2,1)} %param.18, bf16[32]{0:T(256)(128)(2,1)} %param.22, bf16[32]{0:T(256)(128)(2,1)} %param.23, bf16[32]{0:T(256)(128)(2,1)} %param.24), dimensions={0} | concatenate | bytes 1408 | tf_op jit(solution)/shard_map/concatenate | solution.py:365
  11.9 88.2 %gather.1 = (bf16[4,256,1024]{2,1,0:T(8,128)(2,1)}, bf16[4,256,1024]{2,1,0:T(8,128)(2,1)}, bf16[8,128,768]{2,1,0:T(8,128)(2,1)}, bf16[8,128,1024]{2,1,0:T(8,128)...) custom-call(bf16[256,1024]{1,0:T(8,128)(2,1)} %bitcast.116, ...), custom_call_target="tpu_custom_call" | custom-call | tf_op jit(solution)/shard_map/gather/pallas_call | solution.py:311
  101.9 1.9 convert_reduce_fusion.1
  103.9 2.3 multiply_reduce_fusion.1
  108.4 1.9 convolution_add_fusion
  113.2 3.1 fusion
  116.3 4.0 %exponential_reduce_fusion = f32[4,1024]{1,0:T(4,128)S(1)} fusion(f32[4,1024,1024]{1,2,0:T(8,128)S(1)} %get-tuple-element.63, f32[4,1024]{1,0:T(4,128)S(1)} %get-tuple-element.62, pred[1024,1024]{0,1:T(8,128)(4,1)S(1)} %fusion.13), kind=kLoop, calls=%fused_computation.3 | loop fusion | flops 16773120 | bytes 17858560 | tf_op jit(solution)/shard_map/reduce_sum | solution.py:73
  120.3 1.7 copy-done
  122.0 4.6 %convolution_convert_fusion.4 = bf16[4,64,1024]{2,1,0:T(8,128)(2,1)S(1)} fusion(bf16[1024,4,64]{0,2,1:T(8,128)(2,1)S(1)} %bitcast.121, f32[4,1024,1024]{1,2,0:T(8,128)S(1)} %get-tuple-element.63, f32[4,1024]{1,0:T(4,128)S(1)} %log_add_fusion, pred[1024,1024]{0,1:T(8,128)(4,1)S(1)} %fusion.13), kind=kOutput, calls=%fused_computation.54 | convolution fusion | flops 553910272 | bytes 18890752 | tf_op jit(solution)/shard_map/shqk,skhd->sqhd/dot_general | solution.py:76
  128.3 2.3 convolution_convert_fusion.6
  131.4 9.1 %convolution_convert_fusion.3 = bf16[4,64,1024]{2,1,0:T(8,128)(2,1)} fusion(bf16[1024,4,64]{0,2,1:T(8,128)(2,1)S(1)} %bitcast.136, f32[4,1024,1024]{1,2,0:T(8,128)} %copy-done, f32[4,1024]{1,0:T(4,128)} %copy-done.28, pred[1024,1024]{0,1:T(8,128)(4,1)S(1)} %fusion.13), kind=kOutput, calls=%fused_computation.53 | convolution fusion | flops 553910272 | bytes 18890752 | tf_op jit(solution)/shard_map/shqk,sqhd->skhd/dot_general | solution.py:92
  140.5 15.4 %multiply_reduce_fusion = (f32[4,1024]{1,0:T(4,128)}, f32[4,1024,1024]{1,2,0:T(8,128)}) fusion(f32[4,1024,1024]{1,2,0:T(8,128)} %copy-done, f32[4,1024]{1,0:T(4,128)} %copy-done.28, pred[1024,1024]{0,1:T(8,128)(4,1)S(1)} %fusion.13, bf16[1024,4,64]{0,2,1:T(8,128)(2,1)} %bitcast.137, bf16[1024,4,64]{0,2,1:T(8,128)(2,1)} %bitcast.122), kind=kOutput, calls=%fused_computation.1 | convolution fusion | flops 557838336 | bytes 35684352 | tf_op jit(solution)/shard_map/sqhd,skhd->shqk/dot_general | solution.py:79
  156.0 8.8 %multiply_convert_fusion = bf16[4,1024,1024]{1,2,0:T(8,128)(2,1)S(1)} fusion(f32[4,1024,1024]{1,2,0:T(8,128)} %get-tuple-element.65, f32[4,1024,1024]{1,2,0:T(8,128)S(1)} %bitcast.115, f32[4,1024]{1,0:T(4,128)} %get-tuple-element.64, f32[4,1024]{1,0:T(4,128)} %copy-done.28, pred[1024,1024]{0,1:T(8,128)(4,1)S(1)} %fusion.13), kind=kLoop, calls=%fused_computation | loop fusion | flops 25165824 | bytes 43024384 | tf_op jit(solution)/shard_map/convert_element_type | solution.py:83
  164.8 3.8 fusion.19
  173.9 3.0 convolution_convert_fusion.2
  177.9 4.7 %fusion.50 = f32[1024,1024]{1,0:T(8,128)S(1)} fusion(bf16[1024,1024]{1,0:T(8,128)(2,1)} %bitcast.131, bf16[1024,1024]{1,0:T(8,128)(2,1)} %bitcast.160), kind=kOutput, calls=%fused_computation.122 | convolution fusion | flops 2147483648 | bytes 8388608 | tf_op jit(solution)/shard_map/dot_general | solution.py:50
  182.7 5.3 %convert_reduce_fusion = (f32[1024]{0:T(1024)S(1)}, bf16[1024,1024]{1,0:T(8,128)(2,1)S(1)}) fusion(f32[1024,1024]{1,0:T(8,128)S(1)} %fusion.50, f32[1024]{0:T(1024)S(1)} %bitcast.151, bf16[1024,1024]{1,0:T(8,128)(2,1)S(1)} %bitcast.157, bf16[1024,1024]{1,0:T(8,128)(2,1)S(1)} %bitcast.159), kind=kOutput, calls=%fused_computation.21 | convolution fusion | flops 2171599872 | bytes 10493952 | tf_op jit(solution)/shard_map/dot_general | solution.py:44
  189.3 3.8 convolution_convert_fusion.1
  193.2 4.7 %fusion.51 = f32[1024,1024]{1,0:T(8,128)S(1)} fusion(bf16[1024,1024]{1,0:T(8,128)(2,1)} %copy-done.39, bf16[1024,1024]{1,0:T(8,128)(2,1)} %bitcast.161), kind=kOutput, calls=%fused_computation.123 | convolution fusion | flops 2147483648 | bytes 8388608 | tf_op jit(solution)/shard_map/dot_general | solution.py:44
  197.9 3.2 fusion.14
  201.2 5.8 %fusion.47 = f32[1024,1024]{1,0:T(8,128)S(1)} fusion(bf16[1024,1024]{1,0:T(8,128)(2,1)} %bitcast.158, f32[1024,1024]{1,0:T(8,128)} %copy-done.38, f32[1024]{0:T(1024)S(1)} %bitcast.152), kind=kOutput, calls=%fused_computation.120 | convolution fusion | flops 2157969408 | bytes 10489856 | tf_op jit(solution)/shard_map/dot_general | solution.py:50
  207.0 2.1 fusion.15
  209.4 7.3 %convolution_convert_fusion = bf16[1024,1024]{1,0:T(8,128)(2,1)} fusion(bf16[1024,1024]{1,0:T(8,128)(2,1)} %bitcast.155, f32[1024,1024]{1,0:T(8,128)} %copy-done.38, f32[1024]{0:T(1024)S(1)} %bitcast.153), kind=kOutput, calls=%fused_computation.32 | convolution fusion | flops 2159017984 | bytes 8392704 | tf_op jit(solution)/shard_map/dot_general | solution.py:38
  220.0 35.1 %reduce-scatter.13.cloned.1.call-done = bf16[128,1024]{1,0:T(8,128)(2,1)} async-done(((bf16[1024,1024]{1,0:T(8,128)(2,1)}), bf16[128,1024]{1,0:T(8,128)(2,1)}) %reduce-scatter.13.cloned.1.call-update) | async-done | bytes 262160 | tf_op jit(solution)/shard_map/reduce_scatter | solution.py:441
  255.1 1.8 pad_maximum_fusion.5
  256.9 3.6 all-to-all-start
  260.5 32.2 %reduce-scatter.9.cloned.1.call-done = bf16[1,256,1024]{2,1,0:T(8,128)(2,1)} async-done(((bf16[1,1024,1024]{2,1,0:T(8,128)(2,1)}), bf16[1,256,1024]{2,1,0:T(8,128)(2,1)}) %reduce-scatter.9.cloned.1.call-update) | async-done | bytes 524304 | tf_op jit(solution)/shard_map/reduce_scatter | solution.py:455
  292.7 1.6 fusion.31
  294.3 36.4 %reduce-scatter.7.cloned.1.call-done = bf16[1,256,1024]{2,1,0:T(8,128)(2,1)} async-done(((bf16[1,1024,1024]{2,1,0:T(8,128)(2,1)}), bf16[1,256,1024]{2,1,0:T(8,128)(2,1)}) %reduce-scatter.7.cloned.1.call-update) | async-done | bytes 524304 | tf_op jit(solution)/shard_map/reduce_scatter | solution.py:430
  330.7 2.7 convert_reduce_fusion.5
  333.7 40.3 %all-reduce.1 = f32[32,320]{1,0:T(8,128)S(1)} all-reduce(f32[32,320]{1,0:T(8,128)S(1)} %concatenate.62), channel_id=6, replica_groups=mesh['dp'=8,'ctx'=4] {'dp','ctx'}, use_global_device_ids=true, to_apply=%region_18.19.clone | all-reduce | flops 10240 | bytes 81920
  374.6 1.8 convert_element_type.190
  (172 shorter events, 26.4 us)
Async XLA Ops:
  7.2 210.2 %reduce-scatter.15.cloned.1.call-start = ((), (), s32[]{:S(2)}) async-start(), calls=%async_computation.11 | async-start | bytes 589824 | tf_op jit(solution)/shard_map/reduce_scatter | solution.py:443
  100.1 6.9 %copy-start.1 = (bf16[4,256,1024]{2,1,0:T(8,128)(2,1)S(1)}, bf16[4,256,1024]{2,1,0:T(8,128)(2,1)}, u32[]{:S(2)}) copy-start(bf16[4,256,1024]{2,1,0:T(8,128)(2,1)} %get-tuple-element.19) | copy-start | bytes 6291460
  101.2 6.6 %copy-start.26 = (f32[32,384]{1,0:T(8,128)}, f32[32,384]{1,0:T(8,128)S(1)}, u32[]{:S(2)}) copy-start(f32[32,384]{1,0:T(8,128)S(1)} %reshape.533) | copy-start | bytes 147460
  107.9 4.8 %copy-start.5 = (bf16[4,256,1024]{2,1,0:T(8,128)(2,1)}, bf16[4,256,1024]{2,1,0:T(8,128)(2,1)S(1)}, u32[]{:S(2)}) copy-start(bf16[4,256,1024]{2,1,0:T(8,128)(2,1)S(1)} %add_convert_fusion.2) | copy-start | bytes 6291460
  110.4 9.9 %copy-start.4 = (bf16[1024,256]{0,1:T(8,128)(2,1)}, bf16[1024,256]{0,1:T(8,128)(2,1)S(1)}, u32[]{:S(2)}) copy-start(bf16[1024,256]{0,1:T(8,128)(2,1)S(1)} %slice.203) | copy-start | bytes 1572868
  116.3 5.7 %copy-start = (f32[4,1024,1024]{1,2,0:T(8,128)}, f32[4,1024,1024]{1,2,0:T(8,128)S(1)}, u32[]{:S(2)}) copy-start(f32[4,1024,1024]{1,2,0:T(8,128)S(1)} %get-tuple-element.63) | copy-start | bytes 50331652
  120.3 6.4 %copy-start.28 = (f32[4,1024]{1,0:T(4,128)}, f32[4,1024]{1,0:T(4,128)S(1)}, u32[]{:S(2)}) copy-start(f32[4,1024]{1,0:T(4,128)S(1)} %log_add_fusion) | copy-start | bytes 49156
  122.0 4.6 %copy-start.33 = (bf16[4,256,1024]{2,1,0:T(8,128)(2,1)S(1)}, bf16[4,256,1024]{2,1,0:T(8,128)(2,1)}, u32[]{:S(2)}) copy-start(bf16[4,256,1024]{2,1,0:T(8,128)(2,1)} %get-tuple-element.25) | copy-start | bytes 6291460
  122.0 6.3 %copy-start.21 = (bf16[2,128,1024]{2,1,0:T(8,128)(2,1)S(1)}, bf16[2,128,1024]{2,1,0:T(8,128)(2,1)}, u32[]{:S(2)}) copy-start(bf16[2,128,1024]{2,1,0:T(8,128)(2,1)} %get-tuple-element.22) | copy-start | bytes 1572868
  126.6 4.0 %copy-start.23 = (bf16[4,64,1024]{2,1,0:T(8,128)(2,1)}, bf16[4,64,1024]{2,1,0:T(8,128)(2,1)S(1)}, u32[]{:S(2)}) copy-start(bf16[4,64,1024]{2,1,0:T(8,128)(2,1)S(1)} %convolution_convert_fusion.4) | copy-start | bytes 1572868
  128.2 91.8 %reduce-scatter.11.cloned.1.call-start = ((), (), s32[]{:S(2)}) async-start(), calls=%async_computation.9 | async-start | bytes 1769472 | tf_op jit(solution)/shard_map/reduce_scatter | solution.py:460
  131.4 24.5 %slice-start = ((s8[16777216]{0:T(1024)(128)(4,1)}), s8[4194304]{0:T(1024)(128)(4,1)S(1)}, s32[]{:S(2)}) async-start(s8[16777216]{0:T(1024)(128)(4,1)} %bitcast.114), calls=%async_computation.13 | async-start | bytes 8388608
  131.4 24.5 %slice-start.1 = ((s8[16777216]{0:T(1024)(128)(4,1)}), s8[4194304]{0:T(1024)(128)(4,1)S(1)}, s32[]{:S(2)}) async-start(s8[16777216]{0:T(1024)(128)(4,1)} %bitcast.114), calls=%async_computation.14 | async-start | bytes 8388608
  140.5 15.4 %slice-start.2 = ((s8[16777216]{0:T(1024)(128)(4,1)}), s8[4194304]{0:T(1024)(128)(4,1)S(1)}, s32[]{:S(2)}) async-start(s8[16777216]{0:T(1024)(128)(4,1)} %bitcast.114), calls=%async_computation.15 | async-start | bytes 8388608
  140.5 15.4 %slice-start.3 = ((s8[16777216]{0:T(1024)(128)(4,1)}), s8[4194304]{0:T(1024)(128)(4,1)S(1)}, s32[]{:S(2)}) async-start(s8[16777216]{0:T(1024)(128)(4,1)} %bitcast.114), calls=%async_computation.16 | async-start | bytes 8388608
  177.0 78.1 %reduce-scatter.13.cloned.1.call-start = ((), (), s32[]{:S(2)}) async-start(), calls=%async_computation.10 | async-start | bytes 2359296 | tf_op jit(solution)/shard_map/reduce_scatter | solution.py:441
  177.9 4.7 %copy-start.34 = (bf16[4,256,1024]{2,1,0:T(8,128)(2,1)S(1)}, bf16[4,256,1024]{2,1,0:T(8,128)(2,1)}, u32[]{:S(2)}) copy-start(bf16[4,256,1024]{2,1,0:T(8,128)(2,1)} %get-tuple-element.25) | copy-start | bytes 6291460
  177.9 4.7 %copy-start.35 = (bf16[8,128,1024]{2,1,0:T(8,128)(2,1)S(1)}, bf16[8,128,1024]{2,1,0:T(8,128)(2,1)}, u32[]{:S(2)}) copy-start(bf16[8,128,1024]{2,1,0:T(8,128)(2,1)} %get-tuple-element.24) | copy-start | bytes 6291460
  182.6 5.4 %copy-start.38 = (f32[1024,1024]{1,0:T(8,128)}, f32[1024,1024]{1,0:T(8,128)S(1)}, u32[]{:S(2)}) copy-start(f32[1024,1024]{1,0:T(8,128)S(1)} %fusion.50) | copy-start | bytes 12582916
  182.7 6.7 %copy-start.7 = (bf16[1024,1024]{1,0:T(8,128)(2,1)S(1)}, bf16[1024,1024]{1,0:T(8,128)(2,1)}, u32[]{:S(2)}) copy-start(bf16[1024,1024]{1,0:T(8,128)(2,1)} %copy-done.6) | copy-start | bytes 6291460
  193.1 99.5 %reduce-scatter.9.cloned.1.call-start = ((), (), s32[]{:S(2)}) async-start(), calls=%async_computation.8 | async-start | bytes 2621440 | tf_op jit(solution)/shard_map/reduce_scatter | solution.py:455
  193.2 4.7 %copy-start.37 = (bf16[8,128,768]{2,1,0:T(8,128)(2,1)S(1)}, bf16[8,128,768]{2,1,0:T(8,128)(2,1)}, u32[]{:S(2)}) copy-start(bf16[8,128,768]{2,1,0:T(8,128)(2,1)} %get-tuple-element.21) | copy-start | bytes 4718596
  201.2 5.8 %copy-start.22 = (bf16[2,128,1024]{2,1,0:T(8,128)(2,1)S(1)}, bf16[2,128,1024]{2,1,0:T(8,128)(2,1)}, u32[]{:S(2)}) copy-start(bf16[2,128,1024]{2,1,0:T(8,128)(2,1)} %get-tuple-element.22) | copy-start | bytes 1572868
  201.2 5.8 %copy-start.24 = (bf16[4,64,1024]{2,1,0:T(8,128)(2,1)S(1)}, bf16[4,64,1024]{2,1,0:T(8,128)(2,1)}, u32[]{:S(2)}) copy-start(bf16[4,64,1024]{2,1,0:T(8,128)(2,1)} %copy-done.23) | copy-start | bytes 1572868
  201.2 129.5 %reduce-scatter.7.cloned.1.call-start = ((), (), s32[]{:S(2)}) async-start(), calls=%async_computation.7 | async-start | bytes 2621440 | tf_op jit(solution)/shard_map/reduce_scatter | solution.py:430
  209.1 7.6 %copy-start.29 = (f32[32,32]{1,0:T(8,128)S(1)}, f32[32,32]{1,0:T(8,128)}, u32[]{:S(2)}) copy-start(f32[32,32]{1,0:T(8,128)} %get-tuple-element.52) | copy-start | bytes 12292
  209.2 7.7 %copy-start.3 = (bf16[1,256,1024]{2,1,0:T(8,128)(2,1)S(1)}, bf16[1,256,1024]{2,1,0:T(8,128)(2,1)}, u32[]{:S(2)}) copy-start(bf16[1,256,1024]{2,1,0:T(8,128)(2,1)} %param.13) | copy-start | bytes 1572868
  209.2 165.4 %reduce-scatter.17.cloned.1.call-start = ((), (), s32[]{:S(2)}) async-start(), calls=%async_computation.12 | async-start | bytes 2359296 | tf_op jit(solution)/shard_map/reduce_scatter | solution.py:438
  216.8 113.9 %copy-start.8 = (bf16[1,256,1024]{2,1,0:T(8,128)(2,1)S(1)}, bf16[1,256,1024]{2,1,0:T(8,128)(2,1)}, u32[]{:S(2)}) copy-start(bf16[1,256,1024]{2,1,0:T(8,128)(2,1)} %param.25) | copy-start | bytes 1572868
  217.4 2.0 collective-permute-start
  256.9 120.6 %all-to-all-start = ((bf16[4,32,1792]{2,1,0:T(8,128)(2,1)}), bf16[4,32,1792]{2,1,0:T(8,128)(2,1)S(1)}, u32[]{:S(2)}, u32[]{:S(2)}) async-start(bf16[4,32,1792]{2,1,0:T(8,128)(2,1)} %bitcast.38), calls=%async_computation.4 | async-start | bytes 917504 | tf_op jit(solution)/shard_map/all_to_all | solution.py:462
  374.6 5.9 %copy-start.32 = (f32[32]{0:T(128)}, f32[32]{0:T(128)S(1)}, u32[]{:S(2)}) copy-start(f32[32]{0:T(128)S(1)} %get-tuple-element.89) | copy-start | bytes 388
  (20 other events, 48.9 us)
Sparse Core Ops, SparseCore 0:
  128.3 37.7 reduce-scatter.14
  177.1 41.1 reduce-scatter.10
  220.7 34.2 reduce-scatter.12
  258.2 34.4 reduce-scatter.8
  295.5 35.1 reduce-scatter.6
  332.9 35.8 reduce-scatter.16
where the time goes:
time: 396 us; the launch traced here: 388 us
  waiting for transfers between devices  104 us (26%)
  Pallas kernels  88.2 us (22%)
  matrix products  83.2 us (21%)
  blocking collectives  40.3 us (10%)
  other arithmetic  32.2 us (8%)
  local copies, waits for them, and re-layouts  19.7 us (5%)
  between operations  15.2 us (4%)
  starting transfers between devices  5.56 us (1%)
    pallas_call x1, Pallas kernels, gather_all(): pl.pallas_call(functools.partial(gather_kernel, nz, nc), out_shape=[jax.S...  88.2 us
    unnamed x1, blocking collectives  40.3 us
    reduce_scatter x1, waiting for transfers between devices, local(): lax.psum_scatter(partial.astype(b16).reshape(seqs, length, width), 'ctx',...  36.4 us
    reduce_scatter x1, waiting for transfers between devices, local(): lax.psum_scatter(grad_fc1.astype(b16), 'dp', scatter_dimension=0, tiled=T...  35.1 us
    reduce_scatter x1, waiting for transfers between devices, local(): lax.psum_scatter(grad_normed.astype(b16).reshape(seqs, length, width), 'c...  32.2 us
    dot_general x4, matrix products, contract_rows(): lax.dot_general(left, right, (((0,), (0,)), ((), ())), preferred_element_...  15.7 us
    dot_general x4, matrix products, times_transposed(): lax.dot_general(left, right, (((1,), (1,)), ((), ())), preferred_element_...  15.6 us
    dot_general x1, matrix products, backward(): jnp.einsum('sqhd,skhd->shqk', grad_attended, v, preferred_element_type=jn...  15.4 us
  transfers between devices with their start and end apart: 8, of which 3 were waited for; matrix products, arithmetic and copies ran while one was open for 24% of the time, Pallas kernels for 0%

commit v1 on v0

--- a/solution.py
+++ b/solution.py
@@ -2,6 +2,7 @@
 
 import jax
 import jax.numpy as jnp
+import numpy as np
 from jax import lax
 from jax.experimental import pallas as pl
 from jax.experimental.pallas import tpu as pltpu
@@ -97,12 +98,52 @@
     return attended, backward
 
 
-def gather_kernel(
-    nz, nc,
+def dot(left, right, contract):
+    return lax.dot_general(
+        left, right, ((contract[:1], contract[1:]), ((), ())), preferred_element_type=jnp.float32
+    )
+
+
+NORMAL, RIGHT_T, LEFT_T = (1, 0), (1, 1), (0, 0)
+
+
+def turn_tables(length, head_dim, lanes):
+    half = ROT // 2
+    freq = np.float32(1.0) / np.power(
+        np.float32(10000.0), np.arange(0, ROT, 2, dtype=np.float32) / np.float32(ROT)
+    )
+    theta = np.arange(length, dtype=np.float32)[:, None] * freq[None, :]
+    cosine, sine = np.cos(theta), np.sin(theta)
+    keep = np.ones((length, head_dim), np.float32)
+    keep[:, :half] = cosine
+    keep[:, half:ROT] = cosine
+    ahead = np.zeros((length, head_dim), np.float32)
+    ahead[:, :half] = -sine
+    behind = np.zeros((length, head_dim), np.float32)
+    behind[:, half:ROT] = sine
+    return [np.tile(t, (1, lanes // head_dim)) for t in (keep, ahead, behind)]
+
+
+def turn(x, keep, ahead, behind):
+    half, lanes = ROT // 2, x.shape[1]
+    return (
+        x * keep
+        + pltpu.roll(x, lanes - half, axis=1) * ahead
+        + pltpu.roll(x, half, axis=1) * behind
+    )
+
+
+def forward_kernel(
+    nz, nc, marks,
     tok_ref, cot_ref, qkv_ref, fc1_ref, fc2_ref, out_ref, small_ref,
+    seg_row_ref, seg_col_ref, keep_ref, ahead_ref, behind_ref,
+    o_cot, o_qkv, o_fc1, o_fc2, o_out, o_small, o_normed, o_act, o_slope, o_attended, o_gmixed,
     tok_all, cot_all, w_qkv, w_fc1, w_fc2, w_out, small_all,
-    ctx_send, ctx_recv, z_send, z_recv, sib_send, sib_recv, loc,
+    small_rows, vec_d, b_qkv, b_fc1, normed, q_s, k_s, v_s, attended, g_att, act, slope, gmixed,
+    acc_q, acc_k, acc_v, acc_a, bias_s,
+    ctx_send, ctx_recv, z_send, z_recv, sib_send, sib_recv, loc, out_sem,
 ):
+    f32, b16 = jnp.float32, jnp.bfloat16
     d, c = lax.axis_index("dp"), lax.axis_index("ctx")
     z, k = d // 2, lax.rem(d, 2)
     other = 2 * z + 1 - k
@@ -110,6 +151,11 @@
     dl = width // nc
     fr = fc2_ref.shape[0]
     nd = 2 * nz
+    part = tok_ref.shape[0]
+    length = part * nc
+    head_dim = width // HEADS
+    heads = HEADS // nc
+    fl = nd * fr
 
     def ctx_to(j):
         return lax.rem(c + j, nc)
@@ -145,25 +191,19 @@
 
     SMALL, QKV, FC1, TOK, COT, OUT, FC2 = range(7)
 
-    def qkv_pieces(to, owner, sub):
-        return [
-            (qkv_ref.at[:, lanes(t * nc + to, dl)], w_qkv.at[owner, rows(sub), pl.ds(t * dl, dl)])
-            for t in range(3)
-        ]
-
-    def fc1_pieces(to, owner, sub):
-        return [
-            (fc1_ref.at[:, lanes(g * nc + to, fr)], w_fc1.at[owner, rows(sub), pl.ds(g * fr, fr)])
-            for g in range(nd)
-        ]
-
     def ctx_pieces(array, to):
         if array == SMALL:
             return [(small_ref, small_all.at[d, c])]
         if array == QKV:
-            return qkv_pieces(to, d, c)
+            return [
+                (qkv_ref.at[:, lanes(t * nc + to, dl)], w_qkv.at[d, rows(c), pl.ds(t * dl, dl)])
+                for t in range(3)
+            ]
         if array == FC1:
-            return fc1_pieces(to, d, c)
+            return [
+                (fc1_ref.at[:, lanes(g * nc + to, fr)], w_fc1.at[d, rows(c), pl.ds(g * fr, fr)])
+                for g in range(nd)
+            ]
         if array == TOK:
             return [(tok_ref, tok_all.at[c])]
         return [(cot_ref, cot_all.at[c])]
@@ -184,12 +224,21 @@
         for src, dst in ctx_pieces(array, c):
             pltpu.make_async_copy(src, dst, loc.at[array]).start()
 
-    def ctx_finish(array):
+    def ctx_arrive(array, j):
+        got = ctx_whole(array, ctx_from(j))
+        if j == 0:
+            pltpu.make_async_copy(got, got, loc.at[array]).wait()
+        else:
+            remote(got, got, ctx_send.at[array, j], ctx_recv.at[array, j], (d, ctx_to(j))).wait_recv()
+
+    def ctx_sent(array):
         for j in range(1, nc):
             got = ctx_whole(array, ctx_from(j))
-            remote(got, got, ctx_send.at[array, j], ctx_recv.at[array, j], (d, ctx_to(j))).wait()
-        mine = ctx_whole(array, c)
-        pltpu.make_async_copy(mine, mine, loc.at[array]).wait()
+            remote(got, got, ctx_send.at[array, j], ctx_recv.at[array, j], (d, ctx_to(j))).wait_send()
+
+    def ctx_finish(array):
+        for j in range(nc):
+            ctx_arrive(array, j)
 
     blocks = {SMALL: small_all, QKV: w_qkv, FC1: w_fc1, FC2: w_fc2}
 
@@ -214,11 +263,14 @@
             sib_copy(array, j, z_from(j)).start()
 
     def z_finish(array):
+        for j in range(nz):
+            sib_copy(array, j, lax.rem(z + nz - j, nz) * 2 + 1 - k).wait_recv()
+
+    def z_sent(array):
         for j in range(1, nz):
             z_copy(array, j, d).wait_send()
         for j in range(nz):
             sib_copy(array, j, d if j == 0 else z_from(j)).wait_send()
-            sib_copy(array, j, lax.rem(z + nz - j, nz) * 2 + 1 - k).wait_recv()
 
     def out_copy(j, to, sub):
         return remote(out_ref, w_out.at[k, rows(sub), :], ctx_send.at[OUT, j], ctx_recv.at[OUT, j], (d, to))
@@ -228,31 +280,32 @@
     def out_z(j, to):
         return remote(half, half, z_send.at[OUT, j], z_recv.at[OUT, j], (to, c))
 
+    def out_sib(which):
+        piece = w_out.at[which]
+        return remote(piece, piece, sib_send.at[OUT, 0], sib_recv.at[OUT, 0], (other, c))
+
     ctx_start(SMALL)
     ctx_start(QKV)
+    own_out = pltpu.make_async_copy(out_ref, w_out.at[k, rows(c), :], loc.at[OUT])
+
+    @pl.when(z == c)
+    def _():
+        own_out.start()
+
+    for j in range(1, nc):
+        @pl.when(ctx_to(j) == z)
+        def _():
+            out_copy(j, z, c).start()
+
     ctx_start(TOK)
     ctx_start(FC1)
     own_fc2 = pltpu.make_async_copy(fc2_ref, w_fc2.at[d], loc.at[FC2])
     own_fc2.start()
-    own_out = pltpu.make_async_copy(out_ref, w_out.at[k, rows(c), :], loc.at[OUT])
-
-    @pl.when(z == c)
-    def _():
-        own_out.start()
-
-    for j in range(1, nc):
-        @pl.when(ctx_to(j) == z)
-        def _():
-            out_copy(j, z, c).start()
 
     ctx_finish(SMALL)
     z_start(SMALL)
     ctx_finish(QKV)
     z_start(QKV)
-    ctx_start(COT)
-    ctx_finish(FC1)
-    z_start(FC1)
-    z_start(FC2)
 
     @pl.when(z == c)
     def _():
@@ -261,59 +314,259 @@
         own_out.wait()
         for j in range(1, nz):
             out_z(j, z_to(j)).start()
-
+        out_sib(k).start()
+
+    ctx_start(COT)
+    ctx_finish(FC1)
+    z_pass_on(SMALL)
+    z_finish(SMALL)
+
+    def collect(p, carry):
+        small_rows[pl.ds(p, 1), :] = small_all[p // nc, lax.rem(p, nc)]
+        return carry
+
+    lax.fori_loop(0, nd * nc, collect, 0)
+    table = small_rows[...]
+    pack = table.shape[1]
+
+    def vector(mark, size, first, count):
+        entry = lax.broadcasted_iota(jnp.int32, (1, count), 1).astype(f32) + first
+        owner = jnp.floor((entry + 0.5) * (1.0 / size))
+        lane = entry - owner * size + mark
+        pick = lax.broadcasted_iota(jnp.int32, (pack, count), 0).astype(f32) == lane
+        found = dot(table.astype(b16), jnp.where(pick, 1.0, 0.0).astype(b16), NORMAL)
+        here = lax.broadcasted_iota(jnp.int32, (nd * nc, count), 0).astype(f32) == owner
+        return jnp.sum(jnp.where(here, found, 0.0), axis=0, keepdims=True)
+
+    for i in range(2):
+        vec_d[pl.ds(i, 1), :] = vector(marks[2 + i], wr, 0.0, width)
+    for t in range(3):
+        b_qkv[:, pl.ds(t * dl, dl)] = vector(marks[1], 3 * wr, (t * width + c * dl).astype(f32), dl)
+    for g in range(nd):
+        b_fc1[:, pl.ds(g * fr, fr)] = small_all[g, c][:, :fr]
+
+    z_pass_on(QKV)
+    z_start(FC1)
+    z_finish(QKV)
+
+    chunk = 32
+
+    def block_rows(b):
+        return pl.ds(pl.multiple_of(b * part, part), part)
+
+    def normalise_block(b):
+        def step(i, carry):
+            at = pl.multiple_of(i * chunk, chunk)
+            x = tok_all[b, pl.ds(at, chunk), :].astype(f32)
+            x = x - jnp.mean(x, axis=-1, keepdims=True)
+            x = x * lax.rsqrt(jnp.mean(x * x, axis=-1, keepdims=True) + epsilon)
+            normed[pl.ds(pl.multiple_of(b * part, part) + at, chunk), :] = (
+                x * vec_d[0:1, :] + vec_d[1:2, :]
+            ).astype(b16)
+            return carry
+
+        lax.fori_loop(0, part // chunk, step, 0)
+
+    def qkv_block(b):
+        at = block_rows(b)
+        x = normed[at, :]
+        keep = jnp.tile(keep_ref[at, :], (1, dl // keep_ref.shape[1]))
+        ahead = jnp.tile(ahead_ref[at, :], (1, dl // keep_ref.shape[1]))
+        behind = jnp.tile(behind_ref[at, :], (1, dl // keep_ref.shape[1]))
+        for t, to in enumerate((q_s, k_s, v_s)):
+            w = w_qkv[:, :, pl.ds(t * dl, dl)].reshape(width, dl)
+            y = dot(x, w, NORMAL) + b_qkv[:, pl.ds(t * dl, dl)]
+            if t < 2:
+                y = turn(y, keep, ahead, behind)
+            to[at, :] = y.astype(b16)
+
+    for j in range(nc):
+        ctx_arrive(TOK, j)
+        normalise_block(ctx_from(j))
+        qkv_block(ctx_from(j))
+
+    z_pass_on(FC1)
+    z_start(FC2)
+    z_finish(FC1)
+
+    def hidden_block(b, carry):
+        at = block_rows(b)
+        x = normed[at, :]
+        for g in range(0, fl, 256):
+            w = w_fc1[:, :, pl.ds(g, 256)].reshape(width, 256)
+            h = dot(x, w, NORMAL) + b_fc1[:, pl.ds(g, 256)]
+            s = h * h
+            t = jnp.tanh(h * (0.7978845608028654 + (0.7978845608028654 * 0.044715) * s))
+            half_t = 0.5 + 0.5 * t
+            act[at, pl.ds(g, 256)] = (h * half_t).astype(b16)
+            slope[at, pl.ds(g, 256)] = half_t + 0.5 * h * (1.0 - t * t) * (
+                0.7978845608028654 + (3 * 0.7978845608028654 * 0.044715) * s
+            )
+        return carry
+
+    lax.fori_loop(0, nc, hidden_block, 0)
+
+    ctx_finish(COT)
+    for j in range(1, nz):
+        @pl.when(lax.rem(z + nz - j, nz) == c)
+        def _():
+            out_z(j, z_to(j)).wait_recv()
+            out_sib(k).start()
+    out_sib(1 - k).wait_recv()
+
+    w_o = w_out[...].reshape(dl, width)
+
+    def g_att_block(b, carry):
+        g_att[block_rows(b), :] = dot(cot_all[b], w_o, RIGHT_T).astype(b16)
+        return carry
+
+    lax.fori_loop(0, nc, g_att_block, 0)
+
+    tile = 256
+    reach = 512 // tile
+    scale = float(head_dim) ** (-0.5)
+    acc_k[...] = jnp.zeros_like(acc_k)
+    acc_v[...] = jnp.zeros_like(acc_v)
+    for i in range(length // tile):
+        first = max(0, i - reach) * tile
+        count = (i + 1) * tile - first
+        at = pl.ds(i * tile, tile)
+        to = pl.ds(first, count)
+        same = seg_col_ref[at, :1] == seg_row_ref[:1, to]
+        row = lax.broadcasted_iota(jnp.int32, (tile, count), 0) + (i * tile - first)
+        col = lax.broadcasted_iota(jnp.int32, (tile, count), 1)
+        bias_s[:, :count] = jnp.where(same & (col <= row), 0.0, -1e30)
+        acc_q[...] = jnp.zeros_like(acc_q)
+        acc_a[...] = jnp.zeros_like(acc_a)
+
+        def head_step(h, carry):
+            lane = lax.broadcasted_iota(jnp.int32, (1, dl), 1)
+            mine = (lane >= h * head_dim) & (lane < (h + 1) * head_dim)
+            only = jnp.where(mine, 1.0, 0.0)
+            only_low = only.astype(b16)
+            qh = q_s[at, :] * only_low
+            gh = g_att[at, :] * only_low
+            keys, values = k_s[to, :], v_s[to, :]
+            s = dot(qh, keys, RIGHT_T) * scale + bias_s[:, :count]
+            e = jnp.exp(s - jnp.max(s, axis=-1, keepdims=True))
+            p = e * (1.0 / jnp.sum(e, axis=-1, keepdims=True))
+            p_low = p.astype(b16)
+            acc_a[...] += dot(p_low, values, NORMAL) * only
+            gw = dot(gh, values, RIGHT_T)
+            gs = (p * (gw - jnp.sum(gw * p, axis=-1, keepdims=True))).astype(b16)
+            acc_q[...] += dot(gs, keys, NORMAL) * only
+            acc_k[to, :] += dot(gs, qh, LEFT_T)
+            acc_v[to, :] += dot(p_low, gh, LEFT_T)
+            return carry
+
+        lax.fori_loop(0, heads, head_step, 0)
+        attended[at, :] = acc_a[...].astype(b16)
+        wide = (1, dl // keep_ref.shape[1])
+        gmixed[at, pl.ds(0, dl)] = turn(
+            acc_q[...] * scale,
+            jnp.tile(keep_ref[at, :], wide),
+            -jnp.tile(ahead_ref[at, :], wide),
+            -jnp.tile(behind_ref[at, :], wide),
+        ).astype(b16)
+
+    def finish_block(b, carry):
+        at = block_rows(b)
+        wide = (1, dl // keep_ref.shape[1])
+        gmixed[at, pl.ds(dl, dl)] = turn(
+            acc_k[at, :] * scale,
+            jnp.tile(keep_ref[at, :], wide),
+            -jnp.tile(ahead_ref[at, :], wide),
+            -jnp.tile(behind_ref[at, :], wide),
+        ).astype(b16)
+        gmixed[at, pl.ds(2 * dl, dl)] = acc_v[at, :].astype(b16)
+        return carry
+
+    lax.fori_loop(0, nc, finish_block, 0)
+
+    own_fc2.wait()
+    z_pass_on(FC2)
+    z_finish(FC2)
+
+    for array in (SMALL, QKV, FC1, FC2):
+        z_sent(array)
+    for array in (SMALL, QKV, FC1, TOK, COT):
+        ctx_sent(array)
     for j in range(1, nc):
         @pl.when(ctx_to(j) == z)
         def _():
             out_copy(j, z, c).wait_send()
 
-    z_pass_on(SMALL)
-    z_finish(SMALL)
-    z_pass_on(QKV)
-    z_finish(QKV)
-    ctx_finish(TOK)
-    z_pass_on(FC1)
-    z_finish(FC1)
-    ctx_finish(COT)
-    own_fc2.wait()
-    z_pass_on(FC2)
-    z_finish(FC2)
-
-    for j in range(1, nz):
-        @pl.when(lax.rem(z + nz - j, nz) == c)
-        def _():
-            out_z(j, z_to(j)).wait_recv()
-
     @pl.when(z == c)
     def _():
         for j in range(1, nz):
             out_z(j, z_to(j)).wait_send()
 
-    give = remote(half, half, sib_send.at[OUT, 0], sib_recv.at[OUT, 0], (other, c))
-    give.start()
-    give.wait()
-
-
-def gather_all(nz, nc, tokens, cotangent, qkv_weight, fc1_weight, fc2_weight, out_weight, small):
+    out_sib(k).wait_send()
+
+    saves = [
+        (cot_all, o_cot), (w_qkv, o_qkv), (w_fc1, o_fc1), (w_fc2, o_fc2), (w_out, o_out),
+        (small_all, o_small), (normed, o_normed), (act, o_act), (slope, o_slope),
+        (attended, o_attended), (gmixed, o_gmixed),
+    ]
+    for n, (src, dst) in enumerate(saves):
+        pltpu.make_async_copy(src, dst, out_sem.at[n]).start()
+    for n, (src, dst) in enumerate(saves):
+        pltpu.make_async_copy(src, dst, out_sem.at[n]).wait()
+
+
+def forward_all(nz, nc, marks, tokens, cotangent, segments, qkv_weight, fc1_weight, fc2_weight, out_weight, small):
     part, width = tokens.shape
     wr, fr = qkv_weight.shape[0], fc2_weight.shape[0]
     nd, dl = 2 * nz, width // nc
-    b16 = jnp.bfloat16
-    shapes = [
+    length, fl = part * nc, 2 * nz * fr
+    f32, b16 = jnp.float32, jnp.bfloat16
+    tables = [jnp.asarray(t) for t in turn_tables(length, width // HEADS, 128)]
+    seg_row = jnp.broadcast_to(segments.reshape(1, length), (8, length))
+    seg_col = jnp.broadcast_to(segments.reshape(length, 1), (length, 128))
+    gathered = [
         ((nc, part, width), b16),
         ((nc, part, width), b16),
         ((nd, nc * wr, 3 * dl), b16),
-        ((nd, nc * wr, nd * fr), b16),
+        ((nd, nc * wr, fl), b16),
         ((nd, fr, width), b16),
         ((2, nc * wr, width), b16),
-        ((nd, nc) + small.shape, jnp.float32),
+        ((nd, nc) + small.shape, f32),
     ]
+    shapes = gathered[1:] + [
+        ((length, width), b16),
+        ((length, fl), b16),
+        ((length, fl), f32),
+        ((length, dl), b16),
+        ((length, 3 * dl), b16),
+    ]
+    work = gathered + [
+        ((nd * nc, small.shape[1]), f32),
+        ((8, width), f32),
+        ((1, 3 * dl), f32),
+        ((1, fl), f32),
+        ((length, width), b16),
+        ((length, dl), b16),
+        ((length, dl), b16),
+        ((length, dl), b16),
+        ((length, dl), b16),
+        ((length, dl), b16),
+        ((length, fl), b16),
+        ((length, fl), f32),
+        ((length, 3 * dl), b16),
+        ((256, dl), f32),
+        ((length, dl), f32),
+        ((length, dl), f32),
+        ((256, dl), f32),
+        ((256, 768), f32),
+    ]
+    hbm, vmem = pl.BlockSpec(memory_space=pl.ANY), pl.BlockSpec(memory_space=pltpu.VMEM)
     return pl.pallas_call(
-        functools.partial(gather_kernel, nz, nc),
+        functools.partial(forward_kernel, nz, nc, marks),
         out_shape=[jax.ShapeDtypeStruct(s, t) for s, t in shapes],
-        in_specs=[pl.BlockSpec(memory_space=pl.ANY)] * 7,
-        out_specs=[pl.BlockSpec(memory_space=pl.ANY)] * 7,
-        scratch_shapes=[
+        in_specs=[hbm] * 7 + [vmem] * 5,
+        out_specs=[hbm] * len(shapes),
+        scratch_shapes=[pltpu.VMEM(s, t) for s, t in work]
+        + [
             pltpu.SemaphoreType.DMA((7, nc)),
             pltpu.SemaphoreType.DMA((7, nc)),
             pltpu.SemaphoreType.DMA((7, nz)),
@@ -321,10 +574,13 @@
             pltpu.SemaphoreType.DMA((7, nz)),
             pltpu.SemaphoreType.DMA((7, nz)),
             pltpu.SemaphoreType.DMA((7,)),
+            pltpu.SemaphoreType.DMA((len(shapes),)),
         ],
-        compiler_params=pltpu.CompilerParams(collective_id=0, has_side_effects=True),
-        name="gather",
-    )(tokens, cotangent, qkv_weight, fc1_weight, fc2_weight, out_weight, small)
+        compiler_params=pltpu.CompilerParams(
+            collective_id=0, has_side_effects=True, vmem_limit_bytes=60 * 2**20
+        ),
+        name="forward",
+    )(tokens, cotangent, qkv_weight, fc1_weight, fc2_weight, out_weight, small, seg_row, seg_col, *tables)
 
 
 def local(
@@ -356,7 +612,7 @@
     mine = lax.axis_index("ctx")
     devices = dp * ctx
 
-    pieces = [qkv_bias, fc1_bias, out_bias, fc2_bias, norm_gain, norm_shift]
+    pieces = [fc1_bias, qkv_bias, norm_gain, norm_shift, out_bias, fc2_bias]
     marks = [0]
     for piece in pieces:
         marks.append(marks[-1] + piece.shape[0])
@@ -364,19 +620,19 @@
     if direct:
         vector = jnp.concatenate(pieces).astype(f32)
         vector = jnp.pad(vector, (0, -marks[-1] % 128))[None]
-        tokens_all, cot_all, w_qkv, w_fc1, w_fc2, w_out, small = gather_all(
+        cot_all, w_qkv, w_fc1, w_fc2, w_out, small, normed, act, slope, attended, grad_mixed = forward_all(
             dp // 2,
             ctx,
+            tuple(marks),
             tokens[0],
             cotangent[0],
+            segments[0],
             qkv_weight,
             fc1_weight,
             fc2_weight,
             out_weight,
             vector,
         )
-        tokens_all = tokens_all.reshape(seqs, length, width)
-        cot_all = cot_all.reshape(seqs, length, width)
         w_qkv, w_fc1 = w_qkv.reshape(width, 3 * dl), w_fc1.reshape(width, fl)
         w_fc2, w_out = w_fc2.reshape(fl, width), w_out.reshape(dl, width)
         small = small.reshape(devices, -1)
@@ -384,12 +640,12 @@
         small = lax.all_gather(jnp.concatenate(pieces), BOTH, axis=0)
     parts = [small[:, a:b] for a, b in zip(marks, marks[1:])]
     b_qkv = lax.dynamic_index_in_dim(
-        parts[0].reshape(3, ctx, dl), mine, 1, keepdims=False
+        parts[1].reshape(3, ctx, dl), mine, 1, keepdims=False
     ).reshape(3 * dl)
     b_fc1 = lax.dynamic_index_in_dim(
-        parts[1].reshape(dp, ctx, fr), mine, 1, keepdims=False
+        parts[0].reshape(dp, ctx, fr), mine, 1, keepdims=False
     ).reshape(fl)
-    b_out, b_fc2, gain, shift = [p.reshape(width).astype(f32) for p in parts[2:]]
+    gain, shift, b_out, b_fc2 = [p.reshape(width).astype(f32) for p in parts[2:]]
 
     out_perm = [(b, (b % dp) * ctx + b // dp) for b in range(devices)]
     out_back = [(j, i) for i, j in out_perm]
@@ -408,24 +664,26 @@
         tokens_all = lax.all_gather(tokens, "ctx", axis=1, tiled=True)
         cot_all = lax.all_gather(cotangent, "ctx", axis=1, tiled=True)
 
-    positions = jnp.arange(length, dtype=jnp.int32)
-    cosine, sine = angles(positions, ROT)
-
-    scaled_all, _ = normalise(tokens_all.astype(f32).reshape(rows, width))
-    normed = (scaled_all * gain + shift).astype(b16)
     grad_out = cot_all.reshape(rows, width)
-
-    mixed = times(normed, w_qkv) + b_qkv.astype(f32)
-    shape4 = (seqs, length, heads, head_dim)
-    q = rotate(mixed[:, :dl].reshape(shape4), cosine, sine, ROT).astype(b16)
-    k = rotate(mixed[:, dl : 2 * dl].reshape(shape4), cosine, sine, ROT).astype(b16)
-    v = mixed[:, 2 * dl :].astype(b16).reshape(shape4)
-    attended, attention_back = attention(q, k, v, segments, None, cosine, sine)
-    attended = attended.reshape(rows, dl).astype(b16)
-
-    hidden = times(normed, w_fc1) + b_fc1.astype(f32)
-    act, gelu_back = jax.vjp(gelu_tanh, hidden)
-    act = act.astype(b16)
+    if not direct:
+        positions = jnp.arange(length, dtype=jnp.int32)
+        cosine, sine = angles(positions, ROT)
+
+        scaled_all, _ = normalise(tokens_all.astype(f32).reshape(rows, width))
+        normed = (scaled_all * gain + shift).astype(b16)
+
+        mixed = times(normed, w_qkv) + b_qkv.astype(f32)
+        shape4 = (seqs, length, heads, head_dim)
+        q = rotate(mixed[:, :dl].reshape(shape4), cosine, sine, ROT).astype(b16)
+        k = rotate(mixed[:, dl : 2 * dl].reshape(shape4), cosine, sine, ROT).astype(b16)
+        v = mixed[:, 2 * dl :].astype(b16).reshape(shape4)
+        attended, attention_back = attention(q, k, v, segments, None, cosine, sine)
+        attended = attended.reshape(rows, dl).astype(b16)
+
+        hidden = times(normed, w_fc1) + b_fc1.astype(f32)
+        act, gelu_back = jax.vjp(gelu_tanh, hidden)
+        act = act.astype(b16)
+
     partial = times(attended, w_out) + times(act, w_fc2)
     summed = lax.psum_scatter(
         partial.astype(b16).reshape(seqs, length, width), "ctx", scatter_dimension=1, tiled=True
@@ -433,7 +691,7 @@
     result = (tokens.astype(f32) + summed.astype(f32) + (b_out + b_fc2)).astype(b16)
 
     grad_act = times_transposed(grad_out, w_fc2)
-    grad_hidden = gelu_back(grad_act)[0].astype(b16)
+    grad_hidden = (grad_act * slope if direct else gelu_back(grad_act)[0]).astype(b16)
     grad_fc2 = contract_rows(act, grad_out)
     grad_fc2 = lax.psum_scatter(grad_fc2.astype(b16), "dp", scatter_dimension=0, tiled=True)
     grad_fc1 = contract_rows(normed, grad_hidden)
@@ -441,16 +699,17 @@
     grad_fc1 = lax.psum_scatter(grad_fc1.astype(b16), "dp", scatter_dimension=0, tiled=True)
     grad_out_w = contract_rows(attended, grad_out)
     grad_out_w = lax.psum_scatter(grad_out_w.astype(b16), "dp", scatter_dimension=0, tiled=True)
-    grad_attended = times_transposed(grad_out, w_out).astype(b16).reshape(shape4)
-    grad_q, grad_k, grad_v = attention_back(grad_attended)
-    grad_mixed = jnp.concatenate(
-        [
-            rotate(grad_q, cosine, -sine, ROT).reshape(rows, dl),
-            rotate(grad_k, cosine, -sine, ROT).reshape(rows, dl),
-            grad_v.reshape(rows, dl),
-        ],
-        axis=1,
-    ).astype(b16)
+    if not direct:
+        grad_attended = times_transposed(grad_out, w_out).astype(b16).reshape(shape4)
+        grad_q, grad_k, grad_v = attention_back(grad_attended)
+        grad_mixed = jnp.concatenate(
+            [
+                rotate(grad_q, cosine, -sine, ROT).reshape(rows, dl),
+                rotate(grad_k, cosine, -sine, ROT).reshape(rows, dl),
+                grad_v.reshape(rows, dl),
+            ],
+            axis=1,
+        ).astype(b16)
     grad_normed = times_transposed(grad_hidden, w_fc1) + times_transposed(grad_mixed, w_qkv)
     grad_normed = lax.psum_scatter(
         grad_normed.astype(b16).reshape(seqs, length, width), "ctx", scatter_dimension=1, tiled=True
@@ -501,7 +760,7 @@
         axis=1,
     )
     sums = lax.psum_scatter(sums, BOTH, scatter_dimension=0, tiled=True)[0]
-    at = [0, marks[1], marks[2], marks[3], marks[3] + wr, marks[3] + 2 * wr]
+    at = [0, 3 * wr, marks[2], marks[2] + wr, marks[2] + 2 * wr, marks[2] + 3 * wr]
     g_qkv_b, g_fc1_b, g_bias, g_gain, g_shift = [sums[a:b] for a, b in zip(at, at[1:])]
     return (
         result,

time: 396 us -> 379 us (0.957); the launches traced: 388 us -> 378 us
  waiting for transfers between devices: 104 us -> 153 us
  matrix products: 83.2 us -> 37.5 us
  other arithmetic: 32.2 us -> 9.5 us
  Pallas kernels: 88.2 us -> 104 us
  local copies, waits for them, and re-layouts: 19.7 us -> 14.5 us
    dot_general x6 -> x0, matrix products: 37.5 us -> none  [the longest x1 15.4 us: backward(): jnp.einsum('sqhd,skhd->shqk', grad_attended, v, preferred_element_type=jn...]
    reduce_scatter x1, waiting for transfers between devices: 0.01 us -> 33.7 us  [local(): lax.psum_scatter(grad_qkv.astype(b16), 'dp', scatter_dimension=0, tiled=T...]
    pallas_call x1, Pallas kernels: 88.2 us -> 104 us  [forward_all(): pl.pallas_call(functools.partial(forward_kernel, nz, nc, marks), out_shap...]
    reduce_scatter x1, waiting for transfers between devices: 0.02 us -> 13 us  [local(): lax.psum_scatter(grad_out_w.astype(b16), 'dp', scatter_dimension=0, tiled...]
    convert_element_type x4 -> x0, other arithmetic: 10.4 us -> none  [the longest x1 8.79 us: backward(): grad_scores = (probs * (grad_weights - row_dot)).astype(jnp.bfloat16)]
    dot_general x4 -> x2, matrix products: 14.4 us -> 6.64 us  [times(): return jnp.dot(left, right, preferred_element_type=jnp.float32)]
    unnamed x92 -> x26, local copies, waits for them, and re-layouts: 8.48 us -> 1.72 us
    dot_general x4 -> x3, matrix products: 15.6 us -> 10.9 us  [times_transposed(): lax.dot_general(left, right, (((1,), (1,)), ((), ())), preferred_element_...]
  transfers between devices with their start and end apart: 8 -> 8, of which waited for: 3 -> 5; matrix products, arithmetic and copies ran while one was open for 24% -> 12% of each run, Pallas kernels for 0% -> 0%
where the time goes in v1:
time: 379 us; the launch traced here: 378 us
  waiting for transfers between devices  153 us (40%)
  Pallas kernels  104 us (27%)
  blocking collectives  39.5 us (10%)
  matrix products  37.5 us (10%)
  local copies, waits for them, and re-layouts  14.5 us (4%)
  between operations  14.4 us (4%)
  other arithmetic  9.5 us (3%)
  starting transfers between devices  5.81 us (2%)
    pallas_call x1, Pallas kernels, forward_all(): pl.pallas_call(functools.partial(forward_kernel, nz, nc, marks), out_shap...  104 us
    unnamed x1, blocking collectives  39.5 us
    reduce_scatter x1, waiting for transfers between devices, local(): lax.psum_scatter(partial.astype(b16).reshape(seqs, length, width), 'ctx',...  36.6 us
    reduce_scatter x1, waiting for transfers between devices, local(): lax.psum_scatter(grad_fc1.astype(b16), 'dp', scatter_dimension=0, tiled=T...  36 us
    reduce_scatter x1, waiting for transfers between devices, local(): lax.psum_scatter(grad_normed.astype(b16).reshape(seqs, length, width), 'c...  33.8 us
    reduce_scatter x1, waiting for transfers between devices, local(): lax.psum_scatter(grad_qkv.astype(b16), 'dp', scatter_dimension=0, tiled=T...  33.7 us
    dot_general x4, matrix products, contract_rows(): lax.dot_general(left, right, (((0,), (0,)), ((), ())), preferred_element_...  19.9 us
    reduce_scatter x1, waiting for transfers between devices, local(): lax.psum_scatter(grad_out_w.astype(b16), 'dp', scatter_dimension=0, tiled...  13 us
  transfers between devices with their start and end apart: 8, of which 5 were waited for; matrix products, arithmetic and copies ran while one was open for 12% of the time, Pallas kernels for 0%

profile of v1, /device:TPU:0, one launch (start us, length us, event | category | flops | bytes accessed | tf_op | source)
XLA Modules:
  0.0 378.2 jit_solution(10860234622685163750)
XLA Ops:
  7.2 4.1 %concatenate.9 = bf16[352]{0:T(512)(128)(2,1)S(1)} concatenate(bf16[128]{0:T(256)(128)(2,1)} %param.23, bf16[96]{0:T(256)(128)(2,1)} %param.19, bf16[32]{0:T(256)(128)(2,1)} %param.26, bf16[32]{0:T(256)(128)(2,1)} %param.27, bf16[32]{0:T(256)(128)(2,1)} %param.21, bf16[32]{0:T(256)(128)(2,1)} %param.25), dimensions={0} | concatenate | bytes 1408 | tf_op jit(solution)/shard_map/concatenate | solution.py:621
  11.3 0.6 reshape.163.small_ref
  11.9 1.7 broadcast_in_dim.40.seg_col_ref
  13.6 1.3 broadcast_in_dim.39.seg_row_ref
  14.9 103.8 %forward.1 = (bf16[4,256,1024]{2,1,0:T(8,128)(2,1)}, bf16[8,128,768]{2,1,0:T(8,128)(2,1)}, bf16[8,128,1024]{2,1,0:T(8,128)(2,1)}, bf16[8,128,1024]{2,1,0:T(8,128...) custom-call(bf16[256,1024]{1,0:T(8,128)(2,1)} %bitcast.51, ...), custom_call_target="tpu_custom_call" | custom-call | tf_op jit(solution)/shard_map/forward/pallas_call | solution.py:563
  118.7 3.4 convolution_convert_fusion.3
  122.4 5.3 %convert_reduce_fusion = (f32[1024]{0:T(1024)S(1)}, bf16[1024,1024]{1,0:T(8,128)(2,1)S(1)}) fusion(f32[1024,1024]{1,0:T(8,128)} %get-tuple-element.29, bf16[1024,1024]{1,0:T(8,128)(2,1)S(1)} %bitcast.54, bf16[1024,1024]{1,0:T(8,128)(2,1)} %bitcast.65), kind=kOutput, calls=%fused_computation | convolution fusion | flops 2151676928 | bytes 10489856 | tf_op jit(solution)/shard_map/dot_general | solution.py:45
  127.8 2.4 fusion.18
  130.4 3.2 fusion
  133.7 4.6 %fusion.17 = f32[1024,1024]{1,0:T(8,128)S(1)} fusion(bf16[1024,1024]{1,0:T(8,128)(2,1)} %get-tuple-element.25, bf16[1024,1024]{1,0:T(8,128)(2,1)} %bitcast.66), kind=kOutput, calls=%fused_computation.47 | convolution fusion | flops 2147483648 | bytes 8388608 | tf_op jit(solution)/shard_map/dot_general | solution.py:51
  138.3 2.0 fusion.1
  140.4 5.1 %convolution_convert_fusion.2 = bf16[1024,768]{1,0:T(8,128)(2,1)} fusion(bf16[1024,1024]{1,0:T(8,128)(2,1)} %get-tuple-element.33, bf16[1024,768]{1,0:T(8,128)(2,1)} %get-tuple-element.31), kind=kOutput, calls=%fused_computation.8 | convolution fusion | flops 1611399168 | bytes 5242880 | tf_op jit(solution)/shard_map/dot_general | solution.py:39
  145.6 6.1 %convolution_convert_fusion.1 = bf16[1024,1024]{1,0:T(8,128)(2,1)} fusion(bf16[1024,1024]{1,0:T(8,128)(2,1)} %get-tuple-element.33, bf16[1024,1024]{1,0:T(8,128)(2,1)} %copy-done.11), kind=kOutput, calls=%fused_computation.7 | convolution fusion | flops 2148532224 | bytes 6291456 | tf_op jit(solution)/shard_map/dot_general | solution.py:39
  152.0 5.3 %convolution_convert_fusion = bf16[1024,1024]{1,0:T(8,128)(2,1)} fusion(bf16[1024,1024]{1,0:T(8,128)(2,1)} %get-tuple-element.25, bf16[1024,1024]{1,0:T(8,128)(2,1)S(1)} %bitcast.55), kind=kOutput, calls=%fused_computation.6 | convolution fusion | flops 2148532224 | bytes 6291456 | tf_op jit(solution)/shard_map/dot_general | solution.py:39
  157.5 0.8 copy-done
  158.9 13.0 %reduce-scatter.15.cloned.1.call-done = bf16[32,1024]{1,0:T(8,128)(2,1)} async-done(((bf16[256,1024]{1,0:T(8,128)(2,1)}), bf16[32,1024]{1,0:T(8,128)(2,1)}) %reduce-scatter.15.cloned.1.call-update) | async-done | bytes 65552 | tf_op jit(solution)/shard_map/reduce_scatter | solution.py:701
  171.8 1.5 collective-permute-start
  174.0 0.7 convert_element_type.73
  174.6 33.8 %reduce-scatter.9.cloned.1.call-done = bf16[1,256,1024]{2,1,0:T(8,128)(2,1)} async-done(((bf16[1,1024,1024]{2,1,0:T(8,128)(2,1)}), bf16[1,256,1024]{2,1,0:T(8,128)(2,1)}) %reduce-scatter.9.cloned.1.call-update) | async-done | bytes 524304 | tf_op jit(solution)/shard_map/reduce_scatter | solution.py:714
  208.5 1.6 fusion.15
  210.1 36.6 %reduce-scatter.7.cloned.1.call-done = bf16[1,256,1024]{2,1,0:T(8,128)(2,1)} async-done(((bf16[1,1024,1024]{2,1,0:T(8,128)(2,1)}), bf16[1,256,1024]{2,1,0:T(8,128)(2,1)}) %reduce-scatter.7.cloned.1.call-update) | async-done | bytes 524304 | tf_op jit(solution)/shard_map/reduce_scatter | solution.py:688
  246.7 2.7 convert_reduce_fusion.4
  249.6 33.7 %reduce-scatter.11.cloned.1.call-done = bf16[128,768]{1,0:T(8,128)(2,1)} async-done(((bf16[1024,768]{1,0:T(8,128)(2,1)}), bf16[128,768]{1,0:T(8,128)(2,1)}) %reduce-scatter.11.cloned.1.call-update) | async-done | bytes 196624 | tf_op jit(solution)/shard_map/reduce_scatter | solution.py:719
  283.2 36.0 %reduce-scatter.13.cloned.1.call-done = bf16[128,1024]{1,0:T(8,128)(2,1)} async-done(((bf16[1024,1024]{1,0:T(8,128)(2,1)}), bf16[128,1024]{1,0:T(8,128)(2,1)}) %reduce-scatter.13.cloned.1.call-update) | async-done | bytes 262160 | tf_op jit(solution)/shard_map/reduce_scatter | solution.py:699
  319.3 1.8 pad_maximum_fusion
  321.1 3.7 all-to-all-start
  324.8 39.5 %all-reduce.1 = f32[32,320]{1,0:T(8,128)S(1)} all-reduce(f32[32,320]{1,0:T(8,128)S(1)} %concatenate.11), channel_id=6, replica_groups=mesh['dp'=8,'ctx'=4] {'dp','ctx'}, use_global_device_ids=true, to_apply=%region_13.14.clone | all-reduce | flops 10240 | bytes 81920
  364.4 0.6 dynamic-slice_bitcast_fusion
  365.0 1.8 convert_element_type.75
  367.3 0.6 dynamic-slice_bitcast_fusion.2
  368.4 1.0 reshape.162
  369.9 0.9 reshape.155
  (68 shorter events, 4.6 us)
Async XLA Ops:
  7.2 164.6 %reduce-scatter.15.cloned.1.call-start = ((), (), s32[]{:S(2)}) async-start(), calls=%async_computation.11 | async-start | bytes 589824 | tf_op jit(solution)/shard_map/reduce_scatter | solution.py:701
  118.7 3.7 copy-start.2
  122.1 86.4 %reduce-scatter.9.cloned.1.call-start = ((), (), s32[]{:S(2)}) async-start(), calls=%async_computation.8 | async-start | bytes 2621440 | tf_op jit(solution)/shard_map/reduce_scatter | solution.py:714
  122.4 5.4 %copy-start.9 = (bf16[8,128,1024]{2,1,0:T(8,128)(2,1)S(1)}, bf16[8,128,1024]{2,1,0:T(8,128)(2,1)}, u32[]{:S(2)}) copy-start(bf16[8,128,1024]{2,1,0:T(8,128)(2,1)} %get-tuple-element.30) | copy-start | bytes 6291460
  127.7 2.4 copy-start.11
  127.7 2.4 copy-start.4
  127.8 2.6 copy-start.10
  133.6 113.1 %reduce-scatter.7.cloned.1.call-start = ((), (), s32[]{:S(2)}) async-start(), calls=%async_computation.7 | async-start | bytes 2621440 | tf_op jit(solution)/shard_map/reduce_scatter | solution.py:688
  133.7 4.7 %copy-start.1 = (bf16[1024,256]{1,0:T(8,128)(2,1)S(1)}, bf16[1024,256]{1,0:T(8,128)(2,1)}, u32[]{:S(2)}) copy-start(bf16[1024,256]{1,0:T(8,128)(2,1)} %get-tuple-element.23) | copy-start | bytes 1572868
  133.7 4.7 %copy-start.6 = (bf16[2,128,1024]{2,1,0:T(8,128)(2,1)S(1)}, bf16[2,128,1024]{2,1,0:T(8,128)(2,1)}, u32[]{:S(2)}) copy-start(bf16[2,128,1024]{2,1,0:T(8,128)(2,1)} %get-tuple-element.24) | copy-start | bytes 1572868
  140.4 142.9 %reduce-scatter.11.cloned.1.call-start = ((), (), s32[]{:S(2)}) async-start(), calls=%async_computation.9 | async-start | bytes 1769472 | tf_op jit(solution)/shard_map/reduce_scatter | solution.py:719
  145.5 173.7 %reduce-scatter.13.cloned.1.call-start = ((), (), s32[]{:S(2)}) async-start(), calls=%async_computation.10 | async-start | bytes 2359296 | tf_op jit(solution)/shard_map/reduce_scatter | solution.py:699
  151.7 213.3 %reduce-scatter.17.cloned.1.call-start = ((), (), s32[]{:S(2)}) async-start(), calls=%async_computation.12 | async-start | bytes 2359296 | tf_op jit(solution)/shard_map/reduce_scatter | solution.py:696
  151.9 5.4 %copy-start.7 = (f32[8,4,1,384]{3,2,1,0:T(1,128)S(1)}, f32[8,4,1,384]{3,2,1,0:T(1,128)}, u32[]{:S(2)}) copy-start(f32[8,4,1,384]{3,2,1,0:T(1,128)} %get-tuple-element.27) | copy-start | bytes 147460
  157.3 1.0 copy-start
  157.3 16.0 %copy-start.5 = (bf16[1024,768]{1,0:T(8,128)(2,1)S(1)}, bf16[1024,768]{1,0:T(8,128)(2,1)}, u32[]{:S(2)}) copy-start(bf16[1024,768]{1,0:T(8,128)(2,1)} %get-tuple-element.31) | copy-start | bytes 4718596
  158.3 88.3 %copy-start.3 = (bf16[1,256,1024]{2,1,0:T(8,128)(2,1)S(1)}, bf16[1,256,1024]{2,1,0:T(8,128)(2,1)}, u32[]{:S(2)}) copy-start(bf16[1,256,1024]{2,1,0:T(8,128)(2,1)} %param.28) | copy-start | bytes 1572868
  171.8 2.1 collective-permute-start
  321.1 46.8 %all-to-all-start = ((bf16[4,32,1792]{2,1,0:T(8,128)(2,1)}), bf16[4,32,1792]{2,1,0:T(8,128)(2,1)S(1)}, u32[]{:S(2)}, u32[]{:S(2)}) async-start(bf16[4,32,1792]{2,1,0:T(8,128)(2,1)} %bitcast.10), calls=%async_computation.4 | async-start | bytes 917504 | tf_op jit(solution)/shard_map/all_to_all | solution.py:721
  365.0 5.9 %copy-start.8 = (f32[32]{0:T(128)}, f32[32]{0:T(128)S(1)}, u32[]{:S(2)}) copy-start(f32[32]{0:T(128)S(1)} %get-tuple-element.71) | copy-start | bytes 388
Sparse Core Ops, SparseCore 0:
  122.2 49.5 reduce-scatter.14
  175.1 33.3 reduce-scatter.8
  211.5 35.1 reduce-scatter.6
  248.9 34.2 reduce-scatter.10
  285.5 33.7 reduce-scatter.12
  321.5 34.6 reduce-scatter.16

commit v2 on v1

v2 whole, which is shorter than its diff:
```python
import functools

import jax
import jax.numpy as jnp
import numpy as np
from jax import lax
from jax.experimental import pallas as pl
from jax.experimental.pallas import tpu as pltpu
from jax.sharding import PartitionSpec as P

HEADS = 16
ROT = 32
epsilon = 1e-05
BOTH = ("dp", "ctx")
MESH = pl.DeviceIdType.MESH


def angles(positions, rotary):
    freq_table = 1.0 / 10000.0 ** (jnp.arange(0, rotary, 2, dtype=jnp.float32) / rotary)
    theta = positions.astype(jnp.float32)[:, None] * freq_table[None, :]
    return (jnp.cos(theta)[:, None, :], jnp.sin(theta)[:, None, :])


def rotate(tensor, cosine, sine_table, rotary):
    half_len = rotary // 2
    first_half = tensor[..., :half_len]
    second_half = tensor[..., half_len:rotary]
    return jnp.concatenate(
        [
            first_half * cosine - second_half * sine_table,
            second_half * cosine + first_half * sine_table,
            tensor[..., rotary:],
        ],
        axis=-1,
    )


def contract_rows(left, right):
    return lax.dot_general(
        left, right, (((0,), (0,)), ((), ())), preferred_element_type=jnp.float32
    )


def times_transposed(left, right):
    return lax.dot_general(
        left, right, (((1,), (1,)), ((), ())), preferred_element_type=jnp.float32
    )


def times(left, right):
    return jnp.dot(left, right, preferred_element_type=jnp.float32)


def gelu_tanh(hidden_in):
    return jax.nn.gelu(hidden_in, approximate=True)


def normalise(inputs):
    center = inputs - jnp.mean(inputs, axis=-1, keepdims=True)
    inverse = lax.rsqrt(jnp.mean(center * center, axis=-1, keepdims=True) + epsilon)
    return center * inverse, inverse


def attention(q, k, v, segments, back, cosine, sine):
    length, head_dim = q.shape[1], q.shape[3]
    scale = float(head_dim) ** (-0.5)
    index = jnp.arange(length, dtype=jnp.int32)
    allowed = (segments[:, :, None] == segments[:, None, :]) & (index[None, :] <= index[:, None])[
        None
    ]
    scores = jnp.einsum("sqhd,skhd->shqk", q, k, preferred_element_type=jnp.float32) * scale
    scores = jnp.where(allowed[:, None], scores, -1e30)
    row_max = jnp.max(scores, axis=-1, keepdims=True)
    log_total = row_max + jnp.log(jnp.sum(jnp.exp(scores - row_max), axis=-1, keepdims=True))
    probs = jnp.exp(scores - log_total)
    probs_low = probs.astype(jnp.bfloat16)
    attended = jnp.einsum("shqk,skhd->sqhd", probs_low, v, preferred_element_type=jnp.float32)

    def backward(grad_attended):
        grad_weights = jnp.einsum(
            "sqhd,skhd->shqk", grad_attended, v, preferred_element_type=jnp.float32
        )
        row_dot = jnp.sum(grad_weights * probs, axis=-1, keepdims=True)
        grad_scores = (probs * (grad_weights - row_dot)).astype(jnp.bfloat16)
        grad_q = (
            jnp.einsum("shqk,skhd->sqhd", grad_scores, k, preferred_element_type=jnp.float32)
            * scale
        )
        grad_k = (
            jnp.einsum("shqk,sqhd->skhd", grad_scores, q, preferred_element_type=jnp.float32)
            * scale
        )
        grad_v = jnp.einsum(
            "shqk,sqhd->skhd", probs_low, grad_attended, preferred_element_type=jnp.float32
        )
        return grad_q, grad_k, grad_v

    return attended, backward


def local(
    dp,
    ctx,
    tokens,
    segments,
    qkv_weight,
    qkv_bias,
    out_weight,
    out_bias,
    fc1_weight,
    fc1_bias,
    fc2_weight,
    fc2_bias,
    norm_gain,
    norm_shift,
    cotangent,
):
    f32, b16 = jnp.float32, jnp.bfloat16
    seqs, part, width = tokens.shape
    length = part * ctx
    rows = seqs * length
    ff = fc1_weight.shape[1]
    fl, dl = ff // ctx, width // ctx
    heads = HEADS // ctx
    head_dim = width // HEADS
    wr, fr = qkv_weight.shape[0], fc2_weight.shape[0]
    mine = lax.axis_index("ctx")
    devices = dp * ctx

    pieces = [qkv_bias, fc1_bias, out_bias, fc2_bias, norm_gain, norm_shift]
    marks = [0]
    for piece in pieces:
        marks.append(marks[-1] + piece.shape[0])
    small = lax.all_gather(jnp.concatenate(pieces), BOTH, axis=0)
    parts = [small[:, a:b] for a, b in zip(marks, marks[1:])]
    b_qkv = lax.dynamic_index_in_dim(
        parts[0].reshape(3, ctx, dl), mine, 1, keepdims=False
    ).reshape(3 * dl)
    b_fc1 = lax.dynamic_index_in_dim(
        parts[1].reshape(dp, ctx, fr), mine, 1, keepdims=False
    ).reshape(fl)
    b_out, b_fc2, gain, shift = [p.reshape(width).astype(f32) for p in parts[2:]]

    send_qkv = jnp.moveaxis(qkv_weight.reshape(wr, 3, ctx, dl), 2, 0).reshape(ctx, wr, 3 * dl)
    send_fc1 = jnp.moveaxis(fc1_weight.reshape(wr, dp, ctx, fr), 2, 0).reshape(ctx, wr, fl)
    sent = lax.all_to_all(
        jnp.concatenate([send_qkv, send_fc1], axis=2), "ctx", split_axis=0, concat_axis=0
    )
    out_perm = [(b, (b % dp) * ctx + b // dp) for b in range(devices)]
    out_back = [(j, i) for i, j in out_perm]
    out_piece = lax.ppermute(out_weight, BOTH, out_perm)
    w_qkv = lax.all_gather(sent[:, :, : 3 * dl], "dp", axis=0).reshape(width, 3 * dl)
    w_fc1 = lax.all_gather(sent[:, :, 3 * dl :], "dp", axis=0).reshape(width, fl)
    w_fc2 = lax.all_gather(fc2_weight, "dp", axis=0).reshape(fl, width)
    w_out = lax.all_gather(out_piece, "dp", axis=0).reshape(dl, width)

    tokens_all = lax.all_gather(tokens, "ctx", axis=1, tiled=True)
    cot_all = lax.all_gather(cotangent, "ctx", axis=1, tiled=True)

    positions = jnp.arange(length, dtype=jnp.int32)
    cosine, sine = angles(positions, ROT)

    scaled_all, _ = normalise(tokens_all.astype(f32).reshape(rows, width))
    normed = (scaled_all * gain + shift).astype(b16)
    grad_out = cot_all.reshape(rows, width)

    mixed = times(normed, w_qkv) + b_qkv.astype(f32)
    shape4 = (seqs, length, heads, head_dim)
    q = rotate(mixed[:, :dl].reshape(shape4), cosine, sine, ROT).astype(b16)
    k = rotate(mixed[:, dl : 2 * dl].reshape(shape4), cosine, sine, ROT).astype(b16)
    v = mixed[:, 2 * dl :].astype(b16).reshape(shape4)
    attended, attention_back = attention(q, k, v, segments, None, cosine, sine)
    attended = attended.reshape(rows, dl).astype(b16)

    hidden = times(normed, w_fc1) + b_fc1.astype(f32)
    act, gelu_back = jax.vjp(gelu_tanh, hidden)
    act = act.astype(b16)
    partial = times(attended, w_out) + times(act, w_fc2)
    summed = lax.psum_scatter(
        partial.astype(b16).reshape(seqs, length, width), "ctx", scatter_dimension=1, tiled=True
    )
    result = (tokens.astype(f32) + summed.astype(f32) + (b_out + b_fc2)).astype(b16)

    grad_act = times_transposed(grad_out, w_fc2)
    grad_hidden = gelu_back(grad_act)[0].astype(b16)
    grad_fc2 = contract_rows(act, grad_out)
    grad_fc2 = lax.psum_scatter(grad_fc2.astype(b16), "dp", scatter_dimension=0, tiled=True)
    grad_fc1 = contract_rows(normed, grad_hidden)
    grad_fc1_b = jnp.sum(grad_hidden, axis=0, dtype=f32)
    grad_fc1 = lax.psum_scatter(grad_fc1.astype(b16), "dp", scatter_dimension=0, tiled=True)
    grad_out_w = contract_rows(attended, grad_out)
    grad_out_w = lax.psum_scatter(grad_out_w.astype(b16), "dp", scatter_dimension=0, tiled=True)
    grad_attended = times_transposed(grad_out, w_out).astype(b16).reshape(shape4)
    grad_q, grad_k, grad_v = attention_back(grad_attended)
    grad_mixed = jnp.concatenate(
        [
            rotate(grad_q, cosine, -sine, ROT).reshape(rows, dl),
            rotate(grad_k, cosine, -sine, ROT).reshape(rows, dl),
            grad_v.reshape(rows, dl),
        ],
        axis=1,
    ).astype(b16)
    grad_normed = times_transposed(grad_hidden, w_fc1) + times_transposed(grad_mixed, w_qkv)
    grad_normed = lax.psum_scatter(
        grad_normed.astype(b16).reshape(seqs, length, width), "ctx", scatter_dimension=1, tiled=True
    ).astype(f32)
    grad_qkv = contract_rows(normed, grad_mixed)
    grad_qkv_b = jnp.sum(grad_mixed, axis=0, dtype=f32)
    grad_qkv = lax.psum_scatter(grad_qkv.astype(b16), "dp", scatter_dimension=0, tiled=True)

    back = lax.all_to_all(
        jnp.concatenate([grad_qkv, grad_fc1], axis=1).reshape(ctx, wr, 3 * dl + fl),
        "ctx",
        split_axis=0,
        concat_axis=0,
    ).astype(f32)
    grad_qkv = jnp.moveaxis(back[:, :, : 3 * dl].reshape(ctx, wr, 3, dl), 0, 2).reshape(
        wr, 3 * width
    )
    grad_fc1 = jnp.moveaxis(back[:, :, 3 * dl :].reshape(ctx, wr, dp, fr), 0, 2).reshape(wr, ff)
    grad_out_w = lax.ppermute(grad_out_w, BOTH, out_back).astype(f32)
    grad_fc2 = grad_fc2.astype(f32)

    grad_normed = grad_normed.reshape(seqs, part, width)
    own = tokens.astype(f32)
    cot = cotangent.astype(f32)
    scaled, inverse = normalise(own)
    grad_gain = jnp.sum(grad_normed * scaled, axis=(0, 1))
    grad_shift = jnp.sum(grad_normed, axis=(0, 1))
    grad_scaled = grad_normed * gain
    grad_input = inverse * (
        grad_scaled
        - jnp.mean(grad_scaled, axis=-1, keepdims=True)
        - scaled * jnp.mean(grad_scaled * scaled, axis=-1, keepdims=True)
    )
    grad_tokens = (cot + grad_input).astype(b16)

    wide_qkv_b = lax.dynamic_update_index_in_dim(
        jnp.zeros((3, ctx, dl), f32), grad_qkv_b.reshape(3, dl), mine, 1
    )
    wide_fc1_b = lax.dynamic_update_index_in_dim(
        jnp.zeros((dp, ctx, fr), f32), grad_fc1_b.reshape(dp, fr), mine, 1
    )
    bias_out = jnp.sum(cot, axis=(0, 1))
    sums = jnp.concatenate(
        [
            x.reshape(devices, -1)
            for x in (wide_qkv_b, wide_fc1_b, bias_out, grad_gain, grad_shift)
        ],
        axis=1,
    )
    sums = lax.psum_scatter(sums, BOTH, scatter_dimension=0, tiled=True)[0]
    at = [0, marks[1], marks[2], marks[3], marks[3] + wr, marks[3] + 2 * wr]
    g_qkv_b, g_fc1_b, g_bias, g_gain, g_shift = [sums[a:b] for a, b in zip(at, at[1:])]
    return (
        result,
        grad_tokens,
        grad_qkv,
        g_qkv_b,
        grad_out_w,
        g_bias,
        grad_fc1,
        g_fc1_b,
        grad_fc2,
        g_bias,
        g_gain,
        g_shift,
    )


def dot(left, right, contract):
    return lax.dot_general(
        left, right, ((contract[:1], contract[1:]), ((), ())), preferred_element_type=jnp.float32
    )


NORMAL, RIGHT_T, LEFT_T = (1, 0), (1, 1), (0, 0)


def turn_tables(length, head_dim, lanes):
    half = ROT // 2
    freq = np.float32(1.0) / np.power(
        np.float32(10000.0), np.arange(0, ROT, 2, dtype=np.float32) / np.float32(ROT)
    )
    theta = np.arange(length, dtype=np.float32)[:, None] * freq[None, :]
    cosine, sine = np.cos(theta), np.sin(theta)
    keep = np.ones((length, head_dim), np.float32)
    keep[:, :half] = cosine
    keep[:, half:ROT] = cosine
    ahead = np.zeros((length, head_dim), np.float32)
    ahead[:, :half] = -sine
    behind = np.zeros((length, head_dim), np.float32)
    behind[:, half:ROT] = sine
    return [np.tile(t, (1, lanes // head_dim)) for t in (keep, ahead, behind)]


def turn(x, keep, ahead, behind):
    half, lanes = ROT // 2, x.shape[1]
    return (
        x * keep
        + pltpu.roll(x, lanes - half, axis=1) * ahead
        + pltpu.roll(x, half, axis=1) * behind
    )


def layer_kernel(
    nz, nc, marks,
    tok_ref, cot_ref, qkv_ref, fc1_ref, fc2_ref, out_ref, small_ref,
    seg_row_ref, seg_col_ref, keep_ref, ahead_ref, behind_ref,
    o_result, o_tokens, o_qkv, o_out, o_fc1, o_fc2, o_sums,
    tok_all, cot_all, w_qkv, w_fc1, w_fc2, w_out, small_all,
    small_rows, vec_d, b_qkv, b_fc1, normed, q_s, k_s, v_s, attended, g_att, act, slope, gmixed,
    acc_q, acc_k, acc_v, acc_a, bias_s, g_hidden,
    give_qkv, give_fc1, give_fc2, give_out, got_qkv, got_fc1, got_fc2, got_out,
    own_qkv, own_fc1, own_fc2, own_out_g, far_qkv, far_fc1, far_fc2, far_out,
    part_got, part_own, norm_got, norm_own,
    swap_qkv, swap_fc1, swap_out, swapped_qkv, swapped_fc1, swapped_out,
    sums, sums_sib, sums_z, sums_mine,
    ctx_send, ctx_recv, z_send, z_recv, sib_send, sib_recv, loc,
    back_z_send, back_z_recv, back_sib_send, back_sib_recv, back_ctx_send, back_ctx_recv,
):
    f32, b16 = jnp.float32, jnp.bfloat16
    d, c = lax.axis_index("dp"), lax.axis_index("ctx")
    z, k = d // 2, lax.rem(d, 2)
    other = 2 * z + 1 - k
    wr, width = out_ref.shape
    dl = width // nc
    fr = fc2_ref.shape[0]
    nd = 2 * nz
    part = tok_ref.shape[0]
    length = part * nc
    head_dim = width // HEADS
    heads = HEADS // nc
    fl = nd * fr

    def ctx_to(j):
        return lax.rem(c + j, nc)

    def ctx_from(j):
        return lax.rem(c + nc - j, nc)

    def z_to(j):
        return 2 * lax.rem(z + j, nz) + k

    def z_from(j):
        return 2 * lax.rem(z + nz - j, nz) + k

    barrier = pltpu.get_barrier_semaphore()
    for j in range(1, nc):
        pl.semaphore_signal(barrier, inc=1, device_id=(d, ctx_to(j)), device_id_type=MESH)
    for j in range(1, nz):
        pl.semaphore_signal(barrier, inc=1, device_id=(z_to(j), c), device_id_type=MESH)
    pl.semaphore_signal(barrier, inc=1, device_id=(other, c), device_id_type=MESH)
    pl.semaphore_wait(barrier, nc + nz - 1)

    def remote(src, dst, send, recv, device):
        return pltpu.make_async_remote_copy(
            src_ref=src, dst_ref=dst, send_sem=send, recv_sem=recv,
            device_id=device, device_id_type=MESH,
        )

    def rows(at):
        return pl.ds(pl.multiple_of(at * wr, wr), wr)

    def lanes(at, size):
        return pl.ds(pl.multiple_of(at * size, size), size)

    SMALL, QKV, FC1, TOK, COT, OUT, FC2 = range(7)

    def ctx_pieces(array, to):
        if array == SMALL:
            return [(small_ref, small_all.at[d, c])]
        if array == QKV:
            return [
                (qkv_ref.at[:, lanes(t * nc + to, dl)], w_qkv.at[d, rows(c), pl.ds(t * dl, dl)])
                for t in range(3)
            ]
        if array == FC1:
            return [
                (fc1_ref.at[:, lanes(g * nc + to, fr)], w_fc1.at[d, rows(c), pl.ds(g * fr, fr)])
                for g in range(nd)
            ]
        if array == TOK:
            return [(tok_ref, tok_all.at[c])]
        return [(cot_ref, cot_all.at[c])]

    def ctx_whole(array, sub):
        return {
            SMALL: lambda: small_all.at[d, sub],
            QKV: lambda: w_qkv.at[d, rows(sub), :],
            FC1: lambda: w_fc1.at[d, rows(sub), :],
            TOK: lambda: tok_all.at[sub],
            COT: lambda: cot_all.at[sub],
        }[array]()

    def ctx_start(array):
        for j in range(1, nc):
            for src, dst in ctx_pieces(array, ctx_to(j)):
                remote(src, dst, ctx_send.at[array, j], ctx_recv.at[array, j], (d, ctx_to(j))).start()
        for src, dst in ctx_pieces(array, c):
            pltpu.make_async_copy(src, dst, loc.at[array]).start()

    def ctx_arrive(array, j):
        got = ctx_whole(array, ctx_from(j))
        if j == 0:
            pltpu.make_async_copy(got, got, loc.at[array]).wait()
        else:
            remote(got, got, ctx_send.at[array, j], ctx_recv.at[array, j], (d, ctx_to(j))).wait_recv()

    def ctx_sent(array):
        for j in range(1, nc):
            got = ctx_whole(array, ctx_from(j))
            remote(got, got, ctx_send.at[array, j], ctx_recv.at[array, j], (d, ctx_to(j))).wait_send()

    def ctx_finish(array):
        for j in range(nc):
            ctx_arrive(array, j)

    blocks = {SMALL: small_all, QKV: w_qkv, FC1: w_fc1, FC2: w_fc2}

    def z_copy(array, j, own):
        block = blocks[array].at[own]
        src = fc2_ref if array == FC2 else block
        return remote(src, block, z_send.at[array, j], z_recv.at[array, j], (z_to(j), c))

    def sib_copy(array, j, at):
        block = blocks[array].at[at]
        src = fc2_ref if array == FC2 and j == 0 else block
        return remote(src, block, sib_send.at[array, j], sib_recv.at[array, j], (other, c))

    def z_start(array):
        for j in range(1, nz):
            z_copy(array, j, d).start()
        sib_copy(array, 0, d).start()

    def z_pass_on(array):
        for j in range(1, nz):
            z_copy(array, j, z_from(j)).wait_recv()
            sib_copy(array, j, z_from(j)).start()

    def z_finish(array):
        for j in range(nz):
            sib_copy(array, j, lax.rem(z + nz - j, nz) * 2 + 1 - k).wait_recv()

    def z_sent(array):
        for j in range(1, nz):
            z_copy(array, j, d).wait_send()
        for j in range(nz):
            sib_copy(array, j, d if j == 0 else z_from(j)).wait_send()

    def out_copy(j, to, sub):
        return remote(out_ref, w_out.at[k, rows(sub), :], ctx_send.at[OUT, j], ctx_recv.at[OUT, j], (d, to))

    half = w_out.at[k]

    def out_z(j, to):
        return remote(half, half, z_send.at[OUT, j], z_recv.at[OUT, j], (to, c))

    def out_sib(which):
        piece = w_out.at[which]
        return remote(piece, piece, sib_send.at[OUT, 0], sib_recv.at[OUT, 0], (other, c))

    ctx_start(SMALL)
    ctx_start(QKV)
    own_out = pltpu.make_async_copy(out_ref, w_out.at[k, rows(c), :], loc.at[OUT])

    @pl.when(z == c)
    def _():
        own_out.start()

    for j in range(1, nc):
        @pl.when(ctx_to(j) == z)
        def _():
            out_copy(j, z, c).start()

    ctx_start(TOK)
    ctx_start(FC1)
    copy_fc2 = pltpu.make_async_copy(fc2_ref, w_fc2.at[d], loc.at[FC2])
    copy_fc2.start()

    ctx_finish(SMALL)
    z_start(SMALL)
    ctx_finish(QKV)
    z_start(QKV)

    @pl.when(z == c)
    def _():
        for j in range(1, nc):
            out_copy(j, z, ctx_from(j)).wait_recv()
        own_out.wait()
        for j in range(1, nz):
            out_z(j, z_to(j)).start()
        out_sib(k).start()

    ctx_start(COT)
    ctx_finish(FC1)
    z_pass_on(SMALL)
    z_finish(SMALL)

    def collect(p, carry):
        small_rows[pl.ds(p, 1), :] = small_all[p // nc, lax.rem(p, nc)]
        return carry

    lax.fori_loop(0, nd * nc, collect, 0)
    table = small_rows[...]
    pack = table.shape[1]

    def vector(mark, size, first, count):
        entry = lax.broadcasted_iota(jnp.int32, (1, count), 1).astype(f32) + first
        owner = jnp.floor((entry + 0.5) * (1.0 / size))
        lane = entry - owner * size + mark
        pick = lax.broadcasted_iota(jnp.int32, (pack, count), 0).astype(f32) == lane
        found = dot(table.astype(b16), jnp.where(pick, 1.0, 0.0).astype(b16), NORMAL)
        here = lax.broadcasted_iota(jnp.int32, (nd * nc, count), 0).astype(f32) == owner
        return jnp.sum(jnp.where(here, found, 0.0), axis=0, keepdims=True)

    for i in range(2):
        vec_d[pl.ds(i, 1), :] = vector(marks[2 + i], wr, 0.0, width)
    vec_d[2:3, :] = vector(marks[4], wr, 0.0, width) + vector(marks[5], wr, 0.0, width)
    for t in range(3):
        b_qkv[:, pl.ds(t * dl, dl)] = vector(marks[1], 3 * wr, (t * width + c * dl).astype(f32), dl)
    for g in range(nd):
        b_fc1[:, pl.ds(g * fr, fr)] = small_all[g, c][:, :fr]

    z_pass_on(QKV)
    z_start(FC1)
    z_finish(QKV)

    chunk = 32

    def block_rows(b):
        return pl.ds(pl.multiple_of(b * part, part), part)

    def normalise_block(b):
        def step(i, carry):
            at = pl.multiple_of(i * chunk, chunk)
            x = tok_all[b, pl.ds(at, chunk), :].astype(f32)
            x = x - jnp.mean(x, axis=-1, keepdims=True)
            x = x * lax.rsqrt(jnp.mean(x * x, axis=-1, keepdims=True) + epsilon)
            normed[pl.ds(pl.multiple_of(b * part, part) + at, chunk), :] = (
                x * vec_d[0:1, :] + vec_d[1:2, :]
            ).astype(b16)
            return carry

        lax.fori_loop(0, part // chunk, step, 0)

    def qkv_block(b):
        at = block_rows(b)
        x = normed[at, :]
        keep = jnp.tile(keep_ref[at, :], (1, dl // keep_ref.shape[1]))
        ahead = jnp.tile(ahead_ref[at, :], (1, dl // keep_ref.shape[1]))
        behind = jnp.tile(behind_ref[at, :], (1, dl // keep_ref.shape[1]))
        for t, to in enumerate((q_s, k_s, v_s)):
            w = w_qkv[:, :, pl.ds(t * dl, dl)].reshape(width, dl)
            y = dot(x, w, NORMAL) + b_qkv[:, pl.ds(t * dl, dl)]
            if t < 2:
                y = turn(y, keep, ahead, behind)
            to[at, :] = y.astype(b16)

    for j in range(nc):
        ctx_arrive(TOK, j)
        normalise_block(ctx_from(j))
        qkv_block(ctx_from(j))

    z_pass_on(FC1)
    z_start(FC2)
    z_finish(FC1)

    def hidden_block(b, carry):
        at = block_rows(b)
        x = normed[at, :]
        for g in range(0, fl, 256):
            w = w_fc1[:, :, pl.ds(g, 256)].reshape(width, 256)
            h = dot(x, w, NORMAL) + b_fc1[:, pl.ds(g, 256)]
            s = h * h
            t = jnp.tanh(h * (0.7978845608028654 + (0.7978845608028654 * 0.044715) * s))
            half_t = 0.5 + 0.5 * t
            act[at, pl.ds(g, 256)] = (h * half_t).astype(b16)
            slope[at, pl.ds(g, 256)] = half_t + 0.5 * h * (1.0 - t * t) * (
                0.7978845608028654 + (3 * 0.7978845608028654 * 0.044715) * s
            )
        return carry

    lax.fori_loop(0, nc, hidden_block, 0)

    ctx_finish(COT)

    gives = {QKV: give_qkv, FC1: give_fc1, FC2: give_fc2, OUT: give_out}
    gots = {QKV: got_qkv, FC1: got_fc1, FC2: got_fc2, OUT: got_out}
    owns = {QKV: own_qkv, FC1: own_fc1, FC2: own_fc2, OUT: own_out_g}
    fars = {QKV: far_qkv, FC1: far_fc1, FC2: far_fc2, OUT: far_out}

    def cotangents():
        return cot_all[...].reshape(length, width)

    def weight_gradient(array, left, right):
        give, own = gives[array], owns[array]
        size = give.shape[1]

        def step(i, carry):
            both = dot(left[:, lanes(i, 2 * size)], right(), LEFT_T)
            low, high = both[:size], both[size:]
            own[i] = jnp.where(k == 0, low, high)
            give[i] = jnp.where(k == 0, high, low).astype(b16)
            return carry

        lax.fori_loop(0, give.shape[0], step, 0)
        to_sibling(array).start()

    def to_sibling(array):
        return remote(
            gives[array], gots[array], back_sib_send.at[array], back_sib_recv.at[array], (other, c)
        )

    def z_other(j):
        return lax.rem(z + j, nz)

    def to_owner(array, j):
        block = gives[array].at[0 if array == OUT else z_other(j)]
        return remote(
            block, fars[array].at[j - 1], back_z_send.at[array, j], back_z_recv.at[array, j], (z_to(j), c)
        )

    def add_sibling(array):
        to_sibling(array).wait()
        give, got, own = gives[array], gots[array], owns[array]
        for j in range(1, nz):
            if array == OUT:
                @pl.when(z_other(j) == c)
                def _():
                    give[0] = (own[0] + got[0].astype(f32)).astype(b16)
                    to_owner(OUT, j).start()
            else:
                at = z_other(j)
                give[at] = (own[at] + got[at].astype(f32)).astype(b16)
                to_owner(array, j).start()

    def total(array):
        at = 0 if array == OUT else z
        x = owns[array][at] + gots[array][at].astype(f32)
        for j in range(1, nz):
            x = x + fars[array][j - 1].astype(f32)
        return x

    PART, NORM, SUMS = TOK, COT, SMALL

    def over_ctx(array, src, dst, j, to):
        return remote(src, dst, back_ctx_send.at[array, j], back_ctx_recv.at[array, j], (d, to))

    weight_gradient(FC2, act, cotangents)

    for j in range(1, nz):
        @pl.when(lax.rem(z + nz - j, nz) == c)
        def _():
            out_z(j, z_to(j)).wait_recv()
            out_sib(k).start()
    out_sib(1 - k).wait_recv()

    w_o = w_out[...].reshape(dl, width)

    def g_att_block(b, carry):
        g_att[block_rows(b), :] = dot(cot_all[b], w_o, RIGHT_T).astype(b16)
        return carry

    lax.fori_loop(0, nc, g_att_block, 0)
    add_sibling(FC2)

    tile = 256
    reach = 512 // tile
    scale = float(head_dim) ** (-0.5)
    acc_k[...] = jnp.zeros_like(acc_k)
    acc_v[...] = jnp.zeros_like(acc_v)
    for i in range(length // tile):
        first = max(0, i - reach) * tile
        count = (i + 1) * tile - first
        at = pl.ds(i * tile, tile)
        to = pl.ds(first, count)
        same = seg_col_ref[at, :1] == seg_row_ref[:1, to]
        row = lax.broadcasted_iota(jnp.int32, (tile, count), 0) + (i * tile - first)
        col = lax.broadcasted_iota(jnp.int32, (tile, count), 1)
        bias_s[:, :count] = jnp.where(same & (col <= row), 0.0, -1e30)
        acc_q[...] = jnp.zeros_like(acc_q)
        acc_a[...] = jnp.zeros_like(acc_a)

        def head_step(h, carry):
            lane = lax.broadcasted_iota(jnp.int32, (1, dl), 1)
            mine = (lane >= h * head_dim) & (lane < (h + 1) * head_dim)
            only = jnp.where(mine, 1.0, 0.0)
            only_low = only.astype(b16)
            qh = q_s[at, :] * only_low
            gh = g_att[at, :] * only_low
            keys, values = k_s[to, :], v_s[to, :]
            s = dot(qh, keys, RIGHT_T) * scale + bias_s[:, :count]
            e = jnp.exp(s - jnp.max(s, axis=-1, keepdims=True))
            p = e * (1.0 / jnp.sum(e, axis=-1, keepdims=True))
            p_low = p.astype(b16)
            acc_a[...] += dot(p_low, values, NORMAL) * only
            gw = dot(gh, values, RIGHT_T)
            gs = (p * (gw - jnp.sum(gw * p, axis=-1, keepdims=True))).astype(b16)
            acc_q[...] += dot(gs, keys, NORMAL) * only
            acc_k[to, :] += dot(gs, qh, LEFT_T)
            acc_v[to, :] += dot(p_low, gh, LEFT_T)
            return carry

        lax.fori_loop(0, heads, head_step, 0)
        attended[at, :] = acc_a[...].astype(b16)
        wide = (1, dl // keep_ref.shape[1])
        gmixed[at, pl.ds(0, dl)] = turn(
            acc_q[...] * scale,
            jnp.tile(keep_ref[at, :], wide),
            -jnp.tile(ahead_ref[at, :], wide),
            -jnp.tile(behind_ref[at, :], wide),
        ).astype(b16)

    def finish_block(b, carry):
        at = block_rows(b)
        wide = (1, dl // keep_ref.shape[1])
        gmixed[at, pl.ds(dl, dl)] = turn(
            acc_k[at, :] * scale,
            jnp.tile(keep_ref[at, :], wide),
            -jnp.tile(ahead_ref[at, :], wide),
            -jnp.tile(behind_ref[at, :], wide),
        ).astype(b16)
        gmixed[at, pl.ds(2 * dl, dl)] = acc_v[at, :].astype(b16)
        return carry

    lax.fori_loop(0, nc, finish_block, 0)

    weight_gradient(QKV, normed, lambda: gmixed[...])
    weight_gradient(OUT, attended, cotangents)

    copy_fc2.wait()
    z_pass_on(FC2)
    z_finish(FC2)

    def hidden_gradient(b, carry):
        at = block_rows(b)
        g = cot_all[b]
        for i in range(nd):
            to = pl.ds(i * fr, fr)
            g_hidden[at, to] = (dot(g, w_fc2[i], RIGHT_T) * slope[at, to]).astype(b16)
        return carry

    lax.fori_loop(0, nc, hidden_gradient, 0)
    add_sibling(QKV)
    add_sibling(OUT)
    weight_gradient(FC1, normed, lambda: g_hidden[...])

    def result_term(b):
        at = block_rows(b)
        return dot(attended[at, :], w_out[...].reshape(dl, width), NORMAL) + dot(
            act[at, :], w_fc2[...].reshape(fl, width), NORMAL
        )

    for j in range(1, nc):
        b = ctx_to(j)
        tok_all[b] = result_term(b).astype(b16)
        over_ctx(PART, tok_all.at[b], part_got.at[j - 1], j, b).start()
    part_own[...] = result_term(c)
    add_sibling(FC1)

    def normed_term(b):
        at = block_rows(b)
        return dot(g_hidden[at, :], w_fc1[...].reshape(width, fl), RIGHT_T) + dot(
            gmixed[at, :], w_qkv[...].reshape(width, 3 * dl), RIGHT_T
        )

    for j in range(1, nc):
        b = ctx_to(j)
        cot_all[b] = normed_term(b).astype(b16)
        over_ctx(NORM, cot_all.at[b], norm_got.at[j - 1], j, b).start()
    norm_own[...] = normed_term(c)

    ones = jnp.ones((8, length), b16)
    sums[0, :, pl.ds(0, 3 * dl)] = dot(ones, gmixed[...], NORMAL)[:1]
    sums[0, :, pl.ds(3 * dl, fl)] = dot(ones, g_hidden[...], NORMAL)[:1]
    at_sum = 3 * dl + fl
    sums[0, :, pl.ds(at_sum, width)] = dot(ones[:, :part], cot_all[c], NORMAL)[:1]

    for j in range(1, nc):
        over_ctx(PART, tok_all.at[c], part_got.at[j - 1], j, c).wait_recv()

    def result_step(i, carry):
        at = pl.ds(pl.multiple_of(i * chunk, chunk), chunk)
        y = tok_all[c, at, :].astype(f32) + part_own[at, :] + vec_d[2:3, :]
        for j in range(1, nc):
            y = y + part_got[j - 1, at, :].astype(f32)
        o_result[at, :] = y.astype(b16)
        return carry

    lax.fori_loop(0, part // chunk, result_step, 0)

    for j in range(1, nc):
        over_ctx(NORM, cot_all.at[c], norm_got.at[j - 1], j, c).wait_recv()

    def norm_step(i, carry):
        gain_sum, shift_sum = carry
        at = pl.ds(pl.multiple_of(i * chunk, chunk), chunk)
        x = tok_all[c, at, :].astype(f32)
        x = x - jnp.mean(x, axis=-1, keepdims=True)
        inverse = lax.rsqrt(jnp.mean(x * x, axis=-1, keepdims=True) + epsilon)
        x = x * inverse
        g = norm_own[at, :]
        for j in range(1, nc):
            g = g + norm_got[j - 1, at, :].astype(f32)
        v = g * vec_d[0:1, :]
        y = inverse * (
            v - jnp.mean(v, axis=-1, keepdims=True) - x * jnp.mean(v * x, axis=-1, keepdims=True)
        )
        o_tokens[at, :] = (cot_all[c, at, :].astype(f32) + y).astype(b16)
        return (
            gain_sum + jnp.sum(g * x, axis=0, keepdims=True),
            shift_sum + jnp.sum(g, axis=0, keepdims=True),
        )

    zero = jnp.zeros((1, width), f32)
    gain_sum, shift_sum = lax.fori_loop(0, part // chunk, norm_step, (zero, zero))
    sums[0, :, pl.ds(at_sum + width, width)] = gain_sum
    sums[0, :, pl.ds(at_sum + 2 * width, width)] = shift_sum

    sum_sib = remote(sums.at[0], sums_sib.at[0], back_sib_send.at[SUMS], back_sib_recv.at[SUMS], (other, c))
    sum_sib.start()
    sum_sib.wait()
    sums[1] = sums[0] + sums_sib[0]

    def sum_z(j):
        return remote(
            sums.at[1], sums_z.at[j - 1], back_z_send.at[SUMS, j], back_z_recv.at[SUMS, j], (z_to(j), c)
        )

    for j in range(1, nz):
        sum_z(j).start()

    def from_owner(array):
        for j in range(1, nz):
            to_owner(array, j).wait_recv()

    from_owner(FC2)
    o_fc2[...] = total(FC2)

    swaps = {QKV: (swap_qkv, swapped_qkv), FC1: (swap_fc1, swapped_fc1)}

    def place(array, source, x):
        if array == QKV:
            for t in range(3):
                o_qkv[:, lanes(t * nc + source, dl)] = x[:, t * dl : (t + 1) * dl]
        else:
            for g in range(nd):
                o_fc1[:, lanes(g * nc + source, fr)] = x[:, g * fr : (g + 1) * fr]

    def swap_start(array):
        from_owner(array)
        src, dst = swaps[array]
        own = owns[array]
        own[z] = total(array)
        for j in range(1, nc):
            src[j - 1] = own[z, rows(ctx_to(j)), :].astype(b16)
            over_ctx(array, src.at[j - 1], dst.at[j - 1], j, ctx_to(j)).start()
        place(array, c, own[z, rows(c), :])

    def swap_finish(array):
        src, dst = swaps[array]
        for j in range(1, nc):
            over_ctx(array, src.at[j - 1], dst.at[j - 1], j, ctx_to(j)).wait_recv()
            place(array, ctx_from(j), dst[j - 1].astype(f32))

    swap_start(QKV)

    @pl.when(z == c)
    def _():
        from_owner(OUT)
        own_out_g[0] = total(OUT)
        for j in range(1, nc):
            swap_out[j - 1] = own_out_g[0, rows(ctx_to(j)), :].astype(b16)
            over_ctx(OUT, swap_out.at[j - 1], swapped_out.at[0], j, ctx_to(j)).start()
        o_out[...] = own_out_g[0, rows(c), :]

    for j in range(1, nz):
        sum_z(j).wait()
    mine_sum = sums[1]
    for j in range(1, nz):
        mine_sum = mine_sum + sums_z[j - 1]
    sums_mine[0] = mine_sum
    o_sums[c] = mine_sum
    for j in range(1, nc):
        over_ctx(SUMS, sums_mine.at[0], o_sums.at[c], j, ctx_to(j)).start()

    swap_finish(QKV)
    for j in range(1, nc):
        @pl.when(ctx_from(j) == z)
        def _():
            over_ctx(OUT, swap_out.at[0], swapped_out.at[0], j, ctx_to(j)).wait_recv()
            o_out[...] = swapped_out[0].astype(f32)
    for j in range(1, nc):
        over_ctx(SUMS, sums_mine.at[0], o_sums.at[ctx_from(j)], j, ctx_to(j)).wait_recv()

    swap_start(FC1)
    swap_finish(FC1)

    for array in (SMALL, QKV, FC1, FC2):
        z_sent(array)
    for array in (SMALL, QKV, FC1, TOK, COT):
        ctx_sent(array)
    for j in range(1, nc):
        @pl.when(ctx_to(j) == z)
        def _():
            out_copy(j, z, c).wait_send()

    @pl.when(z == c)
    def _():
        for j in range(1, nz):
            out_z(j, z_to(j)).wait_send()

    out_sib(k).wait_send()
    for array in (QKV, FC1, FC2):
        for j in range(1, nz):
            to_owner(array, j).wait_send()
    for j in range(1, nz):
        @pl.when(z_other(j) == c)
        def _():
            to_owner(OUT, j).wait_send()
    for j in range(1, nc):
        over_ctx(PART, tok_all.at[c], part_got.at[j - 1], j, c).wait_send()
        over_ctx(NORM, cot_all.at[c], norm_got.at[j - 1], j, c).wait_send()
        over_ctx(SUMS, sums_mine.at[0], o_sums.at[c], j, ctx_to(j)).wait_send()
        for array in (QKV, FC1):
            over_ctx(array, swaps[array][0].at[j - 1], swaps[array][1].at[j - 1], j, c).wait_send()

    @pl.when(z == c)
    def _():
        for j in range(1, nc):
            over_ctx(OUT, swap_out.at[j - 1], swapped_out.at[0], j, ctx_to(j)).wait_send()


def layer_all(nz, nc, marks, tokens, cotangent, segments, qkv_weight, fc1_weight, fc2_weight, out_weight, small):
    part, width = tokens.shape
    wr, fr = qkv_weight.shape[0], fc2_weight.shape[0]
    nd, dl = 2 * nz, width // nc
    length, fl = part * nc, 2 * nz * fr
    cw = nc * wr
    f32, b16 = jnp.float32, jnp.bfloat16
    tables = [jnp.asarray(t) for t in turn_tables(length, width // HEADS, 128)]
    seg_row = jnp.broadcast_to(segments.reshape(1, length), (8, length))
    seg_col = jnp.broadcast_to(segments.reshape(length, 1), (length, 128))
    pack = small.shape[1]
    total = 3 * dl + fl + 3 * width
    tile, window = 256, 768
    results = [
        ((part, width), b16),
        ((part, width), b16),
        ((wr, 3 * width), f32),
        ((wr, width), f32),
        ((wr, fl * nc), f32),
        ((fr, width), f32),
        ((nc, 1, total), f32),
    ]
    work = [
        ((nc, part, width), b16),
        ((nc, part, width), b16),
        ((nd, cw, 3 * dl), b16),
        ((nd, cw, fl), b16),
        ((nd, fr, width), b16),
        ((2, cw, width), b16),
        ((nd, nc, 1, pack), f32),
        ((nd * nc, pack), f32),
        ((8, width), f32),
        ((1, 3 * dl), f32),
        ((1, fl), f32),
        ((length, width), b16),
        ((length, dl), b16),
        ((length, dl), b16),
        ((length, dl), b16),
        ((length, dl), b16),
        ((length, dl), b16),
        ((length, fl), b16),
        ((length, fl), f32),
        ((length, 3 * dl), b16),
        ((tile, dl), f32),
        ((length, dl), f32),
        ((length, dl), f32),
        ((tile, dl), f32),
        ((tile, window), f32),
        ((length, fl), b16),
    ]
    grads = [(nz, cw, 3 * dl), (nz, cw, fl), (nz, fr, width), (1, cw, width)]
    fars = [(nz - 1,) + g[1:] for g in grads]
    work += [(g, b16) for g in grads] + [(g, b16) for g in grads] + [(g, f32) for g in grads]
    work += [(g, b16) for g in fars]
    work += [((nc - 1, part, width), b16), ((part, width), f32)] * 2
    work += [((nc - 1, wr, n), b16) for n in (3 * dl, fl, width)]
    work += [((nc - 1, wr, n), b16) for n in (3 * dl, fl)] + [((1, wr, width), b16)]
    work += [((n, 1, total), f32) for n in (2, 1, nz - 1, 1)]
    dma = pltpu.SemaphoreType.DMA
    sems = [(7, nc), (7, nc), (7, nz), (7, nz), (7, nz), (7, nz), (7,)]
    sems += [(7, nz), (7, nz), (7,), (7,), (7, nc), (7, nc)]
    hbm, vmem = pl.BlockSpec(memory_space=pl.ANY), pl.BlockSpec(memory_space=pltpu.VMEM)
    return pl.pallas_call(
        functools.partial(layer_kernel, nz, nc, marks),
        out_shape=[jax.ShapeDtypeStruct(s, t) for s, t in results],
        in_specs=[hbm] * 7 + [vmem] * 5,
        out_specs=[vmem] * len(results),
        scratch_shapes=[pltpu.VMEM(s, t) for s, t in work] + [dma(s) for s in sems],
        compiler_params=pltpu.CompilerParams(
            collective_id=0, has_side_effects=True, vmem_limit_bytes=62 * 2**20
        ),
        name="layer",
    )(tokens, cotangent, qkv_weight, fc1_weight, fc2_weight, out_weight, small, seg_row, seg_col, *tables)


def local_direct(
    dp,
    ctx,
    tokens,
    segments,
    qkv_weight,
    qkv_bias,
    out_weight,
    out_bias,
    fc1_weight,
    fc1_bias,
    fc2_weight,
    fc2_bias,
    norm_gain,
    norm_shift,
    cotangent,
):
    width = tokens.shape[-1]
    dl, fl = width // ctx, fc1_weight.shape[1] // ctx
    wr, fr = qkv_weight.shape[0], fc2_weight.shape[0]
    pieces = [fc1_bias, qkv_bias, norm_gain, norm_shift, out_bias, fc2_bias]
    marks = [0]
    for piece in pieces:
        marks.append(marks[-1] + piece.shape[0])
    vector = jnp.concatenate(pieces).astype(jnp.float32)
    vector = jnp.pad(vector, (0, -marks[-1] % 128))[None]
    result, grad_tokens, grad_qkv, grad_out, grad_fc1, grad_fc2, sums = layer_all(
        dp // 2,
        ctx,
        tuple(marks),
        tokens[0],
        cotangent[0],
        segments[0],
        qkv_weight,
        fc1_weight,
        fc2_weight,
        out_weight,
        vector,
    )
    sums = sums[:, 0]
    mine, group = lax.axis_index("ctx"), lax.axis_index("dp")
    place = group * ctx + mine
    whole_qkv = jnp.moveaxis(sums[:, : 3 * dl].reshape(ctx, 3, dl), 0, 1).reshape(3 * width)
    g_qkv_b = lax.dynamic_slice_in_dim(whole_qkv, place * 3 * wr, 3 * wr)
    g_fc1_b = lax.dynamic_slice(sums, (mine, 3 * dl + group * fr), (1, fr))[0]
    wide = jnp.sum(sums[:, 3 * dl + fl :], axis=0).reshape(3, width)
    wide = lax.dynamic_slice(wide, (0, place * wr), (3, wr))
    return (
        result[None],
        grad_tokens[None],
        grad_qkv,
        g_qkv_b,
        grad_out,
        wide[0],
        grad_fc1,
        g_fc1_b,
        grad_fc2,
        wide[0],
        wide[1],
        wide[2],
    )


def solution(mesh):
    sizes = (mesh.shape["dp"], mesh.shape["ctx"])
    seq, mat, vec = P("dp", "ctx", None), P(BOTH, None), P(BOTH)

    def spread(*args):
        dp, ctx = sizes
        tokens, qkv_weight, fc2_weight = args[0], args[2], args[8]
        direct = (
            dp == 2 * ctx
            and tokens.shape[0] == 1
            and tokens.shape[1] % 256 == 0
            and qkv_weight.shape[0] % 32 == 0
            and fc2_weight.shape[0] % 128 == 0
        )
        return (local_direct if direct else local)(*sizes, *args)

    placed = (seq, P("dp", None), mat, vec, mat, vec, mat, vec, mat, vec, vec, vec, seq)
    return jax.shard_map(
        spread,
        mesh=mesh,
        in_specs=placed,
        out_specs=(seq, seq, mat, vec, mat, vec, mat, vec, mat, vec, vec, vec),
        check_vma=False,
    )
```

time: 379 us -> 217 us (0.57)
  waiting for transfers between devices: 153 us -> 0 us
  Pallas kernels: 104 us -> 201 us
  blocking collectives: 39.5 us -> 0 us
  matrix products: 37.5 us -> 0 us
  between operations: 14.4 us -> 0.76 us
  other arithmetic: 9.5 us -> 0.03 us
  starting transfers between devices: 5.81 us -> 0 us
    reduce_scatter x6 -> x0, waiting for transfers between devices: 153 us -> none  [the longest x1 36.6 us: local(): lax.psum_scatter(partial.astype(b16).reshape(seqs, length, width), 'ctx',...]
    pallas_call x1, Pallas kernels: 104 us -> 201 us  [layer_all(): pl.pallas_call(functools.partial(layer_kernel, nz, nc, marks), out_shape=...]
    unnamed x1 -> x0, blocking collectives: 39.5 us -> none
    dot_general x9 -> x0, matrix products: 37.5 us -> none  [the longest x4 19.9 us: contract_rows(): lax.dot_general(left, right, (((0,), (0,)), ((), ())), preferred_element_...]
    unnamed x26 -> x35, local copies, waits for them, and re-layouts: 1.72 us -> 9.02 us
    reduce_sum x5 -> x1, other arithmetic: 5.01 us -> 0.03 us  [local_direct(): wide = jnp.sum(sums[:, 3 * dl + fl:], axis=0).reshape(3, width)]
    concatenate x2 -> x1, local copies, waits for them, and re-layouts: 4.18 us -> 0.1 us  [local_direct(): vector = jnp.concatenate(pieces).astype(jnp.float32)]
  transfers between devices with their start and end apart: 8 -> 0, of which waited for: 5 -> 0; matrix products, arithmetic and copies ran while one was open for 12% -> 0% of each run, Pallas kernels for 0% -> 0%
where the time goes in v2:
time: 217 us; the launch traced here: 216 us
  Pallas kernels  201 us (93%)
  local copies, waits for them, and re-layouts  13.6 us (6%)
    pallas_call x1, Pallas kernels, layer_all(): pl.pallas_call(functools.partial(layer_kernel, nz, nc, marks), out_shape=...  201 us
    unnamed x35, local copies, waits for them, and re-layouts  9.02 us

profile of v2, /device:TPU:0, one launch (start us, length us, event | category | flops | bytes accessed | tf_op | source)
XLA Modules:
  0.0 215.7 jit_solution(182379902734526727)
XLA Ops:
  0.6 0.0 copy-start.10
  0.7 0.0 copy-start.11
  0.7 0.0 copy-start.12
  0.7 0.0 copy-start.7
  0.7 0.0 copy-start.8
  0.7 0.6 copy-done.10
  1.3 0.0 copy-done.11
  1.3 0.0 copy-done.12
  1.3 0.0 copy-done.7
  1.3 0.0 copy-done.8
  1.4 0.0 copy-done.9
  1.4 0.1 concatenate.3
  1.5 0.6 reshape.39.small_ref
  2.1 0.1 copy-done.5
  2.2 0.6 broadcast_in_dim.26.seg_row_ref
  2.8 1.0 broadcast_in_dim.27.seg_col_ref
  3.8 201.2 %layer.1 = (bf16[256,1024]{1,0:T(8,128)(2,1)}, bf16[256,1024]{1,0:T(8,128)(2,1)}, f32[32,3072]{1,0:T(8,128)}, f32[32,1024]{1,0:T(8,128)}, f32[32,4096]{1,0:T(8,1...) custom-call(bf16[256,1024]{1,0:T(8,128)(2,1)} %bitcast.21, bf16[256,1024]{1,0:T(8,128)(2,1)} %bitcast.22, ...), custom_call_target="tpu_custom_call" | custom-call | tf_op jit(solution)/shard_map/layer/pallas_call | solution.py:997
  205.0 0.9 copy.31
  206.0 0.6 dynamic_slice.9
  206.6 0.1 constant_dynamic-slice_fusion
  206.7 0.5 slice_bitcast_fusion
  207.2 1.1 dynamic-slice_bitcast_fusion
  208.3 0.5 copy.39
  208.9 1.9 copy.40
  210.8 0.8 copy.41
  211.6 0.4 copy-done.3
  212.0 0.7 copy.42
  212.7 0.2 copy-done.4
  213.0 0.7 copy.43
  213.6 0.8 copy.44
  214.4 0.4 copy-done
  214.9 0.8 copy.45
  (16 shorter events, 0.1 us)
Async XLA Ops:
  0.6 0.7 copy-start.10
  0.7 0.7 copy-start.11
  0.7 0.7 copy-start.12
  0.7 0.7 copy-start.7
  0.7 0.7 copy-start.8
  0.7 0.7 copy-start.9
  1.5 0.7 copy-start.5
  207.2 1.1 copy-start.6
  208.9 1.9 copy-start.2
  210.8 1.2 copy-start.3
  212.0 1.0 copy-start.4
  212.0 1.7 copy-start.1
  213.6 1.2 copy-start

commit v3 on v2

--- a/solution.py
+++ b/solution.py
@@ -303,19 +303,25 @@
     )
 
 
+DELTAS = (-2, 2, -1, 1)
+SLOTS = (0, 0, 1, 2)
+PASSED = 4
+
+
 def layer_kernel(
     nz, nc, marks,
     tok_ref, cot_ref, qkv_ref, fc1_ref, fc2_ref, out_ref, small_ref,
-    seg_row_ref, seg_col_ref, keep_ref, ahead_ref, behind_ref,
+    seg_ref, keep_ref, ahead_ref, behind_ref,
     o_result, o_tokens, o_qkv, o_out, o_fc1, o_fc2, o_sums,
     tok_all, cot_all, w_qkv, w_fc1, w_fc2, w_out, small_all,
     small_rows, vec_d, b_qkv, b_fc1, normed, q_s, k_s, v_s, attended, g_att, act, slope, gmixed,
     acc_q, acc_k, acc_v, acc_a, bias_s, g_hidden,
     give_qkv, give_fc1, give_fc2, give_out, got_qkv, got_fc1, got_fc2, got_out,
     own_qkv, own_fc1, own_fc2, own_out_g, far_qkv, far_fc1, far_fc2, far_out,
+    pass_qkv, pass_fc1, pass_fc2, pass_out, log_s, seg_col,
     part_got, part_own, norm_got, norm_own,
     swap_qkv, swap_fc1, swap_out, swapped_qkv, swapped_fc1, swapped_out,
-    sums, sums_sib, sums_z, sums_mine,
+    sums, sums_sib, sums_z,
     ctx_send, ctx_recv, z_send, z_recv, sib_send, sib_recv, loc,
     back_z_send, back_z_recv, back_sib_send, back_sib_recv, back_ctx_send, back_ctx_recv,
 ):
@@ -339,19 +345,22 @@
     def ctx_from(j):
         return lax.rem(c + nc - j, nc)
 
-    def z_to(j):
-        return 2 * lax.rem(z + j, nz) + k
-
-    def z_from(j):
-        return 2 * lax.rem(z + nz - j, nz) + k
+    def exists(delta):
+        return (z + delta >= 0) & (z + delta < nz)
+
+    def plane(delta):
+        return 2 * jnp.clip(z + delta, 0, nz - 1) + k
 
     barrier = pltpu.get_barrier_semaphore()
     for j in range(1, nc):
         pl.semaphore_signal(barrier, inc=1, device_id=(d, ctx_to(j)), device_id_type=MESH)
-    for j in range(1, nz):
-        pl.semaphore_signal(barrier, inc=1, device_id=(z_to(j), c), device_id_type=MESH)
+    for delta in DELTAS:
+        @pl.when(exists(delta))
+        def _():
+            pl.semaphore_signal(barrier, inc=1, device_id=(plane(delta), c), device_id_type=MESH)
     pl.semaphore_signal(barrier, inc=1, device_id=(other, c), device_id_type=MESH)
-    pl.semaphore_wait(barrier, nc + nz - 1)
+    planes = jnp.minimum(z, 2) + jnp.minimum(nz - 1 - z, 2)
+    pl.semaphore_wait(barrier, nc + planes)
 
     def remote(src, dst, send, recv, device):
         return pltpu.make_async_remote_copy(
@@ -365,7 +374,8 @@
     def lanes(at, size):
         return pl.ds(pl.multiple_of(at * size, size), size)
 
-    SMALL, QKV, FC1, TOK, COT, OUT, FC2 = range(7)
+    SMALL, QKV, FC1, TOK, COT, OUT, FC2, FC2B = range(8)
+    part_fc2 = fr // 2
 
     def ctx_pieces(array, to):
         if array == SMALL:
@@ -416,45 +426,97 @@
         for j in range(nc):
             ctx_arrive(array, j)
 
-    blocks = {SMALL: small_all, QKV: w_qkv, FC1: w_fc1, FC2: w_fc2}
-
-    def z_copy(array, j, own):
-        block = blocks[array].at[own]
-        src = fc2_ref if array == FC2 else block
-        return remote(src, block, z_send.at[array, j], z_recv.at[array, j], (z_to(j), c))
-
-    def sib_copy(array, j, at):
-        block = blocks[array].at[at]
-        src = fc2_ref if array == FC2 and j == 0 else block
-        return remote(src, block, sib_send.at[array, j], sib_recv.at[array, j], (other, c))
-
-    def z_start(array):
-        for j in range(1, nz):
-            z_copy(array, j, d).start()
-        sib_copy(array, 0, d).start()
-
-    def z_pass_on(array):
-        for j in range(1, nz):
-            z_copy(array, j, z_from(j)).wait_recv()
-            sib_copy(array, j, z_from(j)).start()
+    def block_of(array, at):
+        if array in (FC2, FC2B):
+            return w_fc2.at[at, pl.ds(0 if array == FC2 else part_fc2, part_fc2), :]
+        return {SMALL: small_all, QKV: w_qkv, FC1: w_fc1}[array].at[at]
+
+    near_low, near_high = z == 1, z == nz - 2
+
+    def z_copy(array, n, delta, owner):
+        block = block_of(array, owner)
+        src = block
+        if array in (FC2, FC2B) and n < PASSED:
+            src = fc2_ref.at[pl.ds(0 if array == FC2 else part_fc2, part_fc2), :]
+        return remote(src, block, z_send.at[array, n], z_recv.at[array, n], (plane(delta), c))
+
+    def z_got(array, n, owner):
+        block = block_of(array, owner)
+        return remote(block, block, z_send.at[array, n], z_recv.at[array, n], (d, c))
+
+    def sib_copy(array, at):
+        block = block_of(array, 2 * at + k)
+        return remote(block, block, sib_send.at[array, at], sib_recv.at[array, at], (other, c))
+
+    def z_own(array):
+        for n, delta in enumerate(DELTAS):
+            @pl.when(exists(delta))
+            def _():
+                z_copy(array, n, delta, d).start()
+        if array not in (FC2, FC2B):
+            sib_copy(array, z).start()
+
+    def z_forward(array):
+        @pl.when(near_high)
+        def _():
+            z_got(array, DELTAS.index(2), k).wait_recv()
+            z_copy(array, PASSED, 1, k).start()
+
+        @pl.when(near_low)
+        def _():
+            z_got(array, DELTAS.index(-2), d + 4).wait_recv()
+            z_copy(array, PASSED, -1, d + 4).start()
+
+    def z_arrive(array):
+        for n, delta in enumerate(DELTAS):
+            done = near_high if delta == 2 else near_low if delta == -2 else None
+            wanted = exists(-delta) if done is None else exists(-delta) & jnp.logical_not(done)
+
+            @pl.when(wanted)
+            def _():
+                z_got(array, n, plane(-delta)).wait_recv()
+
+        @pl.when(z == 0)
+        def _():
+            z_got(array, PASSED, 2 * (nz - 1) + k).wait_recv()
+
+        @pl.when(z == nz - 1)
+        def _():
+            z_got(array, PASSED, k).wait_recv()
+
+        for at in range(nz):
+            if array in (FC2, FC2B):
+                sib_copy(array, at).start()
+            else:
+                @pl.when(z != at)
+                def _():
+                    sib_copy(array, at).start()
 
     def z_finish(array):
-        for j in range(nz):
-            sib_copy(array, j, lax.rem(z + nz - j, nz) * 2 + 1 - k).wait_recv()
+        for at in range(nz):
+            block = block_of(array, 2 * at + 1 - k)
+            remote(block, block, sib_send.at[array, at], sib_recv.at[array, at], (other, c)).wait_recv()
 
     def z_sent(array):
-        for j in range(1, nz):
-            z_copy(array, j, d).wait_send()
-        for j in range(nz):
-            sib_copy(array, j, d if j == 0 else z_from(j)).wait_send()
+        for n, delta in enumerate(DELTAS):
+            @pl.when(exists(delta))
+            def _():
+                z_copy(array, n, delta, d).wait_send()
+
+        @pl.when(near_high | near_low)
+        def _():
+            z_copy(array, PASSED, 1, k).wait_send()
+
+        for at in range(nz):
+            sib_copy(array, at).wait_send()
 
     def out_copy(j, to, sub):
         return remote(out_ref, w_out.at[k, rows(sub), :], ctx_send.at[OUT, j], ctx_recv.at[OUT, j], (d, to))
 
     half = w_out.at[k]
 
-    def out_z(j, to):
-        return remote(half, half, z_send.at[OUT, j], z_recv.at[OUT, j], (to, c))
+    def out_z(n, delta):
+        return remote(half, half, z_send.at[OUT, n], z_recv.at[OUT, n], (plane(delta), c))
 
     def out_sib(which):
         piece = w_out.at[which]
@@ -462,6 +524,7 @@
 
     ctx_start(SMALL)
     ctx_start(QKV)
+    z_own(FC2)
     own_out = pltpu.make_async_copy(out_ref, w_out.at[k, rows(c), :], loc.at[OUT])
 
     @pl.when(z == c)
@@ -473,28 +536,34 @@
         def _():
             out_copy(j, z, c).start()
 
+    ctx_start(FC1)
     ctx_start(TOK)
-    ctx_start(FC1)
     copy_fc2 = pltpu.make_async_copy(fc2_ref, w_fc2.at[d], loc.at[FC2])
     copy_fc2.start()
 
     ctx_finish(SMALL)
-    z_start(SMALL)
+    z_own(SMALL)
     ctx_finish(QKV)
-    z_start(QKV)
+    z_own(QKV)
 
     @pl.when(z == c)
     def _():
         for j in range(1, nc):
             out_copy(j, z, ctx_from(j)).wait_recv()
         own_out.wait()
-        for j in range(1, nz):
-            out_z(j, z_to(j)).start()
+        for n, delta in enumerate(DELTAS):
+            @pl.when(exists(delta))
+            def _():
+                out_z(n, delta).start()
         out_sib(k).start()
 
+    ctx_finish(FC1)
     ctx_start(COT)
-    ctx_finish(FC1)
-    z_pass_on(SMALL)
+    z_forward(SMALL)
+    z_arrive(SMALL)
+    z_forward(FC2)
+    z_forward(QKV)
+    z_own(FC1)
     z_finish(SMALL)
 
     def collect(p, carry):
@@ -522,9 +591,10 @@
     for g in range(nd):
         b_fc1[:, pl.ds(g * fr, fr)] = small_all[g, c][:, :fr]
 
-    z_pass_on(QKV)
-    z_start(FC1)
+    z_arrive(QKV)
     z_finish(QKV)
+
+    seg_col[...] = jnp.broadcast_to(seg_ref[...].astype(f32), (128, length)).T
 
     chunk = 32
 
@@ -562,8 +632,49 @@
         normalise_block(ctx_from(j))
         qkv_block(ctx_from(j))
 
-    z_pass_on(FC1)
-    z_start(FC2)
+    z_forward(FC1)
+    z_own(FC2B)
+
+    tile = 256
+    reach = 512 // tile
+    scale = float(head_dim) ** (-0.5)
+
+    def spans(i):
+        first = max(0, i - reach) * tile
+        count = (i + 1) * tile - first
+        return pl.ds(i * tile, tile), pl.ds(first, count), count
+
+    def mask(i):
+        at, to, count = spans(i)
+        same = seg_col[at, :1] == seg_ref[:1, to].astype(f32)
+        row = lax.broadcasted_iota(jnp.int32, (tile, count), 0) + (tile * i - to.start)
+        col = lax.broadcasted_iota(jnp.int32, (tile, count), 1)
+        bias_s[:, :count] = jnp.where(same & (col <= row), 0.0, -1e30)
+
+    def only_head(h):
+        lane = lax.broadcasted_iota(jnp.int32, (1, dl), 1)
+        return jnp.where((lane >= h * head_dim) & (lane < (h + 1) * head_dim), 1.0, 0.0)
+
+    for i in range(length // tile):
+        at, to, count = spans(i)
+        mask(i)
+        acc_a[...] = jnp.zeros_like(acc_a)
+
+        def forward_step(h, carry):
+            only = only_head(h)
+            s = dot(q_s[at, :] * only.astype(b16), k_s[to, :], RIGHT_T) * scale + bias_s[:, :count]
+            top = jnp.max(s, axis=-1, keepdims=True)
+            e = jnp.exp(s - top)
+            sum_e = jnp.sum(e, axis=-1, keepdims=True)
+            log_s[h, at, :] = top + jnp.log(sum_e)
+            p_low = (e * (1.0 / sum_e)).astype(b16)
+            acc_a[...] += dot(p_low, v_s[to, :], NORMAL) * only
+            return carry
+
+        lax.fori_loop(0, heads, forward_step, 0, unroll=True)
+        attended[at, :] = acc_a[...].astype(b16)
+
+    z_arrive(FC1)
     z_finish(FC1)
 
     def hidden_block(b, carry):
@@ -583,12 +694,14 @@
 
     lax.fori_loop(0, nc, hidden_block, 0)
 
+    z_forward(FC2B)
     ctx_finish(COT)
 
     gives = {QKV: give_qkv, FC1: give_fc1, FC2: give_fc2, OUT: give_out}
     gots = {QKV: got_qkv, FC1: got_fc1, FC2: got_fc2, OUT: got_out}
     owns = {QKV: own_qkv, FC1: own_fc1, FC2: own_fc2, OUT: own_out_g}
     fars = {QKV: far_qkv, FC1: far_fc1, FC2: far_fc2, OUT: far_out}
+    passes = {QKV: pass_qkv, FC1: pass_fc1, FC2: pass_fc2, OUT: pass_out}
 
     def cotangents():
         return cot_all[...].reshape(length, width)
@@ -612,35 +725,75 @@
             gives[array], gots[array], back_sib_send.at[array], back_sib_recv.at[array], (other, c)
         )
 
-    def z_other(j):
-        return lax.rem(z + j, nz)
-
-    def to_owner(array, j):
-        block = gives[array].at[0 if array == OUT else z_other(j)]
+    def to_owner(array, n, delta):
+        block = gives[array].at[0 if array == OUT else jnp.clip(z + delta, 0, nz - 1)]
         return remote(
-            block, fars[array].at[j - 1], back_z_send.at[array, j], back_z_recv.at[array, j], (z_to(j), c)
-        )
+            block, fars[array].at[SLOTS[n]], back_z_send.at[array, n], back_z_recv.at[array, n], (plane(delta), c)
+        )
+
+    def to_pass(array, delta):
+        block = gives[array].at[0 if array == OUT else jnp.clip(z + 3 * delta, 0, nz - 1)]
+        return remote(
+            block, passes[array], back_z_send.at[array, PASSED], back_z_recv.at[array, PASSED], (plane(delta), c)
+        )
+
+    def wanted(array, at):
+        return (at == c) if array == OUT else True
+
+    def mix(array, at):
+        i = 0 if array == OUT else at
+        gives[array][i] = (owns[array][i] + gots[array][i].astype(f32)).astype(b16)
 
     def add_sibling(array):
         to_sibling(array).wait()
-        give, got, own = gives[array], gots[array], owns[array]
-        for j in range(1, nz):
-            if array == OUT:
-                @pl.when(z_other(j) == c)
-                def _():
-                    give[0] = (own[0] + got[0].astype(f32)).astype(b16)
-                    to_owner(OUT, j).start()
-            else:
-                at = z_other(j)
-                give[at] = (own[at] + got[at].astype(f32)).astype(b16)
-                to_owner(array, j).start()
-
-    def total(array):
+        for delta in (-1, 1):
+            far = z + 3 * delta
+
+            @pl.when((z == (nz - 1 if delta < 0 else 0)) & wanted(array, far))
+            def _():
+                mix(array, far)
+                to_pass(array, delta).start()
+        for n, delta in enumerate(DELTAS):
+            hold = {-2: near_high, 2: near_low}.get(delta)
+            go = exists(delta) & wanted(array, z + delta)
+            if hold is not None:
+                go = go & jnp.logical_not(hold)
+
+            @pl.when(go)
+            def _():
+                mix(array, z + delta)
+                to_owner(array, n, delta).start()
+
+    def pass_back(array):
+        for near, delta in ((near_high, -2), (near_low, 2)):
+            @pl.when(near & wanted(array, z + delta))
+            def _():
+                to_pass(array, delta).wait_recv()
+                i = 0 if array == OUT else z + delta
+                gives[array][i] = (
+                    owns[array][i] + gots[array][i].astype(f32) + passes[array][...].astype(f32)
+                ).astype(b16)
+                to_owner(array, DELTAS.index(delta), delta).start()
+
+    def gather_total(array):
         at = 0 if array == OUT else z
-        x = owns[array][at] + gots[array][at].astype(f32)
-        for j in range(1, nz):
-            x = x + fars[array][j - 1].astype(f32)
-        return x
+        own = owns[array]
+        own[at] = own[at] + gots[array][at].astype(f32)
+        for n, delta in enumerate(DELTAS):
+            @pl.when(exists(-delta))
+            def _():
+                to_owner(array, n, delta).wait_recv()
+                own[at] = own[at] + fars[array][SLOTS[n]].astype(f32)
+
+    def owner_sent(array):
+        for n, delta in enumerate(DELTAS):
+            @pl.when(exists(delta) & wanted(array, z + delta))
+            def _():
+                to_owner(array, n, delta).wait_send()
+        for delta in (-1, 1):
+            @pl.when((z == (nz - 1 if delta < 0 else 0)) & wanted(array, z + 3 * delta))
+            def _():
+                to_pass(array, delta).wait_send()
 
     PART, NORM, SUMS = TOK, COT, SMALL
 
@@ -649,10 +802,20 @@
 
     weight_gradient(FC2, act, cotangents)
 
-    for j in range(1, nz):
-        @pl.when(lax.rem(z + nz - j, nz) == c)
+    for n, delta in enumerate(DELTAS):
+        @pl.when(z - delta == c)
         def _():
-            out_z(j, z_to(j)).wait_recv()
+            out_z(n, delta).wait_recv()
+            out_sib(k).start()
+
+    for at, near, delta in ((0, near_high, 1), (nz - 1, near_low, -1)):
+        @pl.when((c == at) & near)
+        def _():
+            out_z(PASSED, delta).start()
+
+        @pl.when((c == at) & (z == nz - 1 - at))
+        def _():
+            out_z(PASSED, delta).wait_recv()
             out_sib(k).start()
     out_sib(1 - k).wait_recv()
 
@@ -663,48 +826,48 @@
         return carry
 
     lax.fori_loop(0, nc, g_att_block, 0)
+    copy_fc2.wait()
+    z_arrive(FC2)
+    z_arrive(FC2B)
     add_sibling(FC2)
-
-    tile = 256
-    reach = 512 // tile
-    scale = float(head_dim) ** (-0.5)
+    z_finish(FC2)
+    z_finish(FC2B)
+
+    def result_term(b):
+        at = block_rows(b)
+        return dot(attended[at, :], w_out[...].reshape(dl, width), NORMAL) + dot(
+            act[at, :], w_fc2[...].reshape(fl, width), NORMAL
+        )
+
+    for j in range(1, nc):
+        b = ctx_to(j)
+        tok_all[b] = result_term(b).astype(b16)
+        over_ctx(PART, tok_all.at[b], part_got.at[j - 1], j, b).start()
+    part_own[...] = result_term(c)
+
     acc_k[...] = jnp.zeros_like(acc_k)
     acc_v[...] = jnp.zeros_like(acc_v)
+    wide = (1, dl // keep_ref.shape[1])
     for i in range(length // tile):
-        first = max(0, i - reach) * tile
-        count = (i + 1) * tile - first
-        at = pl.ds(i * tile, tile)
-        to = pl.ds(first, count)
-        same = seg_col_ref[at, :1] == seg_row_ref[:1, to]
-        row = lax.broadcasted_iota(jnp.int32, (tile, count), 0) + (i * tile - first)
-        col = lax.broadcasted_iota(jnp.int32, (tile, count), 1)
-        bias_s[:, :count] = jnp.where(same & (col <= row), 0.0, -1e30)
+        at, to, count = spans(i)
+        mask(i)
         acc_q[...] = jnp.zeros_like(acc_q)
-        acc_a[...] = jnp.zeros_like(acc_a)
-
-        def head_step(h, carry):
-            lane = lax.broadcasted_iota(jnp.int32, (1, dl), 1)
-            mine = (lane >= h * head_dim) & (lane < (h + 1) * head_dim)
-            only = jnp.where(mine, 1.0, 0.0)
+
+        def backward_step(h, carry):
+            only = only_head(h)
             only_low = only.astype(b16)
             qh = q_s[at, :] * only_low
             gh = g_att[at, :] * only_low
             keys, values = k_s[to, :], v_s[to, :]
-            s = dot(qh, keys, RIGHT_T) * scale + bias_s[:, :count]
-            e = jnp.exp(s - jnp.max(s, axis=-1, keepdims=True))
-            p = e * (1.0 / jnp.sum(e, axis=-1, keepdims=True))
-            p_low = p.astype(b16)
-            acc_a[...] += dot(p_low, values, NORMAL) * only
+            p = jnp.exp(dot(qh, keys, RIGHT_T) * scale + bias_s[:, :count] - log_s[h, at, :])
             gw = dot(gh, values, RIGHT_T)
             gs = (p * (gw - jnp.sum(gw * p, axis=-1, keepdims=True))).astype(b16)
             acc_q[...] += dot(gs, keys, NORMAL) * only
             acc_k[to, :] += dot(gs, qh, LEFT_T)
-            acc_v[to, :] += dot(p_low, gh, LEFT_T)
+            acc_v[to, :] += dot(p.astype(b16), gh, LEFT_T)
             return carry
 
-        lax.fori_loop(0, heads, head_step, 0)
-        attended[at, :] = acc_a[...].astype(b16)
-        wide = (1, dl // keep_ref.shape[1])
+        lax.fori_loop(0, heads, backward_step, 0, unroll=True)
         gmixed[at, pl.ds(0, dl)] = turn(
             acc_q[...] * scale,
             jnp.tile(keep_ref[at, :], wide),
@@ -714,7 +877,6 @@
 
     def finish_block(b, carry):
         at = block_rows(b)
-        wide = (1, dl // keep_ref.shape[1])
         gmixed[at, pl.ds(dl, dl)] = turn(
             acc_k[at, :] * scale,
             jnp.tile(keep_ref[at, :], wide),
@@ -726,12 +888,11 @@
 
     lax.fori_loop(0, nc, finish_block, 0)
 
+    pass_back(FC2)
     weight_gradient(QKV, normed, lambda: gmixed[...])
     weight_gradient(OUT, attended, cotangents)
-
-    copy_fc2.wait()
-    z_pass_on(FC2)
-    z_finish(FC2)
+    add_sibling(QKV)
+    add_sibling(OUT)
 
     def hidden_gradient(b, carry):
         at = block_rows(b)
@@ -742,22 +903,6 @@
         return carry
 
     lax.fori_loop(0, nc, hidden_gradient, 0)
-    add_sibling(QKV)
-    add_sibling(OUT)
-    weight_gradient(FC1, normed, lambda: g_hidden[...])
-
-    def result_term(b):
-        at = block_rows(b)
-        return dot(attended[at, :], w_out[...].reshape(dl, width), NORMAL) + dot(
-            act[at, :], w_fc2[...].reshape(fl, width), NORMAL
-        )
-
-    for j in range(1, nc):
-        b = ctx_to(j)
-        tok_all[b] = result_term(b).astype(b16)
-        over_ctx(PART, tok_all.at[b], part_got.at[j - 1], j, b).start()
-    part_own[...] = result_term(c)
-    add_sibling(FC1)
 
     def normed_term(b):
         at = block_rows(b)
@@ -777,6 +922,8 @@
     at_sum = 3 * dl + fl
     sums[0, :, pl.ds(at_sum, width)] = dot(ones[:, :part], cot_all[c], NORMAL)[:1]
 
+    weight_gradient(FC1, normed, lambda: g_hidden[...])
+    add_sibling(FC1)
     for j in range(1, nc):
         over_ctx(PART, tok_all.at[c], part_got.at[j - 1], j, c).wait_recv()
 
@@ -790,6 +937,47 @@
 
     lax.fori_loop(0, part // chunk, result_step, 0)
 
+    pass_back(QKV)
+    pass_back(OUT)
+    gather_total(FC2)
+    o_fc2[...] = own_fc2[z]
+
+    swaps = {QKV: (swap_qkv, swapped_qkv), FC1: (swap_fc1, swapped_fc1)}
+
+    def place(array, source, x):
+        if array == QKV:
+            for t in range(3):
+                o_qkv[:, lanes(t * nc + source, dl)] = x[:, t * dl : (t + 1) * dl]
+        else:
+            for g in range(nd):
+                o_fc1[:, lanes(g * nc + source, fr)] = x[:, g * fr : (g + 1) * fr]
+
+    def swap_start(array):
+        gather_total(array)
+        src, dst = swaps[array]
+        own = owns[array]
+        for j in range(1, nc):
+            src[j - 1] = own[z, rows(ctx_to(j)), :].astype(b16)
+            over_ctx(array, src.at[j - 1], dst.at[j - 1], j, ctx_to(j)).start()
+        place(array, c, own[z, rows(c), :])
+
+    def swap_finish(array):
+        src, dst = swaps[array]
+        for j in range(1, nc):
+            over_ctx(array, src.at[j - 1], dst.at[j - 1], j, ctx_to(j)).wait_recv()
+            place(array, ctx_from(j), dst[j - 1].astype(f32))
+
+    swap_start(QKV)
+
+    @pl.when(z == c)
+    def _():
+        gather_total(OUT)
+        for j in range(1, nc):
+            swap_out[j - 1] = own_out_g[0, rows(ctx_to(j)), :].astype(b16)
+            over_ctx(OUT, swap_out.at[j - 1], swapped_out.at[0], j, ctx_to(j)).start()
+        o_out[...] = own_out_g[0, rows(c), :]
+
+    pass_back(FC1)
     for j in range(1, nc):
         over_ctx(NORM, cot_all.at[c], norm_got.at[j - 1], j, c).wait_recv()
 
@@ -822,68 +1010,17 @@
     sum_sib.start()
     sum_sib.wait()
     sums[1] = sums[0] + sums_sib[0]
-
-    def sum_z(j):
-        return remote(
-            sums.at[1], sums_z.at[j - 1], back_z_send.at[SUMS, j], back_z_recv.at[SUMS, j], (z_to(j), c)
-        )
-
-    for j in range(1, nz):
-        sum_z(j).start()
-
-    def from_owner(array):
-        for j in range(1, nz):
-            to_owner(array, j).wait_recv()
-
-    from_owner(FC2)
-    o_fc2[...] = total(FC2)
-
-    swaps = {QKV: (swap_qkv, swapped_qkv), FC1: (swap_fc1, swapped_fc1)}
-
-    def place(array, source, x):
-        if array == QKV:
-            for t in range(3):
-                o_qkv[:, lanes(t * nc + source, dl)] = x[:, t * dl : (t + 1) * dl]
-        else:
-            for g in range(nd):
-                o_fc1[:, lanes(g * nc + source, fr)] = x[:, g * fr : (g + 1) * fr]
-
-    def swap_start(array):
-        from_owner(array)
-        src, dst = swaps[array]
-        own = owns[array]
-        own[z] = total(array)
-        for j in range(1, nc):
-            src[j - 1] = own[z, rows(ctx_to(j)), :].astype(b16)
-            over_ctx(array, src.at[j - 1], dst.at[j - 1], j, ctx_to(j)).start()
-        place(array, c, own[z, rows(c), :])
-
-    def swap_finish(array):
-        src, dst = swaps[array]
-        for j in range(1, nc):
-            over_ctx(array, src.at[j - 1], dst.at[j - 1], j, ctx_to(j)).wait_recv()
-            place(array, ctx_from(j), dst[j - 1].astype(f32))
-
-    swap_start(QKV)
-
-    @pl.when(z == c)
-    def _():
-        from_owner(OUT)
-        own_out_g[0] = total(OUT)
-        for j in range(1, nc):
-            swap_out[j - 1] = own_out_g[0, rows(ctx_to(j)), :].astype(b16)
-            over_ctx(OUT, swap_out.at[j - 1], swapped_out.at[0], j, ctx_to(j)).start()
-        o_out[...] = own_out_g[0, rows(c), :]
-
-    for j in range(1, nz):
-        sum_z(j).wait()
-    mine_sum = sums[1]
-    for j in range(1, nz):
-        mine_sum = mine_sum + sums_z[j - 1]
-    sums_mine[0] = mine_sum
-    o_sums[c] = mine_sum
+    for n, partner in enumerate((z + 1 - 2 * lax.rem(z, 2), lax.rem(z + 2, nz))):
+        trade = remote(
+            sums.at[n + 1], sums_z.at[n], back_z_send.at[SUMS, n], back_z_recv.at[SUMS, n], (2 * partner + k, c)
+        )
+        trade.start()
+        trade.wait()
+        sums[n + 2] = sums[n + 1] + sums_z[n]
+    sums_mine = sums.at[3]
+    o_sums[c] = sums[3]
     for j in range(1, nc):
-        over_ctx(SUMS, sums_mine.at[0], o_sums.at[c], j, ctx_to(j)).start()
+        over_ctx(SUMS, sums_mine, o_sums.at[c], j, ctx_to(j)).start()
 
     swap_finish(QKV)
     for j in range(1, nc):
@@ -891,13 +1028,13 @@
         def _():
             over_ctx(OUT, swap_out.at[0], swapped_out.at[0], j, ctx_to(j)).wait_recv()
             o_out[...] = swapped_out[0].astype(f32)
+
+    swap_start(FC1)
     for j in range(1, nc):
-        over_ctx(SUMS, sums_mine.at[0], o_sums.at[ctx_from(j)], j, ctx_to(j)).wait_recv()
-
-    swap_start(FC1)
+        over_ctx(SUMS, sums_mine, o_sums.at[ctx_from(j)], j, ctx_to(j)).wait_recv()
     swap_finish(FC1)
 
-    for array in (SMALL, QKV, FC1, FC2):
+    for array in (SMALL, QKV, FC1, FC2, FC2B):
         z_sent(array)
     for array in (SMALL, QKV, FC1, TOK, COT):
         ctx_sent(array)
@@ -908,21 +1045,22 @@
 
     @pl.when(z == c)
     def _():
-        for j in range(1, nz):
-            out_z(j, z_to(j)).wait_send()
+        for n, delta in enumerate(DELTAS):
+            @pl.when(exists(delta))
+            def _():
+                out_z(n, delta).wait_send()
+
+    @pl.when(((c == 0) & near_high) | ((c == nz - 1) & near_low))
+    def _():
+        out_z(PASSED, 1).wait_send()
 
     out_sib(k).wait_send()
-    for array in (QKV, FC1, FC2):
-        for j in range(1, nz):
-            to_owner(array, j).wait_send()
-    for j in range(1, nz):
-        @pl.when(z_other(j) == c)
-        def _():
-            to_owner(OUT, j).wait_send()
+    for array in (QKV, OUT, FC1, FC2):
+        owner_sent(array)
     for j in range(1, nc):
         over_ctx(PART, tok_all.at[c], part_got.at[j - 1], j, c).wait_send()
         over_ctx(NORM, cot_all.at[c], norm_got.at[j - 1], j, c).wait_send()
-        over_ctx(SUMS, sums_mine.at[0], o_sums.at[c], j, ctx_to(j)).wait_send()
+        over_ctx(SUMS, sums_mine, o_sums.at[c], j, ctx_to(j)).wait_send()
         for array in (QKV, FC1):
             over_ctx(array, swaps[array][0].at[j - 1], swaps[array][1].at[j - 1], j, c).wait_send()
 
@@ -940,8 +1078,6 @@
     cw = nc * wr
     f32, b16 = jnp.float32, jnp.bfloat16
     tables = [jnp.asarray(t) for t in turn_tables(length, width // HEADS, 128)]
-    seg_row = jnp.broadcast_to(segments.reshape(1, length), (8, length))
-    seg_col = jnp.broadcast_to(segments.reshape(length, 1), (length, 128))
     pack = small.shape[1]
     total = 3 * dl + fl + 3 * width
     tile, window = 256, 768
@@ -983,28 +1119,79 @@
         ((length, fl), b16),
     ]
     grads = [(nz, cw, 3 * dl), (nz, cw, fl), (nz, fr, width), (1, cw, width)]
-    fars = [(nz - 1,) + g[1:] for g in grads]
+    fars = [(3,) + g[1:] for g in grads]
     work += [(g, b16) for g in grads] + [(g, b16) for g in grads] + [(g, f32) for g in grads]
-    work += [(g, b16) for g in fars]
+    work += [(g, b16) for g in fars] + [(g[1:], b16) for g in grads]
+    work += [((HEADS // nc, length, 1), f32), ((length, 128), f32)]
     work += [((nc - 1, part, width), b16), ((part, width), f32)] * 2
     work += [((nc - 1, wr, n), b16) for n in (3 * dl, fl, width)]
     work += [((nc - 1, wr, n), b16) for n in (3 * dl, fl)] + [((1, wr, width), b16)]
-    work += [((n, 1, total), f32) for n in (2, 1, nz - 1, 1)]
+    work += [((n, 1, total), f32) for n in (4, 1, 2)]
     dma = pltpu.SemaphoreType.DMA
-    sems = [(7, nc), (7, nc), (7, nz), (7, nz), (7, nz), (7, nz), (7,)]
-    sems += [(7, nz), (7, nz), (7,), (7,), (7, nc), (7, nc)]
+    sems = [(7, nc), (7, nc), (8, 5), (8, 5), (8, nz), (8, nz), (7,)]
+    sems += [(7, 5), (7, 5), (7,), (7,), (7, nc), (7, nc)]
     hbm, vmem = pl.BlockSpec(memory_space=pl.ANY), pl.BlockSpec(memory_space=pltpu.VMEM)
     return pl.pallas_call(
         functools.partial(layer_kernel, nz, nc, marks),
         out_shape=[jax.ShapeDtypeStruct(s, t) for s, t in results],
-        in_specs=[hbm] * 7 + [vmem] * 5,
+        in_specs=[hbm] * 7 + [vmem] * 4,
         out_specs=[vmem] * len(results),
         scratch_shapes=[pltpu.VMEM(s, t) for s, t in work] + [dma(s) for s in sems],
         compiler_params=pltpu.CompilerParams(
             collective_id=0, has_side_effects=True, vmem_limit_bytes=62 * 2**20
         ),
         name="layer",
-    )(tokens, cotangent, qkv_weight, fc1_weight, fc2_weight, out_weight, small, seg_row, seg_col, *tables)
+    )(tokens, cotangent, qkv_weight, fc1_weight, fc2_weight, out_weight, small, segments.reshape(1, length), *tables)
+
+
+def finish_kernel(
+    dl, fr, wr,
+    result, tokens, qkv, out, fc1, fc2, sums,
+    o_result, o_tokens, o_qkv, o_out, o_fc1, o_fc2, o_qkv_b, o_out_b, o_fc1_b, o_fc2_b, o_gain, o_shift,
+    row,
+):
+    moves = [(result, o_result), (tokens, o_tokens), (qkv, o_qkv), (out, o_out), (fc1, o_fc1), (fc2, o_fc2)]
+    for source, to in moves:
+        to[...] = source[...]
+    nc, total = sums.shape[0], sums.shape[2]
+    mine, group = lax.axis_index("ctx"), lax.axis_index("dp")
+    place = group * nc + mine
+    width = dl * nc
+    fl = total - 3 * dl - 3 * width
+
+    def piece(values, size):
+        length = values.shape[1]
+        return pltpu.roll(values, length - place * size, axis=1)[0, :size]
+
+    for t in range(3):
+        for rank in range(nc):
+            row[:, pl.ds(t * width + rank * dl, dl)] = sums[rank][:, t * dl : (t + 1) * dl]
+    o_qkv_b[...] = piece(row[...], 3 * wr)
+    at = pl.ds(pl.multiple_of(3 * dl + group * fr, fr), fr)
+    o_fc1_b[...] = sums[mine, :, at][0]
+    for n, outs in enumerate(((o_out_b, o_fc2_b), (o_gain,), (o_shift,))):
+        first = 3 * dl + fl + n * width
+        whole = sums[0][:, first : first + width]
+        for rank in range(1, nc):
+            whole = whole + sums[rank][:, first : first + width]
+        for to in outs:
+            to[...] = piece(whole, wr)
+
+
+def finish_all(dl, fr, wr, arrays):
+    f32 = jnp.float32
+    vmem = pl.BlockSpec(memory_space=pltpu.VMEM)
+    vectors = [3 * wr, wr, fr, wr, wr, wr]
+    nc = arrays[6].shape[0]
+    return pl.pallas_call(
+        functools.partial(finish_kernel, dl, fr, wr),
+        out_shape=[jax.ShapeDtypeStruct(a.shape, a.dtype) for a in arrays[:6]]
+        + [jax.ShapeDtypeStruct((n,), f32) for n in vectors],
+        in_specs=[vmem] * 7,
+        out_specs=[vmem] * 12,
+        scratch_shapes=[pltpu.VMEM((1, 3 * dl * nc), f32)],
+        name="finish",
+    )(*arrays)
 
 
 def local_direct(
@@ -1033,7 +1220,7 @@
         marks.append(marks[-1] + piece.shape[0])
     vector = jnp.concatenate(pieces).astype(jnp.float32)
     vector = jnp.pad(vector, (0, -marks[-1] % 128))[None]
-    result, grad_tokens, grad_qkv, grad_out, grad_fc1, grad_fc2, sums = layer_all(
+    arrays = layer_all(
         dp // 2,
         ctx,
         tuple(marks),
@@ -1046,27 +1233,21 @@
         out_weight,
         vector,
     )
-    sums = sums[:, 0]
-    mine, group = lax.axis_index("ctx"), lax.axis_index("dp")
-    place = group * ctx + mine
-    whole_qkv = jnp.moveaxis(sums[:, : 3 * dl].reshape(ctx, 3, dl), 0, 1).reshape(3 * width)
-    g_qkv_b = lax.dynamic_slice_in_dim(whole_qkv, place * 3 * wr, 3 * wr)
-    g_fc1_b = lax.dynamic_slice(sums, (mine, 3 * dl + group * fr), (1, fr))[0]
-    wide = jnp.sum(sums[:, 3 * dl + fl :], axis=0).reshape(3, width)
-    wide = lax.dynamic_slice(wide, (0, place * wr), (3, wr))
+    result, grad_tokens, *rest = finish_all(dl, fr, wr, arrays)
+    grad_qkv, grad_out, grad_fc1, grad_fc2, g_qkv_b, g_out_b, g_fc1_b, g_fc2_b, g_gain, g_shift = rest
     return (
         result[None],
         grad_tokens[None],
         grad_qkv,
         g_qkv_b,
         grad_out,
-        wide[0],
+        g_out_b,
         grad_fc1,
         g_fc1_b,
         grad_fc2,
-        wide[0],
-        wide[1],
-        wide[2],
+        g_fc2_b,
+        g_gain,
+        g_shift,
     )
 
 
@@ -1078,7 +1259,8 @@
         dp, ctx = sizes
         tokens, qkv_weight, fc2_weight = args[0], args[2], args[8]
         direct = (
-            dp == 2 * ctx
+            dp == 8
+            and ctx == 4
             and tokens.shape[0] == 1
             and tokens.shape[1] % 256 == 0
             and qkv_weight.shape[0] % 32 == 0

time: 217 us -> 159 us (0.73)
  Pallas kernels: 201 us -> 157 us
  local copies, waits for them, and re-layouts: 13.6 us -> 1.35 us
    pallas_call x1, Pallas kernels: 201 us -> 154 us  [layer_all(): pl.pallas_call(functools.partial(layer_kernel, nz, nc, marks), out_shape=...]
    unnamed x35 -> x12, local copies, waits for them, and re-layouts: 9.02 us -> 0.69 us
    pallas_call x0 -> x1, Pallas kernels: none -> 3.29 us  [finish_all(): pl.pallas_call(functools.partial(finish_kernel, dl, fr, wr), out_shape=[j...]
where the time goes in v3:
time: 159 us
  Pallas kernels  157 us (99%)
    pallas_call x1, Pallas kernels, layer_all(): pl.pallas_call(functools.partial(layer_kernel, nz, nc, marks), out_shape=...  154 us
    pallas_call x1, Pallas kernels, finish_all(): pl.pallas_call(functools.partial(finish_kernel, dl, fr, wr), out_shape=[j...  3.29 us

profile of v3, /device:TPU:0, one launch (start us, length us, event | category | flops | bytes accessed | tf_op | source)
XLA Modules:
  0.0 159.2 jit_solution(17223555780920902277)
XLA Ops:
  0.6 0.0 copy-start.3
  0.7 0.0 copy-start.4
  0.7 0.0 copy-start.5
  0.7 0.0 copy-start
  0.7 0.0 copy-start.1
  0.7 0.0 copy-start.2
  0.7 0.6 copy-done.3
  1.3 0.0 copy-done.4
  1.3 0.0 copy-done.5
  1.3 0.0 copy-done
  1.3 0.0 copy-done.1
  1.4 0.0 copy-done.2
  1.4 0.1 concatenate.3
  1.5 0.6 reshape.24.small_ref
  2.1 153.6 %layer.1 = (bf16[256,1024]{1,0:T(8,128)(2,1)}, bf16[256,1024]{1,0:T(8,128)(2,1)}, f32[32,3072]{1,0:T(8,128)}, f32[32,1024]{1,0:T(8,128)}, f32[32,4096]{1,0:T(8,1...) custom-call(bf16[256,1024]{1,0:T(8,128)(2,1)} %bitcast.4, bf16[256,1024]{1,0:T(8,128)(2,1)} %bitcast.5, ...), custom_call_target="tpu_custom_call" | custom-call | tf_op jit(solution)/shard_map/layer/pallas_call | solution.py:1134
  155.7 3.3 %finish.1 = (bf16[256,1024]{1,0:T(8,128)(2,1)}, bf16[256,1024]{1,0:T(8,128)(2,1)}, f32[32,3072]{1,0:T(8,128)}, f32[32,1024]{1,0:T(8,128)}, f32[32,4096]{1,0:T(8,...) custom-call(bf16[256,1024]{1,0:T(8,128)(2,1)} %get-tuple-element.31., ...), custom_call_target="tpu_custom_call" | custom-call | tf_op jit(solution)/shard_map/finish/pallas_call | solution.py:1186
  (1 shorter events, 0.0 us)
Async XLA Ops:
  0.6 0.7 copy-start.3
  0.7 0.7 copy-start.4
  0.7 0.7 copy-start.5
  0.7 0.7 copy-start
  0.7 0.7 copy-start.1
  0.7 0.7 copy-start.2

commit v4 on v3

--- a/solution.py
+++ b/solution.py
@@ -311,16 +311,16 @@
 def layer_kernel(
     nz, nc, marks,
     tok_ref, cot_ref, qkv_ref, fc1_ref, fc2_ref, out_ref, small_ref,
-    seg_ref, keep_ref, ahead_ref, behind_ref,
+    seg_ref, keep_hbm, ahead_hbm, behind_hbm,
     o_result, o_tokens, o_qkv, o_out, o_fc1, o_fc2, o_sums,
     tok_all, cot_all, w_qkv, w_fc1, w_fc2, w_out, small_all,
     small_rows, vec_d, b_qkv, b_fc1, normed, q_s, k_s, v_s, attended, g_att, act, slope, gmixed,
     acc_q, acc_k, acc_v, acc_a, bias_s, g_hidden,
     give_qkv, give_fc1, give_fc2, give_out, got_qkv, got_fc1, got_fc2, got_out,
     own_qkv, own_fc1, own_fc2, own_out_g, far_qkv, far_fc1, far_fc2, far_out,
-    pass_qkv, pass_fc1, pass_fc2, pass_out, log_s, seg_col,
+    pass_qkv, pass_fc1, pass_fc2, pass_out, log_s, seg_col, keep_ref, ahead_ref, behind_ref,
     part_got, part_own, norm_got, norm_own,
-    swap_qkv, swap_fc1, swap_out, swapped_qkv, swapped_fc1, swapped_out,
+    swap_qkv, swap_fc1, swapped_qkv, swapped_fc1, out_planes, give_column, own_column, column_got,
     sums, sums_sib, sums_z,
     ctx_send, ctx_recv, z_send, z_recv, sib_send, sib_recv, loc,
     back_z_send, back_z_recv, back_sib_send, back_sib_recv, back_ctx_send, back_ctx_recv,
@@ -374,8 +374,7 @@
     def lanes(at, size):
         return pl.ds(pl.multiple_of(at * size, size), size)
 
-    SMALL, QKV, FC1, TOK, COT, OUT, FC2, FC2B = range(8)
-    part_fc2 = fr // 2
+    SMALL, QKV, FC1, TOK, COT, OUT, FC2 = range(7)
 
     def ctx_pieces(array, to):
         if array == SMALL:
@@ -426,18 +425,62 @@
         for j in range(nc):
             ctx_arrive(array, j)
 
+    side, across, corner = c + 1 - 2 * lax.rem(c, 2), lax.rem(c + 2, nc), nc - 1 - c
+    first_half, second_half = pl.ds(0, part // 2), pl.ds(part // 2, part // 2)
+
+    def pair_copy(array, n):
+        store = tok_all if array == TOK else cot_all
+        src = tok_ref if array == TOK else cot_ref
+        if n == 1:
+            dst, to = store.at[c], side
+        elif n == 2:
+            dst, to = store.at[c], across
+        elif n == 3:
+            src = store.at[side, first_half, :]
+            dst, to = src, across
+        else:
+            src = store.at[across, second_half, :]
+            dst, to = src, side
+        return remote(src, dst, ctx_send.at[array, n], ctx_recv.at[array, n], (d, to))
+
+    def pair_start(array):
+        store, src = (tok_all, tok_ref) if array == TOK else (cot_all, cot_ref)
+        pair_copy(array, 1).start()
+        pair_copy(array, 2).start()
+        pltpu.make_async_copy(src, store.at[c], loc.at[array]).start()
+
+    def pair_got(array, n):
+        store = tok_all if array == TOK else cot_all
+        got = {
+            0: lambda: store.at[corner, second_half, :],
+            1: lambda: store.at[side],
+            2: lambda: store.at[across],
+            3: lambda: store.at[corner, first_half, :],
+        }[n]()
+        remote(got, got, ctx_send.at[array, n], ctx_recv.at[array, n], (d, side)).wait_recv()
+
+    def pair_forward(array):
+        pair_got(array, 1)
+        pair_copy(array, 3).start()
+        pair_got(array, 2)
+        pair_copy(array, 0).start()
+
+    def pair_own(array):
+        store = tok_all if array == TOK else cot_all
+        pltpu.make_async_copy(store.at[c], store.at[c], loc.at[array]).wait()
+
     def block_of(array, at):
-        if array in (FC2, FC2B):
-            return w_fc2.at[at, pl.ds(0 if array == FC2 else part_fc2, part_fc2), :]
-        return {SMALL: small_all, QKV: w_qkv, FC1: w_fc1}[array].at[at]
+        if array == OUT:
+            return out_planes.at[lax.div(at, 2)]
+        return {SMALL: small_all, QKV: w_qkv, FC1: w_fc1, FC2: w_fc2}[array].at[at]
 
     near_low, near_high = z == 1, z == nz - 2
 
     def z_copy(array, n, delta, owner):
         block = block_of(array, owner)
         src = block
-        if array in (FC2, FC2B) and n < PASSED:
-            src = fc2_ref.at[pl.ds(0 if array == FC2 else part_fc2, part_fc2), :]
+        if array in (FC2, OUT) and n < PASSED:
+            src = fc2_ref if array == FC2 else out_ref
         return remote(src, block, z_send.at[array, n], z_recv.at[array, n], (plane(delta), c))
 
     def z_got(array, n, owner):
@@ -453,7 +496,7 @@
             @pl.when(exists(delta))
             def _():
                 z_copy(array, n, delta, d).start()
-        if array not in (FC2, FC2B):
+        if array not in (FC2, OUT):
             sib_copy(array, z).start()
 
     def z_forward(array):
@@ -484,8 +527,10 @@
         def _():
             z_got(array, PASSED, k).wait_recv()
 
+        if array == OUT:
+            return
         for at in range(nz):
-            if array in (FC2, FC2B):
+            if array == FC2:
                 sib_copy(array, at).start()
             else:
                 @pl.when(z != at)
@@ -507,16 +552,16 @@
         def _():
             z_copy(array, PASSED, 1, k).wait_send()
 
-        for at in range(nz):
-            sib_copy(array, at).wait_send()
+        if array != OUT:
+            for at in range(nz):
+                sib_copy(array, at).wait_send()
 
     def out_copy(j, to, sub):
-        return remote(out_ref, w_out.at[k, rows(sub), :], ctx_send.at[OUT, j], ctx_recv.at[OUT, j], (d, to))
-
-    half = w_out.at[k]
-
-    def out_z(n, delta):
-        return remote(half, half, z_send.at[OUT, n], z_recv.at[OUT, n], (plane(delta), c))
+        piece = out_planes.at[to]
+        return remote(piece, w_out.at[k, rows(sub), :], ctx_send.at[OUT, j], ctx_recv.at[OUT, j], (d, to))
+
+    def own_out():
+        return pltpu.make_async_copy(out_planes.at[c], w_out.at[k, rows(c), :], loc.at[OUT])
 
     def out_sib(which):
         piece = w_out.at[which]
@@ -524,20 +569,15 @@
 
     ctx_start(SMALL)
     ctx_start(QKV)
-    z_own(FC2)
-    own_out = pltpu.make_async_copy(out_ref, w_out.at[k, rows(c), :], loc.at[OUT])
-
-    @pl.when(z == c)
-    def _():
-        own_out.start()
-
-    for j in range(1, nc):
-        @pl.when(ctx_to(j) == z)
-        def _():
-            out_copy(j, z, c).start()
-
+    z_own(OUT)
+    tables = [(keep_hbm, keep_ref), (ahead_hbm, ahead_ref), (behind_hbm, behind_ref)]
+    tables = [pltpu.make_async_copy(a, b, loc.at[8 + n]) for n, (a, b) in enumerate(tables)]
+    for copy in tables:
+        copy.start()
+    copy_out = pltpu.make_async_copy(out_ref, out_planes.at[z], loc.at[7])
+    copy_out.start()
     ctx_start(FC1)
-    ctx_start(TOK)
+    pair_start(TOK)
     copy_fc2 = pltpu.make_async_copy(fc2_ref, w_fc2.at[d], loc.at[FC2])
     copy_fc2.start()
 
@@ -545,25 +585,19 @@
     z_own(SMALL)
     ctx_finish(QKV)
     z_own(QKV)
-
-    @pl.when(z == c)
-    def _():
-        for j in range(1, nc):
-            out_copy(j, z, ctx_from(j)).wait_recv()
-        own_out.wait()
-        for n, delta in enumerate(DELTAS):
-            @pl.when(exists(delta))
-            def _():
-                out_z(n, delta).start()
-        out_sib(k).start()
-
+    z_forward(OUT)
+    z_forward(SMALL)
     ctx_finish(FC1)
-    ctx_start(COT)
-    z_forward(SMALL)
+    z_own(FC1)
+    z_arrive(OUT)
+    copy_out.wait()
+    own_out().start()
+    for j in range(1, nc):
+        out_copy(j, ctx_to(j), c).start()
+    pair_start(COT)
     z_arrive(SMALL)
-    z_forward(FC2)
     z_forward(QKV)
-    z_own(FC1)
+    z_own(FC2)
     z_finish(SMALL)
 
     def collect(p, carry):
@@ -627,13 +661,23 @@
                 y = turn(y, keep, ahead, behind)
             to[at, :] = y.astype(b16)
 
-    for j in range(nc):
-        ctx_arrive(TOK, j)
-        normalise_block(ctx_from(j))
-        qkv_block(ctx_from(j))
+    for copy in tables:
+        copy.wait()
+    pair_own(TOK)
+    normalise_block(c)
+    qkv_block(c)
+    pair_forward(TOK)
+    normalise_block(side)
+    qkv_block(side)
+    normalise_block(across)
+    qkv_block(across)
+    pair_got(TOK, 3)
+    pair_got(TOK, 0)
+    normalise_block(corner)
+    qkv_block(corner)
 
     z_forward(FC1)
-    z_own(FC2B)
+    pair_forward(COT)
 
     tile = 256
     reach = 512 // tile
@@ -694,14 +738,17 @@
 
     lax.fori_loop(0, nc, hidden_block, 0)
 
-    z_forward(FC2B)
-    ctx_finish(COT)
-
-    gives = {QKV: give_qkv, FC1: give_fc1, FC2: give_fc2, OUT: give_out}
+    z_forward(FC2)
+    pair_own(COT)
+    pair_got(COT, 3)
+    pair_got(COT, 0)
+
+    COLUMN = 7
+    gives = {QKV: give_qkv, FC1: give_fc1, FC2: give_fc2, OUT: give_out, COLUMN: give_column}
     gots = {QKV: got_qkv, FC1: got_fc1, FC2: got_fc2, OUT: got_out}
-    owns = {QKV: own_qkv, FC1: own_fc1, FC2: own_fc2, OUT: own_out_g}
-    fars = {QKV: far_qkv, FC1: far_fc1, FC2: far_fc2, OUT: far_out}
-    passes = {QKV: pass_qkv, FC1: pass_fc1, FC2: pass_fc2, OUT: pass_out}
+    owns = {QKV: own_qkv, FC1: own_fc1, FC2: own_fc2, OUT: own_out_g, COLUMN: own_column}
+    fars = {QKV: far_qkv, FC1: far_fc1, FC2: far_fc2, COLUMN: far_out}
+    passes = {QKV: pass_qkv, FC1: pass_fc1, FC2: pass_fc2, COLUMN: pass_out}
 
     def cotangents():
         return cot_all[...].reshape(length, width)
@@ -726,97 +773,106 @@
         )
 
     def to_owner(array, n, delta):
-        block = gives[array].at[0 if array == OUT else jnp.clip(z + delta, 0, nz - 1)]
+        block = gives[array].at[jnp.clip(z + delta, 0, nz - 1)]
         return remote(
             block, fars[array].at[SLOTS[n]], back_z_send.at[array, n], back_z_recv.at[array, n], (plane(delta), c)
         )
 
     def to_pass(array, delta):
-        block = gives[array].at[0 if array == OUT else jnp.clip(z + 3 * delta, 0, nz - 1)]
+        block = gives[array].at[jnp.clip(z + 3 * delta, 0, nz - 1)]
         return remote(
             block, passes[array], back_z_send.at[array, PASSED], back_z_recv.at[array, PASSED], (plane(delta), c)
         )
 
-    def wanted(array, at):
-        return (at == c) if array == OUT else True
-
-    def mix(array, at):
-        i = 0 if array == OUT else at
-        gives[array][i] = (owns[array][i] + gots[array][i].astype(f32)).astype(b16)
-
-    def add_sibling(array):
-        to_sibling(array).wait()
+    def both_cores(array, at):
+        if array == COLUMN:
+            return own_column[at]
+        return owns[array][at] + gots[array][at].astype(f32)
+
+    def send_back(array):
         for delta in (-1, 1):
-            far = z + 3 * delta
-
-            @pl.when((z == (nz - 1 if delta < 0 else 0)) & wanted(array, far))
+            far = jnp.clip(z + 3 * delta, 0, nz - 1)
+
+            @pl.when(z == (nz - 1 if delta < 0 else 0))
             def _():
-                mix(array, far)
+                gives[array][far] = both_cores(array, far).astype(b16)
                 to_pass(array, delta).start()
         for n, delta in enumerate(DELTAS):
             hold = {-2: near_high, 2: near_low}.get(delta)
-            go = exists(delta) & wanted(array, z + delta)
-            if hold is not None:
-                go = go & jnp.logical_not(hold)
+            go = exists(delta) if hold is None else exists(delta) & jnp.logical_not(hold)
+            at = jnp.clip(z + delta, 0, nz - 1)
 
             @pl.when(go)
             def _():
-                mix(array, z + delta)
+                gives[array][at] = both_cores(array, at).astype(b16)
                 to_owner(array, n, delta).start()
+
+    def add_sibling(array):
+        to_sibling(array).wait()
+        send_back(array)
 
     def pass_back(array):
         for near, delta in ((near_high, -2), (near_low, 2)):
-            @pl.when(near & wanted(array, z + delta))
+            at = jnp.clip(z + delta, 0, nz - 1)
+
+            @pl.when(near)
             def _():
                 to_pass(array, delta).wait_recv()
-                i = 0 if array == OUT else z + delta
-                gives[array][i] = (
-                    owns[array][i] + gots[array][i].astype(f32) + passes[array][...].astype(f32)
-                ).astype(b16)
+                gives[array][at] = (both_cores(array, at) + passes[array][...].astype(f32)).astype(b16)
                 to_owner(array, DELTAS.index(delta), delta).start()
 
     def gather_total(array):
-        at = 0 if array == OUT else z
         own = owns[array]
-        own[at] = own[at] + gots[array][at].astype(f32)
+        own[z] = both_cores(array, z)
         for n, delta in enumerate(DELTAS):
             @pl.when(exists(-delta))
             def _():
                 to_owner(array, n, delta).wait_recv()
-                own[at] = own[at] + fars[array][SLOTS[n]].astype(f32)
+                own[z] = own[z] + fars[array][SLOTS[n]].astype(f32)
 
     def owner_sent(array):
         for n, delta in enumerate(DELTAS):
-            @pl.when(exists(delta) & wanted(array, z + delta))
+            @pl.when(exists(delta))
             def _():
                 to_owner(array, n, delta).wait_send()
         for delta in (-1, 1):
-            @pl.when((z == (nz - 1 if delta < 0 else 0)) & wanted(array, z + 3 * delta))
+            @pl.when(z == (nz - 1 if delta < 0 else 0))
             def _():
                 to_pass(array, delta).wait_send()
 
+    def column_copy(j, to):
+        return remote(
+            give_out.at[0, rows(to), :], column_got.at[c], back_ctx_send.at[OUT, j], back_ctx_recv.at[OUT, j], (d, to)
+        )
+
+    def to_columns():
+        to_sibling(OUT).wait()
+        own_out_g[0] = own_out_g[0] + got_out[0].astype(f32)
+        give_out[0] = own_out_g[0].astype(b16)
+        for j in range(1, nc):
+            column_copy(j, ctx_to(j)).start()
+        own_column[c] = own_out_g[0, rows(c), :]
+
+    def from_columns():
+        for j in range(1, nc):
+            source = ctx_from(j)
+            got = column_got.at[source]
+            remote(got, got, back_ctx_send.at[OUT, j], back_ctx_recv.at[OUT, j], (d, source)).wait_recv()
+            own_column[source] = column_got[source].astype(f32)
+        send_back(COLUMN)
+
     PART, NORM, SUMS = TOK, COT, SMALL
 
     def over_ctx(array, src, dst, j, to):
         return remote(src, dst, back_ctx_send.at[array, j], back_ctx_recv.at[array, j], (d, to))
 
     weight_gradient(FC2, act, cotangents)
-
-    for n, delta in enumerate(DELTAS):
-        @pl.when(z - delta == c)
-        def _():
-            out_z(n, delta).wait_recv()
-            out_sib(k).start()
-
-    for at, near, delta in ((0, near_high, 1), (nz - 1, near_low, -1)):
-        @pl.when((c == at) & near)
-        def _():
-            out_z(PASSED, delta).start()
-
-        @pl.when((c == at) & (z == nz - 1 - at))
-        def _():
-            out_z(PASSED, delta).wait_recv()
-            out_sib(k).start()
+    weight_gradient(OUT, attended, cotangents)
+
+    own_out().wait()
+    for j in range(1, nc):
+        out_copy(j, ctx_to(j), ctx_from(j)).wait_recv()
+    out_sib(k).start()
     out_sib(1 - k).wait_recv()
 
     w_o = w_out[...].reshape(dl, width)
@@ -826,29 +882,13 @@
         return carry
 
     lax.fori_loop(0, nc, g_att_block, 0)
-    copy_fc2.wait()
-    z_arrive(FC2)
-    z_arrive(FC2B)
     add_sibling(FC2)
-    z_finish(FC2)
-    z_finish(FC2B)
-
-    def result_term(b):
-        at = block_rows(b)
-        return dot(attended[at, :], w_out[...].reshape(dl, width), NORMAL) + dot(
-            act[at, :], w_fc2[...].reshape(fl, width), NORMAL
-        )
-
-    for j in range(1, nc):
-        b = ctx_to(j)
-        tok_all[b] = result_term(b).astype(b16)
-        over_ctx(PART, tok_all.at[b], part_got.at[j - 1], j, b).start()
-    part_own[...] = result_term(c)
+    to_columns()
 
     acc_k[...] = jnp.zeros_like(acc_k)
     acc_v[...] = jnp.zeros_like(acc_v)
     wide = (1, dl // keep_ref.shape[1])
-    for i in range(length // tile):
+    def attend_back(i):
         at, to, count = spans(i)
         mask(i)
         acc_q[...] = jnp.zeros_like(acc_q)
@@ -875,6 +915,33 @@
             -jnp.tile(behind_ref[at, :], wide),
         ).astype(b16)
 
+    count_tiles = length // tile
+    early = count_tiles // 2
+    for i in range(early):
+        attend_back(i)
+    copy_fc2.wait()
+    z_arrive(FC2)
+    z_finish(FC2)
+
+    def result_term(b):
+        at = block_rows(b)
+        return dot(attended[at, :], w_out[...].reshape(dl, width), NORMAL) + dot(
+            act[at, :], w_fc2[...].reshape(fl, width), NORMAL
+        )
+
+    pair_copy(TOK, 3).wait_send()
+    pair_copy(TOK, 0).wait_send()
+    for j in range(1, nc):
+        b = ctx_to(j)
+        tok_all[b] = result_term(b).astype(b16)
+        over_ctx(PART, tok_all.at[b], part_got.at[j - 1], j, b).start()
+    part_own[...] = result_term(c)
+    from_columns()
+    for i in range(early, count_tiles):
+        if i == count_tiles - 1:
+            pass_back(FC2)
+        attend_back(i)
+
     def finish_block(b, carry):
         at = block_rows(b)
         gmixed[at, pl.ds(dl, dl)] = turn(
@@ -888,11 +955,13 @@
 
     lax.fori_loop(0, nc, finish_block, 0)
 
-    pass_back(FC2)
     weight_gradient(QKV, normed, lambda: gmixed[...])
-    weight_gradient(OUT, attended, cotangents)
+    ones = jnp.ones((8, length), b16)
+    sums[0, :, pl.ds(0, 3 * dl)] = dot(ones, gmixed[...], NORMAL)[:1]
+    at_sum = 3 * dl + fl
+    sums[0, :, pl.ds(at_sum, width)] = dot(ones[:, :part], cot_all[c], NORMAL)[:1]
+    pass_back(COLUMN)
     add_sibling(QKV)
-    add_sibling(OUT)
 
     def hidden_gradient(b, carry):
         at = block_rows(b)
@@ -910,20 +979,17 @@
             gmixed[at, :], w_qkv[...].reshape(width, 3 * dl), RIGHT_T
         )
 
+    pair_copy(COT, 3).wait_send()
+    pair_copy(COT, 0).wait_send()
     for j in range(1, nc):
         b = ctx_to(j)
         cot_all[b] = normed_term(b).astype(b16)
         over_ctx(NORM, cot_all.at[b], norm_got.at[j - 1], j, b).start()
     norm_own[...] = normed_term(c)
 
-    ones = jnp.ones((8, length), b16)
-    sums[0, :, pl.ds(0, 3 * dl)] = dot(ones, gmixed[...], NORMAL)[:1]
+    pass_back(QKV)
+    weight_gradient(FC1, normed, lambda: g_hidden[...])
     sums[0, :, pl.ds(3 * dl, fl)] = dot(ones, g_hidden[...], NORMAL)[:1]
-    at_sum = 3 * dl + fl
-    sums[0, :, pl.ds(at_sum, width)] = dot(ones[:, :part], cot_all[c], NORMAL)[:1]
-
-    weight_gradient(FC1, normed, lambda: g_hidden[...])
-    add_sibling(FC1)
     for j in range(1, nc):
         over_ctx(PART, tok_all.at[c], part_got.at[j - 1], j, c).wait_recv()
 
@@ -936,9 +1002,7 @@
         return carry
 
     lax.fori_loop(0, part // chunk, result_step, 0)
-
-    pass_back(QKV)
-    pass_back(OUT)
+    add_sibling(FC1)
     gather_total(FC2)
     o_fc2[...] = own_fc2[z]
 
@@ -967,17 +1031,10 @@
             over_ctx(array, src.at[j - 1], dst.at[j - 1], j, ctx_to(j)).wait_recv()
             place(array, ctx_from(j), dst[j - 1].astype(f32))
 
+    gather_total(COLUMN)
+    o_out[...] = own_column[z]
+    pass_back(FC1)
     swap_start(QKV)
-
-    @pl.when(z == c)
-    def _():
-        gather_total(OUT)
-        for j in range(1, nc):
-            swap_out[j - 1] = own_out_g[0, rows(ctx_to(j)), :].astype(b16)
-            over_ctx(OUT, swap_out.at[j - 1], swapped_out.at[0], j, ctx_to(j)).start()
-        o_out[...] = own_out_g[0, rows(c), :]
-
-    pass_back(FC1)
     for j in range(1, nc):
         over_ctx(NORM, cot_all.at[c], norm_got.at[j - 1], j, c).wait_recv()
 
@@ -1023,39 +1080,23 @@
         over_ctx(SUMS, sums_mine, o_sums.at[c], j, ctx_to(j)).start()
 
     swap_finish(QKV)
-    for j in range(1, nc):
-        @pl.when(ctx_from(j) == z)
-        def _():
-            over_ctx(OUT, swap_out.at[0], swapped_out.at[0], j, ctx_to(j)).wait_recv()
-            o_out[...] = swapped_out[0].astype(f32)
-
     swap_start(FC1)
     for j in range(1, nc):
         over_ctx(SUMS, sums_mine, o_sums.at[ctx_from(j)], j, ctx_to(j)).wait_recv()
     swap_finish(FC1)
 
-    for array in (SMALL, QKV, FC1, FC2, FC2B):
+    for array in (SMALL, QKV, FC1, FC2, OUT):
         z_sent(array)
-    for array in (SMALL, QKV, FC1, TOK, COT):
+    for array in (SMALL, QKV, FC1):
         ctx_sent(array)
+    for array in (TOK, COT):
+        for n in (1, 2):
+            pair_copy(array, n).wait_send()
     for j in range(1, nc):
-        @pl.when(ctx_to(j) == z)
-        def _():
-            out_copy(j, z, c).wait_send()
-
-    @pl.when(z == c)
-    def _():
-        for n, delta in enumerate(DELTAS):
-            @pl.when(exists(delta))
-            def _():
-                out_z(n, delta).wait_send()
-
-    @pl.when(((c == 0) & near_high) | ((c == nz - 1) & near_low))
-    def _():
-        out_z(PASSED, 1).wait_send()
-
+        out_copy(j, ctx_to(j), c).wait_send()
+        column_copy(j, ctx_to(j)).wait_send()
     out_sib(k).wait_send()
-    for array in (QKV, OUT, FC1, FC2):
+    for array in (QKV, COLUMN, FC1, FC2):
         owner_sent(array)
     for j in range(1, nc):
         over_ctx(PART, tok_all.at[c], part_got.at[j - 1], j, c).wait_send()
@@ -1063,11 +1104,6 @@
         over_ctx(SUMS, sums_mine, o_sums.at[c], j, ctx_to(j)).wait_send()
         for array in (QKV, FC1):
             over_ctx(array, swaps[array][0].at[j - 1], swaps[array][1].at[j - 1], j, c).wait_send()
-
-    @pl.when(z == c)
-    def _():
-        for j in range(1, nc):
-            over_ctx(OUT, swap_out.at[j - 1], swapped_out.at[0], j, ctx_to(j)).wait_send()
 
 
 def layer_all(nz, nc, marks, tokens, cotangent, segments, qkv_weight, fc1_weight, fc2_weight, out_weight, small):
@@ -1119,22 +1155,23 @@
         ((length, fl), b16),
     ]
     grads = [(nz, cw, 3 * dl), (nz, cw, fl), (nz, fr, width), (1, cw, width)]
-    fars = [(3,) + g[1:] for g in grads]
+    passed = grads[:3] + [(nz, wr, width)]
+    fars = [(3,) + g[1:] for g in passed]
     work += [(g, b16) for g in grads] + [(g, b16) for g in grads] + [(g, f32) for g in grads]
-    work += [(g, b16) for g in fars] + [(g[1:], b16) for g in grads]
-    work += [((HEADS // nc, length, 1), f32), ((length, 128), f32)]
+    work += [(g, b16) for g in fars] + [(g[1:], b16) for g in passed]
+    work += [((HEADS // nc, length, 1), f32), ((length, 128), f32)] + [((length, 128), f32)] * 3
     work += [((nc - 1, part, width), b16), ((part, width), f32)] * 2
-    work += [((nc - 1, wr, n), b16) for n in (3 * dl, fl, width)]
-    work += [((nc - 1, wr, n), b16) for n in (3 * dl, fl)] + [((1, wr, width), b16)]
+    work += [((nc - 1, wr, n), b16) for n in (3 * dl, fl)] * 2
+    work += [((nz, wr, width), t) for t in (b16, b16, f32)] + [((nc, wr, width), b16)]
     work += [((n, 1, total), f32) for n in (4, 1, 2)]
     dma = pltpu.SemaphoreType.DMA
-    sems = [(7, nc), (7, nc), (8, 5), (8, 5), (8, nz), (8, nz), (7,)]
-    sems += [(7, 5), (7, 5), (7,), (7,), (7, nc), (7, nc)]
+    sems = [(7, nc), (7, nc), (7, 5), (7, 5), (7, nz), (7, nz), (11,)]
+    sems += [(8, 5), (8, 5), (7,), (7,), (7, nc), (7, nc)]
     hbm, vmem = pl.BlockSpec(memory_space=pl.ANY), pl.BlockSpec(memory_space=pltpu.VMEM)
     return pl.pallas_call(
         functools.partial(layer_kernel, nz, nc, marks),
         out_shape=[jax.ShapeDtypeStruct(s, t) for s, t in results],
-        in_specs=[hbm] * 7 + [vmem] * 4,
+        in_specs=[hbm] * 7 + [vmem] + [hbm] * 3,
         out_specs=[vmem] * len(results),
         scratch_shapes=[pltpu.VMEM(s, t) for s, t in work] + [dma(s) for s in sems],
         compiler_params=pltpu.CompilerParams(

time: 159 us -> 154 us (0.969)
  Pallas kernels: 157 us -> 152 us
    pallas_call x1, Pallas kernels: 154 us -> 149 us  [layer_all(): pl.pallas_call(functools.partial(layer_kernel, nz, nc, marks), out_shape=...]
where the time goes in v4:
time: 154 us
  Pallas kernels  152 us (99%)
    pallas_call x1, Pallas kernels, layer_all(): pl.pallas_call(functools.partial(layer_kernel, nz, nc, marks), out_shape=...  149 us
    pallas_call x1, Pallas kernels, finish_all(): pl.pallas_call(functools.partial(finish_kernel, dl, fr, wr), out_shape=[j...  3.29 us

profile of v4, /device:TPU:0, one launch (start us, length us, event | category | flops | bytes accessed | tf_op | source)
XLA Modules:
  0.0 154.2 jit_solution(5126059929073345912)
XLA Ops:
  0.6 0.0 copy-start.3
  0.7 0.0 copy-start.4
  0.7 0.0 copy-start.5
  0.7 0.0 copy-start
  0.7 0.0 copy-start.1
  0.7 0.0 copy-start.2
  0.7 0.6 copy-done.3
  1.3 0.0 copy-done.4
  1.3 0.0 copy-done.5
  1.3 0.0 copy-done
  1.3 0.0 copy-done.1
  1.4 0.0 copy-done.2
  1.4 0.1 concatenate.3
  1.5 0.6 reshape.24.small_ref
  2.1 148.6 %layer.1 = (bf16[256,1024]{1,0:T(8,128)(2,1)}, bf16[256,1024]{1,0:T(8,128)(2,1)}, f32[32,3072]{1,0:T(8,128)}, f32[32,1024]{1,0:T(8,128)}, f32[32,4096]{1,0:T(8,1...) custom-call(bf16[256,1024]{1,0:T(8,128)(2,1)} %bitcast.4, bf16[256,1024]{1,0:T(8,128)(2,1)} %bitcast.5, ...), custom_call_target="tpu_custom_call" | custom-call | tf_op jit(solution)/shard_map/layer/pallas_call | solution.py:1171
  150.7 3.3 %finish.1 = (bf16[256,1024]{1,0:T(8,128)(2,1)}, bf16[256,1024]{1,0:T(8,128)(2,1)}, f32[32,3072]{1,0:T(8,128)}, f32[32,1024]{1,0:T(8,128)}, f32[32,4096]{1,0:T(8,...) custom-call(bf16[256,1024]{1,0:T(8,128)(2,1)} %get-tuple-element.31., ...), custom_call_target="tpu_custom_call" | custom-call | tf_op jit(solution)/shard_map/finish/pallas_call | solution.py:1223
  (1 shorter events, 0.0 us)
Async XLA Ops:
  0.6 0.7 copy-start.3
  0.7 0.7 copy-start.4
  0.7 0.7 copy-start.5
  0.7 0.7 copy-start
  0.7 0.7 copy-start.1
  0.7 0.7 copy-start.2

commit v5 on v4

--- a/solution.py
+++ b/solution.py
@@ -321,7 +321,7 @@
     pass_qkv, pass_fc1, pass_fc2, pass_out, log_s, seg_col, keep_ref, ahead_ref, behind_ref,
     part_got, part_own, norm_got, norm_own,
     swap_qkv, swap_fc1, swapped_qkv, swapped_fc1, out_planes, give_column, own_column, column_got,
-    sums, sums_sib, sums_z,
+    sums, sums_sib, sums_z, held,
     ctx_send, ctx_recv, z_send, z_recv, sib_send, sib_recv, loc,
     back_z_send, back_z_recv, back_sib_send, back_sib_recv, back_ctx_send, back_ctx_recv,
 ):
@@ -866,6 +866,51 @@
     def over_ctx(array, src, dst, j, to):
         return remote(src, dst, back_ctx_send.at[array, j], back_ctx_recv.at[array, j], (d, to))
 
+    half_rows = part // 2
+    terms = {PART: (tok_all, part_got, part_own), NORM: (cot_all, norm_got, norm_own)}
+
+    def term_copy(array, n):
+        store, got, _ = terms[array]
+        whose, at, slot, to = (
+            (corner, first_half, 2, side),
+            (corner, second_half, 2, across),
+            (side, first_half, 0, side),
+            (side, second_half, 0, side),
+            (across, second_half, 1, across),
+            (across, first_half, 1, across),
+        )[n]
+        return remote(
+            store.at[whose, at, :], got.at[slot, at, :], back_ctx_send.at[array, n], back_ctx_recv.at[array, n], (d, to)
+        )
+
+    def send_terms(array, term):
+        store, _, own = terms[array]
+        store[corner] = term(corner).astype(b16)
+        term_copy(array, 0).start()
+        term_copy(array, 1).start()
+        x = term(side)
+        store[side, first_half, :] = x[:half_rows].astype(b16)
+        held[0] = x[half_rows:]
+        term_copy(array, 2).start()
+        x = term(across)
+        store[across, second_half, :] = x[half_rows:].astype(b16)
+        held[1] = x[:half_rows]
+        term_copy(array, 4).start()
+        own[...] = term(c)
+
+    def pass_terms(array):
+        store, got, _ = terms[array]
+        term_copy(array, 1).wait_recv()
+        store[side, second_half, :] = (held[0] + got[2, second_half, :].astype(f32)).astype(b16)
+        term_copy(array, 3).start()
+        term_copy(array, 0).wait_recv()
+        store[across, first_half, :] = (held[1] + got[2, first_half, :].astype(f32)).astype(b16)
+        term_copy(array, 5).start()
+
+    def terms_arrive(array):
+        for n in range(2, 6):
+            term_copy(array, n).wait_recv()
+
     weight_gradient(FC2, act, cotangents)
     weight_gradient(OUT, attended, cotangents)
 
@@ -931,15 +976,12 @@
 
     pair_copy(TOK, 3).wait_send()
     pair_copy(TOK, 0).wait_send()
-    for j in range(1, nc):
-        b = ctx_to(j)
-        tok_all[b] = result_term(b).astype(b16)
-        over_ctx(PART, tok_all.at[b], part_got.at[j - 1], j, b).start()
-    part_own[...] = result_term(c)
+    send_terms(PART, result_term)
     from_columns()
     for i in range(early, count_tiles):
         if i == count_tiles - 1:
             pass_back(FC2)
+            pass_terms(PART)
         attend_back(i)
 
     def finish_block(b, carry):
@@ -981,23 +1023,18 @@
 
     pair_copy(COT, 3).wait_send()
     pair_copy(COT, 0).wait_send()
-    for j in range(1, nc):
-        b = ctx_to(j)
-        cot_all[b] = normed_term(b).astype(b16)
-        over_ctx(NORM, cot_all.at[b], norm_got.at[j - 1], j, b).start()
-    norm_own[...] = normed_term(c)
-
+    send_terms(NORM, normed_term)
     pass_back(QKV)
     weight_gradient(FC1, normed, lambda: g_hidden[...])
     sums[0, :, pl.ds(3 * dl, fl)] = dot(ones, g_hidden[...], NORMAL)[:1]
-    for j in range(1, nc):
-        over_ctx(PART, tok_all.at[c], part_got.at[j - 1], j, c).wait_recv()
+    pass_terms(NORM)
+    terms_arrive(PART)
 
     def result_step(i, carry):
         at = pl.ds(pl.multiple_of(i * chunk, chunk), chunk)
         y = tok_all[c, at, :].astype(f32) + part_own[at, :] + vec_d[2:3, :]
-        for j in range(1, nc):
-            y = y + part_got[j - 1, at, :].astype(f32)
+        for n in range(2):
+            y = y + part_got[n, at, :].astype(f32)
         o_result[at, :] = y.astype(b16)
         return carry
 
@@ -1035,8 +1072,7 @@
     o_out[...] = own_column[z]
     pass_back(FC1)
     swap_start(QKV)
-    for j in range(1, nc):
-        over_ctx(NORM, cot_all.at[c], norm_got.at[j - 1], j, c).wait_recv()
+    terms_arrive(NORM)
 
     def norm_step(i, carry):
         gain_sum, shift_sum = carry
@@ -1046,8 +1082,8 @@
         inverse = lax.rsqrt(jnp.mean(x * x, axis=-1, keepdims=True) + epsilon)
         x = x * inverse
         g = norm_own[at, :]
-        for j in range(1, nc):
-            g = g + norm_got[j - 1, at, :].astype(f32)
+        for n in range(2):
+            g = g + norm_got[n, at, :].astype(f32)
         v = g * vec_d[0:1, :]
         y = inverse * (
             v - jnp.mean(v, axis=-1, keepdims=True) - x * jnp.mean(v * x, axis=-1, keepdims=True)
@@ -1065,25 +1101,29 @@
 
     sum_sib = remote(sums.at[0], sums_sib.at[0], back_sib_send.at[SUMS], back_sib_recv.at[SUMS], (other, c))
     sum_sib.start()
+    swap_finish(QKV)
     sum_sib.wait()
     sums[1] = sums[0] + sums_sib[0]
-    for n, partner in enumerate((z + 1 - 2 * lax.rem(z, 2), lax.rem(z + 2, nz))):
-        trade = remote(
+    trades = [
+        remote(
             sums.at[n + 1], sums_z.at[n], back_z_send.at[SUMS, n], back_z_recv.at[SUMS, n], (2 * partner + k, c)
         )
-        trade.start()
-        trade.wait()
-        sums[n + 2] = sums[n + 1] + sums_z[n]
+        for n, partner in enumerate((z + 1 - 2 * lax.rem(z, 2), lax.rem(z + 2, nz)))
+    ]
+    trades[0].start()
+    trades[0].wait()
+    sums[2] = sums[1] + sums_z[0]
+    trades[1].start()
+    swap_start(FC1)
+    trades[1].wait()
+    sums[3] = sums[2] + sums_z[1]
     sums_mine = sums.at[3]
-    o_sums[c] = sums[3]
     for j in range(1, nc):
         over_ctx(SUMS, sums_mine, o_sums.at[c], j, ctx_to(j)).start()
-
-    swap_finish(QKV)
-    swap_start(FC1)
+    o_sums[c] = sums[3]
+    swap_finish(FC1)
     for j in range(1, nc):
         over_ctx(SUMS, sums_mine, o_sums.at[ctx_from(j)], j, ctx_to(j)).wait_recv()
-    swap_finish(FC1)
 
     for array in (SMALL, QKV, FC1, FC2, OUT):
         z_sent(array)
@@ -1092,6 +1132,9 @@
     for array in (TOK, COT):
         for n in (1, 2):
             pair_copy(array, n).wait_send()
+    for n in range(6):
+        term_copy(PART, n).wait_send()
+        term_copy(NORM, n).wait_send()
     for j in range(1, nc):
         out_copy(j, ctx_to(j), c).wait_send()
         column_copy(j, ctx_to(j)).wait_send()
@@ -1099,8 +1142,6 @@
     for array in (QKV, COLUMN, FC1, FC2):
         owner_sent(array)
     for j in range(1, nc):
-        over_ctx(PART, tok_all.at[c], part_got.at[j - 1], j, c).wait_send()
-        over_ctx(NORM, cot_all.at[c], norm_got.at[j - 1], j, c).wait_send()
         over_ctx(SUMS, sums_mine, o_sums.at[c], j, ctx_to(j)).wait_send()
         for array in (QKV, FC1):
             over_ctx(array, swaps[array][0].at[j - 1], swaps[array][1].at[j - 1], j, c).wait_send()
@@ -1164,9 +1205,10 @@
     work += [((nc - 1, wr, n), b16) for n in (3 * dl, fl)] * 2
     work += [((nz, wr, width), t) for t in (b16, b16, f32)] + [((nc, wr, width), b16)]
     work += [((n, 1, total), f32) for n in (4, 1, 2)]
+    work += [((2, part // 2, width), f32)]
     dma = pltpu.SemaphoreType.DMA
     sems = [(7, nc), (7, nc), (7, 5), (7, 5), (7, nz), (7, nz), (11,)]
-    sems += [(8, 5), (8, 5), (7,), (7,), (7, nc), (7, nc)]
+    sems += [(8, 5), (8, 5), (7,), (7,), (7, 6), (7, 6)]
     hbm, vmem = pl.BlockSpec(memory_space=pl.ANY), pl.BlockSpec(memory_space=pltpu.VMEM)
     return pl.pallas_call(
         functools.partial(layer_kernel, nz, nc, marks),

time: 154 us -> 150 us (0.974)
  Pallas kernels: 152 us -> 148 us
    pallas_call x1, Pallas kernels: 149 us -> 145 us  [layer_all(): pl.pallas_call(functools.partial(layer_kernel, nz, nc, marks), out_shape=...]
where the time goes in v5:
time: 150 us
  Pallas kernels  148 us (99%)
    pallas_call x1, Pallas kernels, layer_all(): pl.pallas_call(functools.partial(layer_kernel, nz, nc, marks), out_shape=...  145 us
    pallas_call x1, Pallas kernels, finish_all(): pl.pallas_call(functools.partial(finish_kernel, dl, fr, wr), out_shape=[j...  3.29 us

profile of v5, /device:TPU:0, one launch (start us, length us, event | category | flops | bytes accessed | tf_op | source)
XLA Modules:
  0.0 150.0 jit_solution(873007233636145430)
XLA Ops:
  0.6 0.0 copy-start.3
  0.7 0.0 copy-start.4
  0.7 0.0 copy-start.5
  0.7 0.0 copy-start
  0.7 0.0 copy-start.1
  0.7 0.0 copy-start.2
  0.7 0.6 copy-done.3
  1.3 0.0 copy-done.4
  1.3 0.0 copy-done.5
  1.3 0.0 copy-done
  1.3 0.0 copy-done.1
  1.4 0.0 copy-done.2
  1.4 0.1 concatenate.3
  1.5 0.6 reshape.24.small_ref
  2.1 144.5 %layer.1 = (bf16[256,1024]{1,0:T(8,128)(2,1)}, bf16[256,1024]{1,0:T(8,128)(2,1)}, f32[32,3072]{1,0:T(8,128)}, f32[32,1024]{1,0:T(8,128)}, f32[32,4096]{1,0:T(8,1...) custom-call(bf16[256,1024]{1,0:T(8,128)(2,1)} %bitcast.4, bf16[256,1024]{1,0:T(8,128)(2,1)} %bitcast.5, ...), custom_call_target="tpu_custom_call" | custom-call | tf_op jit(solution)/shard_map/layer/pallas_call | solution.py:1213
  146.6 3.3 %finish.1 = (bf16[256,1024]{1,0:T(8,128)(2,1)}, bf16[256,1024]{1,0:T(8,128)(2,1)}, f32[32,3072]{1,0:T(8,128)}, f32[32,1024]{1,0:T(8,128)}, f32[32,4096]{1,0:T(8,...) custom-call(bf16[256,1024]{1,0:T(8,128)(2,1)} %get-tuple-element.31., ...), custom_call_target="tpu_custom_call" | custom-call | tf_op jit(solution)/shard_map/finish/pallas_call | solution.py:1265
  (1 shorter events, 0.0 us)
Async XLA Ops:
  0.6 0.7 copy-start.3
  0.7 0.7 copy-start.4
  0.7 0.7 copy-start.5
  0.7 0.7 copy-start
  0.7 0.7 copy-start.1
  0.7 0.7 copy-start.2

commit v6 on v5

--- a/solution.py
+++ b/solution.py
@@ -961,27 +961,7 @@
         ).astype(b16)
 
     count_tiles = length // tile
-    early = count_tiles // 2
-    for i in range(early):
-        attend_back(i)
-    copy_fc2.wait()
-    z_arrive(FC2)
-    z_finish(FC2)
-
-    def result_term(b):
-        at = block_rows(b)
-        return dot(attended[at, :], w_out[...].reshape(dl, width), NORMAL) + dot(
-            act[at, :], w_fc2[...].reshape(fl, width), NORMAL
-        )
-
-    pair_copy(TOK, 3).wait_send()
-    pair_copy(TOK, 0).wait_send()
-    send_terms(PART, result_term)
-    from_columns()
-    for i in range(early, count_tiles):
-        if i == count_tiles - 1:
-            pass_back(FC2)
-            pass_terms(PART)
+    for i in range(count_tiles):
         attend_back(i)
 
     def finish_block(b, carry):
@@ -1002,8 +982,22 @@
     sums[0, :, pl.ds(0, 3 * dl)] = dot(ones, gmixed[...], NORMAL)[:1]
     at_sum = 3 * dl + fl
     sums[0, :, pl.ds(at_sum, width)] = dot(ones[:, :part], cot_all[c], NORMAL)[:1]
-    pass_back(COLUMN)
+    copy_fc2.wait()
+    z_arrive(FC2)
+    z_finish(FC2)
     add_sibling(QKV)
+
+    def result_term(b):
+        at = block_rows(b)
+        return dot(attended[at, :], w_out[...].reshape(dl, width), NORMAL) + dot(
+            act[at, :], w_fc2[...].reshape(fl, width), NORMAL
+        )
+
+    pair_copy(TOK, 3).wait_send()
+    pair_copy(TOK, 0).wait_send()
+    send_terms(PART, result_term)
+    from_columns()
+    pass_back(FC2)
 
     def hidden_gradient(b, carry):
         at = block_rows(b)
@@ -1014,6 +1008,9 @@
         return carry
 
     lax.fori_loop(0, nc, hidden_gradient, 0)
+    pass_terms(PART)
+    pass_back(QKV)
+    pass_back(COLUMN)
 
     def normed_term(b):
         at = block_rows(b)
@@ -1024,7 +1021,6 @@
     pair_copy(COT, 3).wait_send()
     pair_copy(COT, 0).wait_send()
     send_terms(NORM, normed_term)
-    pass_back(QKV)
     weight_gradient(FC1, normed, lambda: g_hidden[...])
     sums[0, :, pl.ds(3 * dl, fl)] = dot(ones, g_hidden[...], NORMAL)[:1]
     pass_terms(NORM)

time: 150 us -> 155 us (1.033)
  Pallas kernels: 148 us -> 152 us
    pallas_call x1, Pallas kernels: 145 us -> 149 us  [layer_all(): pl.pallas_call(functools.partial(layer_kernel, nz, nc, marks), out_shape=...]
where the time goes in v6:
time: 155 us; the launch traced here: 154 us
  Pallas kernels  152 us (98%)
    pallas_call x1, Pallas kernels, layer_all(): pl.pallas_call(functools.partial(layer_kernel, nz, nc, marks), out_shape=...  149 us
    pallas_call x1, Pallas kernels, finish_all(): pl.pallas_call(functools.partial(finish_kernel, dl, fr, wr), out_shape=[j...  3.29 us

profile of v6, /device:TPU:0, one launch (start us, length us, event | category | flops | bytes accessed | tf_op | source)
XLA Modules:
  0.0 154.4 jit_solution(13301387020129130339)
XLA Ops:
  0.6 0.0 copy-start.3
  0.7 0.0 copy-start.4
  0.7 0.0 copy-start.5
  0.7 0.0 copy-start
  0.7 0.0 copy-start.1
  0.7 0.0 copy-start.2
  0.7 0.6 copy-done.3
  1.3 0.0 copy-done.4
  1.3 0.0 copy-done.5
  1.3 0.0 copy-done
  1.3 0.0 copy-done.1
  1.4 0.0 copy-done.2
  1.4 0.1 concatenate.3
  1.5 0.6 reshape.24.small_ref
  2.1 148.9 %layer.1 = (bf16[256,1024]{1,0:T(8,128)(2,1)}, bf16[256,1024]{1,0:T(8,128)(2,1)}, f32[32,3072]{1,0:T(8,128)}, f32[32,1024]{1,0:T(8,128)}, f32[32,4096]{1,0:T(8,1...) custom-call(bf16[256,1024]{1,0:T(8,128)(2,1)} %bitcast.4, bf16[256,1024]{1,0:T(8,128)(2,1)} %bitcast.5, ...), custom_call_target="tpu_custom_call" | custom-call | tf_op jit(solution)/shard_map/layer/pallas_call | solution.py:1209
  151.0 3.3 %finish.1 = (bf16[256,1024]{1,0:T(8,128)(2,1)}, bf16[256,1024]{1,0:T(8,128)(2,1)}, f32[32,3072]{1,0:T(8,128)}, f32[32,1024]{1,0:T(8,128)}, f32[32,4096]{1,0:T(8,...) custom-call(bf16[256,1024]{1,0:T(8,128)(2,1)} %get-tuple-element.31., ...), custom_call_target="tpu_custom_call" | custom-call | tf_op jit(solution)/shard_map/finish/pallas_call | solution.py:1261
  (1 shorter events, 0.0 us)
Async XLA Ops:
  0.6 0.7 copy-start.3
  0.7 0.7 copy-start.4
  0.7 0.7 copy-start.5
  0.7 0.7 copy-start
  0.7 0.7 copy-start.1
  0.7 0.7 copy-start.2
